TPU v7x, 32 devices: a whole 2x2x4 slice. The times are simulated.
32 devices in a mesh: gx: 2 (over core), gy: 4 (over y, x), gz: 4 (over z).
Axes of the slice: x: 2, y: 2, z: 4, core: 2. Of those that a mesh axis runs over, the one named last changes fastest.
Arguments:
- velocity: float32 [3, 32, 192, 512], P(None, 'gx', 'gz', 'gy'), may hold values from 0.5 to 1.5
- pressure: float32 [32, 192, 512], P('gx', 'gz', 'gy'), may hold values from -3 to 3
- kernel: float32 [8192, 128], P(('gx', 'gy', 'gz')), may hold values from 0.1 to 1
- owners: int32 [8192, 1], P(('gx', 'gy', 'gz')), may hold values from 0 to 7; in each aligned block of 256 rows (0 to 255, 256 to 511, ...) at most 64 rows name the same one
- lines: int32 [8192], P(('gx', 'gy', 'gz')), may hold values from 0 to 767
- point_turbine: int32 [8192], P(('gx', 'gy', 'gz')), may hold values from 0 to 47
- row_counts: int32 [2, 4, 4], P('gx', 'gy', 'gz'), may hold values from 128 to 256
- thrust: float32 [48], replicated, may hold values from 0.4 to 1
- inflow_x: int32 [48], replicated, may hold values from 0 to 31
- inflow_y: int32 [48], replicated, may hold values from 0 to 480
Outputs:
- velocity_out: float32 [3, 32, 192, 512], P(None, 'gx', 'gz', 'gy')
- pressure_out: float32 [32, 192, 512], P('gx', 'gz', 'gy')
Inputs may be any that keep to these rules, and one draw needn't show every extreme that they name: `owners`: among the rows of one device no horizontal block is named by more than 64 rows, and in every draw some device names one block exactly 64 times.
All inputs are finite; a program needn't handle non-finite values.
Results may differ from a plain program's by a relative error of at most 0.00011.
Values sent between devices are 32-bit elements; how exact they have to be, the bound alone decides.
No kernel may reach another device: no remote copies, remote signals or barrier semaphores. Data moves between devices by JAX's collectives and lax.ppermute only.
A program may use at most 64 MiB of HBM per device.

v0:
```python
import jax
import jax.numpy as jnp
from jax import lax
from jax.sharding import PartitionSpec as P

BAND = 32
STEPS = 2
SWEEPS = 8


def extended(cells, sides, width):
    for axis, dim in sides:
        count = lax.axis_size(axis)
        ends = count - 1
        head = lax.slice_in_dim(cells, 0, width, axis=dim)
        tail = lax.slice_in_dim(cells, cells.shape[dim] - width, cells.shape[dim], axis=dim)
        cells = jnp.concatenate(
            [
                lax.ppermute(tail, axis, [(i, (i + 1) % count) for i in range(ends)]),
                cells,
                lax.ppermute(head, axis, [((i + 1) % count, i) for i in range(ends)]),
            ],
            axis=dim,
        )
    return cells


def neighbours(padded):
    total = padded[..., 2:, 1:-1, 1:-1] + padded[..., :-2, 1:-1, 1:-1]
    total = total + padded[..., 1:-1, 2:, 1:-1] + padded[..., 1:-1, :-2, 1:-1]
    total = total + padded[..., 1:-1, 1:-1, 2:] + padded[..., 1:-1, 1:-1, :-2]
    return total


def pressure_faces(press):
    return extended(press, (("gx", 0), ("gy", 2), ("gz", 1)), 1)


def inside_line(index, cells, count):
    places = index * cells - 1 + jnp.arange(cells + 2)
    return ((places >= 0) & (places < cells * count)).astype(jnp.float32)


def body(
    velocity, pressure, kernel, owners, lines, point_turbine, row_counts, thrust, inflow_x, inflow_y
):
    time_step = 0.4
    viscosity = 0.05
    cells_x = velocity.shape[1]
    cells_z = velocity.shape[2]
    cells_y = velocity.shape[3]
    row_total = kernel.shape[0]
    turbines = thrust.shape[0]
    peers_x = lax.axis_size("gx")
    peers_y = lax.axis_size("gy")
    peers = peers_x * peers_y
    capacity = 2 * row_total // peers
    depth_total = cells_z * lax.axis_size("gz")
    start_x = lax.axis_index("gx") * cells_x
    start_y = lax.axis_index("gy") * cells_y
    xplaces = start_x + jnp.arange(cells_x)
    yplaces = start_y + jnp.arange(cells_y)
    pick_x = (inflow_x[:, None] == xplaces[None, :]).astype(jnp.float32)
    band = (
        (yplaces[None, :] >= inflow_y[:, None]) & (yplaces[None, :] < inflow_y[:, None] + BAND)
    ).astype(jnp.float32)
    valid = (jnp.arange(row_total) < row_counts.reshape(())).astype(jnp.float32)
    pick_turbine = (point_turbine[:, None] == jnp.arange(turbines)[None, :]).astype(jnp.float32)
    target = owners[:, 0]
    landing = (target[:, None] == jnp.arange(peers)[None, :]).astype(jnp.int32)
    earlier = jnp.cumsum(landing, axis=0) - landing
    slot_index = jnp.sum(earlier * landing, axis=1)
    inside = None
    mask_x = inside_line(lax.axis_index("gx"), cells_x, peers_x)
    mask_z = inside_line(lax.axis_index("gz"), cells_z, lax.axis_size("gz"))
    mask_y = inside_line(lax.axis_index("gy"), cells_y, peers_y)
    inside = mask_x[:, None, None] * mask_z[None, :, None] * mask_y[None, None, :]
    field = velocity
    press = pressure
    for repeat in range(STEPS):
        plane = jnp.dot(
            pick_x, field[0].reshape(cells_x, cells_z * cells_y), precision=lax.Precision.HIGHEST
        )
        partial_sum = jnp.sum(
            plane.reshape(turbines, cells_z, cells_y) * band[:, None, :], axis=(1, 2)
        )
        total = lax.psum(partial_sum, ("gx", "gy", "gz"))
        uref = total / (BAND * depth_total)
        magnitude = 0.5 * thrust * uref * jnp.abs(uref)
        row_force = jnp.dot(pick_turbine, magnitude, precision=lax.Precision.HIGHEST) * valid
        values = kernel * row_force[:, None]
        send_values = (
            jnp.zeros((peers, capacity, cells_y), jnp.float32).at[target, slot_index].set(values)
        )
        send_lines = jnp.zeros((peers, capacity), jnp.int32).at[target, slot_index].set(lines)
        got_values, got_lines = (
            lax.all_to_all(send_values, ("gx", "gy"), split_axis=0, concat_axis=0, tiled=True),
            lax.all_to_all(send_lines, ("gx", "gy"), split_axis=0, concat_axis=0, tiled=True),
        )
        force = jnp.zeros((cells_x * cells_z, cells_y), jnp.float32)
        force = force.at[got_lines.reshape(-1)].add(got_values.reshape(-1, cells_y))
        force = force.reshape(cells_x, cells_z, cells_y)
        forcing = jnp.stack([force, jnp.zeros_like(force), jnp.zeros_like(force)])
        padded = extended(field, (("gx", 1), ("gy", 3), ("gz", 2)), 1)
        laplace = neighbours(padded) - 6.0 * field
        star = field + time_step * (viscosity * laplace - forcing)
        spad = extended(star, (("gx", 1), ("gy", 3), ("gz", 2)), 1)
        source = 0.5 * (spad[0, 2:, 1:-1, 1:-1] - spad[0, :-2, 1:-1, 1:-1])
        source = source + 0.5 * (spad[1, 1:-1, 1:-1, 2:] - spad[1, 1:-1, 1:-1, :-2])
        source = source + 0.5 * (spad[2, 1:-1, 2:, 1:-1] - spad[2, 1:-1, :-2, 1:-1])
        source_wide = extended(source, (("gx", 0), ("gy", 2), ("gz", 1)), 1)
        for sweep_pair in range(SWEEPS // 2):
            deeper = extended(press, (("gx", 0), ("gy", 2), ("gz", 1)), 2)
            middle = (neighbours(deeper) - source_wide) / 6.0 * inside
            press = (neighbours(middle) - source) / 6.0
        ppad = pressure_faces(press)
        grad_x = 0.5 * (ppad[2:, 1:-1, 1:-1] - ppad[:-2, 1:-1, 1:-1])
        grad_y = 0.5 * (ppad[1:-1, 1:-1, 2:] - ppad[1:-1, 1:-1, :-2])
        grad_z = 0.5 * (ppad[1:-1, 2:, 1:-1] - ppad[1:-1, :-2, 1:-1])
        field = star - jnp.stack([grad_x, grad_y, grad_z])
    return (field, press)


def solution(mesh):
    placed = (
        P(None, "gx", "gz", "gy"),
        P("gx", "gz", "gy"),
        P(("gx", "gy", "gz"), None),
        P(("gx", "gy", "gz"), None),
        P(("gx", "gy", "gz")),
        P(("gx", "gy", "gz")),
        P("gx", "gy", "gz"),
        P(),
        P(),
        P(),
    )
    return jax.shard_map(
        body,
        mesh=mesh,
        in_specs=placed,
        out_specs=(P(None, "gx", "gz", "gy"), P("gx", "gz", "gy")),
        check_vma=False,
    )
```

profile of v0, /device:TPU:12, one launch (start us, length us, event | category | flops | bytes accessed | tf_op | source)
XLA Modules:
  0.0 809.8 jit_solution(7790940023923331849)
XLA Ops:
  8.2 38.7 %scatter_fusion = s32[8,64]{1,0:T(8,128)} fusion(s32[8,64]{1,0:T(8,128)} %broadcast.234, s32[256]{0:T(256)S(1)} %bitcast.94, s32[256]{0:T(256)} %param.14), kind=kCustom, calls=%fused_computation | custom fusion | bytes 5120 | tf_op jit(solution)/shard_map/scatter | solution.py:95
  58.4 41.4 %psum.14 = f32[48]{0:T(128)S(1)} all-reduce(f32[48]{0:T(128)S(1)} %fusion), channel_id=1, replica_groups=mesh['gx'=2,'gy'=4,'gz'=4] {'gx','gy','gz'}, use_global_device_ids=true, to_apply=%region_5.6 | all-reduce | flops 48 | bytes 384 | tf_op jit(solution)/shard_map/psum | solution.py:87
  112.5 28.0 %scatter_fusion.1 = f32[8,64,128]{2,1,0:T(8,128)} fusion(f32[8,64,128]{2,1,0:T(8,128)} %broadcast.242.clone, s32[256]{0:T(256)S(1)} %bitcast.95, f32[256,128]{1,0:T(8,128)S(1)} %broadcast_multiply_fusion.1), kind=kCustom, calls=%fused_computation.1 | custom fusion | bytes 395264 | tf_op jit(solution)/shard_map/scatter | solution.py:93
  216.8 6.9 collective-permute-done.9
  229.8 7.1 collective-permute-done.20
  236.9 5.8 collective-permute-done.21
  262.8 5.3 collective-permute-start.27
  268.0 10.1 %collective-permute-done.26 = f32[20,48,2]{2,1,0:T(8,128)S(1)} collective-permute-done((f32[20,48,2]{2,1,0:T(8,128)S(1)}, f32[20,48,2]{2,1,0:T(8,128)S(1)}, u32[]{:S(2)}, u32[]{:S(2)}) %collective-permute-start.26) | collective-permute-done | bytes 7712 | tf_op jit(solution)/shard_map/ppermute | solution.py:19
  278.2 6.2 collective-permute-done.27
  306.2 5.3 collective-permute-start.33
  311.5 10.1 %collective-permute-done.32 = f32[20,48,2]{2,1,0:T(8,128)S(1)} collective-permute-done((f32[20,48,2]{2,1,0:T(8,128)S(1)}, f32[20,48,2]{2,1,0:T(8,128)S(1)}, u32[]{:S(2)}, u32[]{:S(2)}) %collective-permute-start.32) | collective-permute-done | bytes 7712 | tf_op jit(solution)/shard_map/ppermute | solution.py:19
  321.6 6.2 collective-permute-done.33
  347.9 5.3 collective-permute-start.39
  353.2 10.1 %collective-permute-done.38 = f32[20,48,2]{2,1,0:T(8,128)S(1)} collective-permute-done((f32[20,48,2]{2,1,0:T(8,128)S(1)}, f32[20,48,2]{2,1,0:T(8,128)S(1)}, u32[]{:S(2)}, u32[]{:S(2)}) %collective-permute-start.38) | collective-permute-done | bytes 7712 | tf_op jit(solution)/shard_map/ppermute | solution.py:19
  363.4 6.2 collective-permute-done.39
  395.7 8.6 %collective-permute-done.44 = f32[18,48,1]{2,1,0:T(8,128)S(1)} collective-permute-done((f32[18,48,1]{2,1,0:T(8,128)S(1)}, f32[18,48,1]{2,1,0:T(8,128)S(1)}, u32[]{:S(2)}, u32[]{:S(2)}) %collective-permute-start.44) | collective-permute-done | bytes 3488 | tf_op jit(solution)/shard_map/ppermute | solution.py:21
  404.3 11.8 %collective-permute-done.45 = f32[18,48,1]{2,1,0:T(8,128)S(1)} collective-permute-done((f32[18,48,1]{2,1,0:T(8,128)S(1)}, f32[18,48,1]{2,1,0:T(8,128)S(1)}, u32[]{:S(2)}, u32[]{:S(2)}) %collective-permute-start.45) | collective-permute-done | bytes 3488 | tf_op jit(solution)/shard_map/ppermute | solution.py:19
  431.7 38.0 %psum.15 = f32[48]{0:T(128)S(1)} all-reduce(f32[48]{0:T(128)S(1)} %fusion.1), channel_id=1, replica_groups=mesh['gx'=2,'gy'=4,'gz'=4] {'gx','gy','gz'}, use_global_device_ids=true, to_apply=%region_9.10 | all-reduce | flops 48 | bytes 384 | tf_op jit(solution)/shard_map/psum | solution.py:87
  470.7 28.0 %scatter_fusion.2 = f32[8,64,128]{2,1,0:T(8,128)} fusion(f32[8,64,128]{2,1,0:T(8,128)} %broadcast.242, s32[256]{0:T(256)S(1)} %bitcast.96, f32[256,128]{1,0:T(8,128)S(1)} %broadcast_multiply_fusion), kind=kCustom, calls=%fused_computation.3 | custom fusion | bytes 395264 | tf_op jit(solution)/shard_map/scatter | solution.py:93
  596.9 6.9 collective-permute-done.57
  609.9 7.1 collective-permute-done.68
  617.0 5.8 collective-permute-done.69
  642.2 5.3 collective-permute-start.75
  647.5 10.1 %collective-permute-done.74 = f32[20,48,2]{2,1,0:T(8,128)S(1)} collective-permute-done((f32[20,48,2]{2,1,0:T(8,128)S(1)}, f32[20,48,2]{2,1,0:T(8,128)S(1)}, u32[]{:S(2)}, u32[]{:S(2)}) %collective-permute-start.74) | collective-permute-done | bytes 7712 | tf_op jit(solution)/shard_map/ppermute | solution.py:19
  657.6 6.2 collective-permute-done.75
  684.1 5.3 collective-permute-start.81
  689.4 10.1 %collective-permute-done.80 = f32[20,48,2]{2,1,0:T(8,128)S(1)} collective-permute-done((f32[20,48,2]{2,1,0:T(8,128)S(1)}, f32[20,48,2]{2,1,0:T(8,128)S(1)}, u32[]{:S(2)}, u32[]{:S(2)}) %collective-permute-start.80) | collective-permute-done | bytes 7712 | tf_op jit(solution)/shard_map/ppermute | solution.py:19
  699.5 6.2 collective-permute-done.81
  731.4 10.1 %collective-permute-done.86 = f32[20,48,2]{2,1,0:T(8,128)S(1)} collective-permute-done((f32[20,48,2]{2,1,0:T(8,128)S(1)}, f32[20,48,2]{2,1,0:T(8,128)S(1)}, u32[]{:S(2)}, u32[]{:S(2)}) %collective-permute-start.86) | collective-permute-done | bytes 7712 | tf_op jit(solution)/shard_map/ppermute | solution.py:19
  741.5 6.2 collective-permute-done.87
  773.9 8.6 %collective-permute-done.92 = f32[18,48,1]{2,1,0:T(8,128)S(1)} collective-permute-done((f32[18,48,1]{2,1,0:T(8,128)S(1)}, f32[18,48,1]{2,1,0:T(8,128)S(1)}, u32[]{:S(2)}, u32[]{:S(2)}) %collective-permute-start.92) | collective-permute-done | bytes 3488 | tf_op jit(solution)/shard_map/ppermute | solution.py:21
  782.5 11.8 %collective-permute-done.93 = f32[18,48,1]{2,1,0:T(8,128)S(1)} collective-permute-done((f32[18,48,1]{2,1,0:T(8,128)S(1)}, f32[18,48,1]{2,1,0:T(8,128)S(1)}, u32[]{:S(2)}, u32[]{:S(2)}) %collective-permute-start.93) | collective-permute-done | bytes 3488 | tf_op jit(solution)/shard_map/ppermute | solution.py:19
  (380 shorter events, 427.5 us)
Async XLA Ops:
  1.6 99.4 %collective-permute-start.1 = (f32[3,1,48,128]{3,2,1,0:T(8,128)S(1)}, f32[3,1,48,128]{3,2,1,0:T(8,128)S(1)}, u32[]{:S(2)}, u32[]{:S(2)}) collective-permute-start(f32[3,1,48,128]{3,2,1,0:T(8,128)S(1)} %get-tuple-element.51), channel_id=1, source_target_pairs={{0,16},{1,17},{2,18},{3,19},{4,20},{5,21},{6,22},{7,23},{8,24},{9,... | collective-permute-start | bytes 221192 | tf_op jit(solution)/shard_map/ppermute | solution.py:19
  3.3 97.8 %collective-permute-start = (f32[3,1,48,128]{3,2,1,0:T(8,128)S(1)}, f32[3,1,48,128]{3,2,1,0:T(8,128)S(1)}, u32[]{:S(2)}, u32[]{:S(2)}) collective-permute-start(f32[3,1,48,128]{3,2,1,0:T(8,128)S(1)} %get-tuple-element.50), channel_id=1, source_target_pairs={{16,0},{17,1},{18,2},{19,3},{20,4},{21,5},{22,6},{23,7},{24,8},{25... | collective-permute-start | bytes 221192 | tf_op jit(solution)/shard_map/ppermute | solution.py:21
  46.9 93.5 %all-to-all-start = ((s32[8,1,64]{2,1,0:T(1,128)}), s32[8,1,64]{2,1,0:T(1,128)S(1)}, u32[]{:S(2)}, u32[]{:S(2)}) async-start(s32[8,1,64]{2,1,0:T(1,128)} %bitcast.7), calls=%async_computation | async-start | bytes 8192 | tf_op jit(solution)/shard_map/all_to_all | solution.py:98
  53.5 115.3 %collective-permute-start.6 = (f32[2,48,128]{2,1,0:T(8,128)}, f32[2,48,128]{2,1,0:T(8,128)}, u32[]{:S(2)}, u32[]{:S(2)}) collective-permute-start(f32[2,48,128]{2,1,0:T(8,128)} %get-tuple-element.103), channel_id=1, source_target_pairs={{0,16},{1,17},{2,18},{3,19},{4,20},{5,21},{6,22},{7,23},{8,24},{9,... | collective-permute-start | bytes 147464 | tf_op jit(solution)/shard_map/ppermute | solution.py:19
  56.1 137.9 %collective-permute-start.7 = (f32[2,48,128]{2,1,0:T(8,128)}, f32[2,48,128]{2,1,0:T(8,128)}, u32[]{:S(2)}, u32[]{:S(2)}) collective-permute-start(f32[2,48,128]{2,1,0:T(8,128)} %get-tuple-element.102), channel_id=1, source_target_pairs={{16,0},{17,1},{18,2},{19,3},{20,4},{21,5},{22,6},{23,7},{24,8},{25... | collective-permute-start | bytes 147464 | tf_op jit(solution)/shard_map/ppermute | solution.py:21
  104.5 40.6 %collective-permute-start.2 = (f32[3,18,48,1]{2,3,1,0:T(1,128)S(1)}, f32[3,18,48,1]{2,3,1,0:T(1,128)S(1)}, u32[]{:S(2)}, u32[]{:S(2)}) collective-permute-start(f32[3,18,48,1]{2,3,1,0:T(1,128)S(1)} %copy.29), channel_id=1, source_target_pairs={{0,4},{4,8},{8,12},{1,5},{5,9},{9,13},{2,6},{6,10},{10,14},{3,7},{... | collective-permute-start | bytes 31112 | tf_op jit(solution)/shard_map/ppermute | solution.py:19
  108.4 37.2 %collective-permute-start.3 = (f32[3,18,48,1]{2,3,1,0:T(1,128)S(1)}, f32[3,18,48,1]{2,3,1,0:T(1,128)S(1)}, u32[]{:S(2)}, u32[]{:S(2)}) collective-permute-start(f32[3,18,48,1]{2,3,1,0:T(1,128)S(1)} %copy.30), channel_id=1, source_target_pairs={{4,0},{8,4},{12,8},{5,1},{9,5},{13,9},{6,2},{10,6},{14,10},{7,3},{... | collective-permute-start | bytes 31112 | tf_op jit(solution)/shard_map/ppermute | solution.py:21
  202.0 21.7 %collective-permute-start.9 = (f32[20,48,2]{2,1,0:T(8,128)S(1)}, f32[20,48,2]{2,1,0:T(8,128)S(1)}, u32[]{:S(2)}, u32[]{:S(2)}) collective-permute-start(f32[20,48,2]{2,1,0:T(8,128)S(1)} %get-tuple-element.67), channel_id=1, source_target_pairs={{4,0},{8,4},{12,8},{5,1},{9,5},{13,9},{6,2},{10,6},{14,10},{7,3},{... | collective-permute-start | bytes 23048 | tf_op jit(solution)/shard_map/ppermute | solution.py:21
  207.1 29.7 %collective-permute-start.20 = (f32[18,48,1]{2,1,0:T(8,128)S(1)}, f32[18,48,1]{2,1,0:T(8,128)S(1)}, u32[]{:S(2)}, u32[]{:S(2)}) collective-permute-start(f32[18,48,1]{2,1,0:T(8,128)S(1)} %get-tuple-element.78), channel_id=1, source_target_pairs={{0,4},{4,8},{8,12},{1,5},{5,9},{9,13},{2,6},{6,10},{10,14},{3,7},{... | collective-permute-start | bytes 10376 | tf_op jit(solution)/shard_map/ppermute | solution.py:19
  209.0 33.6 %collective-permute-start.21 = (f32[18,48,1]{2,1,0:T(8,128)S(1)}, f32[18,48,1]{2,1,0:T(8,128)S(1)}, u32[]{:S(2)}, u32[]{:S(2)}) collective-permute-start(f32[18,48,1]{2,1,0:T(8,128)S(1)} %get-tuple-element.79), channel_id=1, source_target_pairs={{4,0},{8,4},{12,8},{5,1},{9,5},{13,9},{6,2},{10,6},{14,10},{7,3},{... | collective-permute-start | bytes 10376 | tf_op jit(solution)/shard_map/ppermute | solution.py:21
  223.9 24.8 %collective-permute-start.10 = (f32[20,2,132]{2,1,0:T(2,128)S(1)}, f32[20,2,132]{2,1,0:T(2,128)S(1)}, u32[]{:S(2)}, u32[]{:S(2)}) collective-permute-start(f32[20,2,132]{2,1,0:T(2,128)S(1)} %get-tuple-element.26), channel_id=1, source_target_pairs={{0,1},{1,2},{2,3},{4,5},{5,6},{6,7},{8,9},{9,10},{10,11},{12,13},{... | collective-permute-start | bytes 63368 | tf_op jit(solution)/shard_map/ppermute | solution.py:19
  227.1 21.7 %collective-permute-start.11 = (f32[20,2,132]{2,1,0:T(2,128)S(1)}, f32[20,2,132]{2,1,0:T(2,128)S(1)}, u32[]{:S(2)}, u32[]{:S(2)}) collective-permute-start(f32[20,2,132]{2,1,0:T(2,128)S(1)} %get-tuple-element.27), channel_id=1, source_target_pairs={{1,0},{2,1},{3,2},{5,4},{6,5},{7,6},{9,8},{10,9},{11,10},{13,12},{... | collective-permute-start | bytes 63368 | tf_op jit(solution)/shard_map/ppermute | solution.py:21
  260.8 17.4 %collective-permute-start.26 = (f32[20,48,2]{2,1,0:T(8,128)S(1)}, f32[20,48,2]{2,1,0:T(8,128)S(1)}, u32[]{:S(2)}, u32[]{:S(2)}) collective-permute-start(f32[20,48,2]{2,1,0:T(8,128)S(1)} %get-tuple-element.64), channel_id=1, source_target_pairs={{0,4},{4,8},{8,12},{1,5},{5,9},{9,13},{2,6},{6,10},{10,14},{3,7},{... | collective-permute-start | bytes 23048 | tf_op jit(solution)/shard_map/ppermute | solution.py:19
  262.8 21.6 %collective-permute-start.27 = (f32[20,48,2]{2,1,0:T(8,128)S(1)}, f32[20,48,2]{2,1,0:T(8,128)S(1)}, u32[]{:S(2)}, u32[]{:S(2)}) collective-permute-start(f32[20,48,2]{2,1,0:T(8,128)S(1)} %get-tuple-element.65), channel_id=1, source_target_pairs={{4,0},{8,4},{12,8},{5,1},{9,5},{13,9},{6,2},{10,6},{14,10},{7,3},{... | collective-permute-start | bytes 23048 | tf_op jit(solution)/shard_map/ppermute | solution.py:21
  304.3 17.4 %collective-permute-start.32 = (f32[20,48,2]{2,1,0:T(8,128)S(1)}, f32[20,48,2]{2,1,0:T(8,128)S(1)}, u32[]{:S(2)}, u32[]{:S(2)}) collective-permute-start(f32[20,48,2]{2,1,0:T(8,128)S(1)} %get-tuple-element.62), channel_id=1, source_target_pairs={{0,4},{4,8},{8,12},{1,5},{5,9},{9,13},{2,6},{6,10},{10,14},{3,7},{... | collective-permute-start | bytes 23048 | tf_op jit(solution)/shard_map/ppermute | solution.py:19
  306.2 21.6 %collective-permute-start.33 = (f32[20,48,2]{2,1,0:T(8,128)S(1)}, f32[20,48,2]{2,1,0:T(8,128)S(1)}, u32[]{:S(2)}, u32[]{:S(2)}) collective-permute-start(f32[20,48,2]{2,1,0:T(8,128)S(1)} %get-tuple-element.63), channel_id=1, source_target_pairs={{4,0},{8,4},{12,8},{5,1},{9,5},{13,9},{6,2},{10,6},{14,10},{7,3},{... | collective-permute-start | bytes 23048 | tf_op jit(solution)/shard_map/ppermute | solution.py:21
  346.0 17.4 %collective-permute-start.38 = (f32[20,48,2]{2,1,0:T(8,128)S(1)}, f32[20,48,2]{2,1,0:T(8,128)S(1)}, u32[]{:S(2)}, u32[]{:S(2)}) collective-permute-start(f32[20,48,2]{2,1,0:T(8,128)S(1)} %get-tuple-element.60), channel_id=1, source_target_pairs={{0,4},{4,8},{8,12},{1,5},{5,9},{9,13},{2,6},{6,10},{10,14},{3,7},{... | collective-permute-start | bytes 23048 | tf_op jit(solution)/shard_map/ppermute | solution.py:19
  347.9 21.6 %collective-permute-start.39 = (f32[20,48,2]{2,1,0:T(8,128)S(1)}, f32[20,48,2]{2,1,0:T(8,128)S(1)}, u32[]{:S(2)}, u32[]{:S(2)}) collective-permute-start(f32[20,48,2]{2,1,0:T(8,128)S(1)} %get-tuple-element.61), channel_id=1, source_target_pairs={{4,0},{8,4},{12,8},{5,1},{9,5},{13,9},{6,2},{10,6},{14,10},{7,3},{... | collective-permute-start | bytes 23048 | tf_op jit(solution)/shard_map/ppermute | solution.py:21
  393.8 22.3 %collective-permute-start.45 = (f32[18,48,1]{2,1,0:T(8,128)S(1)}, f32[18,48,1]{2,1,0:T(8,128)S(1)}, u32[]{:S(2)}, u32[]{:S(2)}) collective-permute-start(f32[18,48,1]{2,1,0:T(8,128)S(1)} %get-tuple-element.76), channel_id=1, source_target_pairs={{0,4},{4,8},{8,12},{1,5},{5,9},{9,13},{2,6},{6,10},{10,14},{3,7},{... | collective-permute-start | bytes 10376 | tf_op jit(solution)/shard_map/ppermute | solution.py:19
  426.5 77.2 %collective-permute-start.48 = (f32[3,1,48,128]{3,2,1,0:T(8,128)S(1)}, f32[3,1,48,128]{3,2,1,0:T(8,128)S(1)}, u32[]{:S(2)}, u32[]{:S(2)}) collective-permute-start(f32[3,1,48,128]{3,2,1,0:T(8,128)S(1)} %get-tuple-element.47), channel_id=1, source_target_pairs={{16,0},{17,1},{18,2},{19,3},{20,4},{21,5},{22,6},{23,7},{24,8},{25... | collective-permute-start | bytes 221192 | tf_op jit(solution)/shard_map/ppermute | solution.py:21
  427.8 75.9 %collective-permute-start.49 = (f32[3,1,48,128]{3,2,1,0:T(8,128)S(1)}, f32[3,1,48,128]{3,2,1,0:T(8,128)S(1)}, u32[]{:S(2)}, u32[]{:S(2)}) collective-permute-start(f32[3,1,48,128]{3,2,1,0:T(8,128)S(1)} %get-tuple-element.46), channel_id=1, source_target_pairs={{0,16},{1,17},{2,18},{3,19},{4,20},{5,21},{6,22},{7,23},{8,24},{9,... | collective-permute-start | bytes 221192 | tf_op jit(solution)/shard_map/ppermute | solution.py:19
  498.7 27.7 %all-to-all-start.2 = ((f32[8,64,128]{2,1,0:T(8,128)}), f32[8,64,128]{2,1,0:T(8,128)S(1)}, u32[]{:S(2)}, u32[]{:S(2)}) async-start(f32[8,64,128]{2,1,0:T(8,128)} %scatter_fusion.2), calls=%async_computation.2 | async-start | bytes 524288 | tf_op jit(solution)/shard_map/all_to_all | solution.py:97
  582.1 21.7 %collective-permute-start.57 = (f32[20,48,2]{2,1,0:T(8,128)S(1)}, f32[20,48,2]{2,1,0:T(8,128)S(1)}, u32[]{:S(2)}, u32[]{:S(2)}) collective-permute-start(f32[20,48,2]{2,1,0:T(8,128)S(1)} %get-tuple-element.59), channel_id=1, source_target_pairs={{4,0},{8,4},{12,8},{5,1},{9,5},{13,9},{6,2},{10,6},{14,10},{7,3},{... | collective-permute-start | bytes 23048 | tf_op jit(solution)/shard_map/ppermute | solution.py:21
  587.2 29.7 %collective-permute-start.68 = (f32[18,48,1]{2,1,0:T(8,128)S(1)}, f32[18,48,1]{2,1,0:T(8,128)S(1)}, u32[]{:S(2)}, u32[]{:S(2)}) collective-permute-start(f32[18,48,1]{2,1,0:T(8,128)S(1)} %get-tuple-element.72), channel_id=1, source_target_pairs={{0,4},{4,8},{8,12},{1,5},{5,9},{9,13},{2,6},{6,10},{10,14},{3,7},{... | collective-permute-start | bytes 10376 | tf_op jit(solution)/shard_map/ppermute | solution.py:19
  589.1 33.6 %collective-permute-start.69 = (f32[18,48,1]{2,1,0:T(8,128)S(1)}, f32[18,48,1]{2,1,0:T(8,128)S(1)}, u32[]{:S(2)}, u32[]{:S(2)}) collective-permute-start(f32[18,48,1]{2,1,0:T(8,128)S(1)} %get-tuple-element.73), channel_id=1, source_target_pairs={{4,0},{8,4},{12,8},{5,1},{9,5},{13,9},{6,2},{10,6},{14,10},{7,3},{... | collective-permute-start | bytes 10376 | tf_op jit(solution)/shard_map/ppermute | solution.py:21
  604.0 25.0 %collective-permute-start.58 = (f32[20,2,132]{2,1,0:T(2,128)S(1)}, f32[20,2,132]{2,1,0:T(2,128)S(1)}, u32[]{:S(2)}, u32[]{:S(2)}) collective-permute-start(f32[20,2,132]{2,1,0:T(2,128)S(1)} %get-tuple-element.18), channel_id=1, source_target_pairs={{0,1},{1,2},{2,3},{4,5},{5,6},{6,7},{8,9},{9,10},{10,11},{12,13},{... | collective-permute-start | bytes 63368 | tf_op jit(solution)/shard_map/ppermute | solution.py:19
  606.1 23.0 %collective-permute-start.59 = (f32[20,2,132]{2,1,0:T(2,128)S(1)}, f32[20,2,132]{2,1,0:T(2,128)S(1)}, u32[]{:S(2)}, u32[]{:S(2)}) collective-permute-start(f32[20,2,132]{2,1,0:T(2,128)S(1)} %get-tuple-element.19), channel_id=1, source_target_pairs={{1,0},{2,1},{3,2},{5,4},{6,5},{7,6},{9,8},{10,9},{11,10},{13,12},{... | collective-permute-start | bytes 63368 | tf_op jit(solution)/shard_map/ppermute | solution.py:21
  642.2 21.6 %collective-permute-start.75 = (f32[20,48,2]{2,1,0:T(8,128)S(1)}, f32[20,48,2]{2,1,0:T(8,128)S(1)}, u32[]{:S(2)}, u32[]{:S(2)}) collective-permute-start(f32[20,48,2]{2,1,0:T(8,128)S(1)} %get-tuple-element.57), channel_id=1, source_target_pairs={{4,0},{8,4},{12,8},{5,1},{9,5},{13,9},{6,2},{10,6},{14,10},{7,3},{... | collective-permute-start | bytes 23048 | tf_op jit(solution)/shard_map/ppermute | solution.py:21
  684.1 21.6 %collective-permute-start.81 = (f32[20,48,2]{2,1,0:T(8,128)S(1)}, f32[20,48,2]{2,1,0:T(8,128)S(1)}, u32[]{:S(2)}, u32[]{:S(2)}) collective-permute-start(f32[20,48,2]{2,1,0:T(8,128)S(1)} %get-tuple-element.55), channel_id=1, source_target_pairs={{4,0},{8,4},{12,8},{5,1},{9,5},{13,9},{6,2},{10,6},{14,10},{7,3},{... | collective-permute-start | bytes 23048 | tf_op jit(solution)/shard_map/ppermute | solution.py:21
  723.9 17.6 %collective-permute-start.86 = (f32[20,48,2]{2,1,0:T(8,128)S(1)}, f32[20,48,2]{2,1,0:T(8,128)S(1)}, u32[]{:S(2)}, u32[]{:S(2)}) collective-permute-start(f32[20,48,2]{2,1,0:T(8,128)S(1)} %get-tuple-element.52), channel_id=1, source_target_pairs={{0,4},{4,8},{8,12},{1,5},{5,9},{9,13},{2,6},{6,10},{10,14},{3,7},{... | collective-permute-start | bytes 23048 | tf_op jit(solution)/shard_map/ppermute | solution.py:19
  726.1 21.6 %collective-permute-start.87 = (f32[20,48,2]{2,1,0:T(8,128)S(1)}, f32[20,48,2]{2,1,0:T(8,128)S(1)}, u32[]{:S(2)}, u32[]{:S(2)}) collective-permute-start(f32[20,48,2]{2,1,0:T(8,128)S(1)} %get-tuple-element.53), channel_id=1, source_target_pairs={{4,0},{8,4},{12,8},{5,1},{9,5},{13,9},{6,2},{10,6},{14,10},{7,3},{... | collective-permute-start | bytes 23048 | tf_op jit(solution)/shard_map/ppermute | solution.py:21
  771.9 22.3 %collective-permute-start.93 = (f32[18,48,1]{2,1,0:T(8,128)S(1)}, f32[18,48,1]{2,1,0:T(8,128)S(1)}, u32[]{:S(2)}, u32[]{:S(2)}) collective-permute-start(f32[18,48,1]{2,1,0:T(8,128)S(1)} %get-tuple-element.70), channel_id=1, source_target_pairs={{0,4},{4,8},{8,12},{1,5},{5,9},{9,13},{2,6},{6,10},{10,14},{3,7},{... | collective-permute-start | bytes 10376 | tf_op jit(solution)/shard_map/ppermute | solution.py:19
  (96 other events, 1353.8 us)
where the time goes:
time: 823 us; the launch traced here: 810 us
  starting transfers between devices  272 us (33%)
  waiting for transfers between devices  233 us (28%)
  local copies, waits for them, and re-layouts  137 us (17%)
  other arithmetic  82.1 us (10%)
  blocking collectives  79.4 us (10%)
    ppermute x48, starting transfers between devices, extended(): lax.ppermute(head, axis, [((i + 1) % count, i) for i in range(ends)])  155 us
    ppermute x48, waiting for transfers between devices, extended(): lax.ppermute(tail, axis, [(i, (i + 1) % count) for i in range(ends)])  124 us
    ppermute x48, waiting for transfers between devices, extended(): lax.ppermute(head, axis, [((i + 1) % count, i) for i in range(ends)])  109 us
    ppermute x48, starting transfers between devices, extended(): lax.ppermute(tail, axis, [(i, (i + 1) % count) for i in range(ends)])  104 us
    psum x2, blocking collectives, body(): total = lax.psum(partial_sum, ('gx', 'gy', 'gz'))  79.4 us
    scatter x2, local copies, waits for them, and re-layouts, body(): jnp.zeros((peers, capacity, cells_y), jnp.float32).at[target, slot_index]  56 us
    scatter x1, local copies, waits for them, and re-layouts, body(): jnp.zeros((peers, capacity), jnp.int32).at[target, slot_index].set(lines)  38.7 us
    mul x8, other arithmetic, body(): middle = (neighbours(deeper) - source_wide) / 6.0 * inside  34.5 us
  transfers between devices with their start and end apart: 99, of which 50 were waited for; matrix products, arithmetic and copies ran while one was open for 19% of the time, Pallas kernels for 0%

commit v1 on v0

v1 whole, which is shorter than its diff:
```python
import functools
import math

import jax
import jax.numpy as jnp
from jax import lax
from jax.experimental import pallas as pl
from jax.experimental.pallas import tpu as pltpu
from jax.sharding import PartitionSpec as P

BAND = 32
STEPS = 2
SWEEPS = 8
TIME_STEP = 0.4
VISCOSITY = 0.05
HA = 2
HB = SWEEPS
ZP = 8
F32 = jnp.float32
BF16 = jnp.bfloat16


def call(kernel, outs, args, smem=(0,), scratch=(), name=None):
    specs = [
        pl.BlockSpec(memory_space=pltpu.SMEM if i in smem else pltpu.VMEM) for i in range(len(args))
    ]
    size = sum(a.size * 4 for a in args) + sum(math.prod(o) * 4 for o in outs)
    return pl.pallas_call(
        kernel,
        out_shape=[jax.ShapeDtypeStruct(o, F32) for o in outs],
        in_specs=specs,
        out_specs=[pl.BlockSpec(memory_space=pltpu.VMEM)] * len(outs),
        scratch_shapes=list(scratch),
        name=name,
        cost_estimate=pl.CostEstimate(flops=size, bytes_accessed=size, transcendentals=0),
        compiler_params=pltpu.CompilerParams(vmem_limit_bytes=48 << 20),
    )(*args)


def lanes_of(shape):
    return lax.broadcasted_iota(jnp.int32, shape, len(shape) - 1)


def rows_of(shape):
    return lax.broadcasted_iota(jnp.int32, shape, len(shape) - 2)


def roll(value, shift, axis):
    shift = shift % value.shape[axis]
    return pltpu.roll(value, shift, axis) if shift else value


def split3(value):
    high = value.astype(BF16)
    rest = value - high.astype(F32)
    middle = rest.astype(BF16)
    return high, middle, (rest - middle.astype(F32)).astype(BF16)


def dot0(left, right):
    return lax.dot_general(left, right, (((0,), (0,)), ((), ())), preferred_element_type=F32)


class Axis:
    def __init__(self, name):
        self.name = name
        self.count = n = lax.axis_size(name)
        self.first = [(i, i ^ 1) for i in range(n)]
        self.second = [((2 * i + 1) % n, (2 * i + 2) % n) for i in range(n // 2)]
        self.second = self.second + [(b, a) for a, b in self.second]
        self.perms = [self.first] if n == 2 else [self.first, self.second]
        self.fold = n in (2, 4)
        self.cross = [(i, i ^ 2) for i in range(n)] if n == 4 else None

    def swap(self, sends):
        return [lax.ppermute(s, self.name, p) for s, p in zip(sends, self.perms)]


def pick_side(index, high, low, which):
    even = (index % 2) == 0
    return jnp.where(even == (which == 0), high, low)


def from_sides(index, count, received, zero):
    even = (index % 2) == 0
    other = received[1] if len(received) > 1 else received[0]
    upper = jnp.where(even, received[0], other)
    lower = jnp.where(even, other, received[0])
    lower = jnp.where(index > 0, lower, zero)
    upper = jnp.where(index < count - 1, upper, zero)
    return lower, upper


def inflow_parts(info, column_of, inflow_x, inflow_y, cells_x, width):
    turbines = inflow_x.shape[0]
    where_x = inflow_x - info[0] * cells_x
    place = lanes_of((turbines, width)) + info[1] * width
    band = (place >= inflow_y) & (place < inflow_y + BAND)
    total = jnp.zeros((turbines, width), F32)
    for x in range(cells_x):
        total = total + jnp.where(where_x == x, column_of(x), 0.0)
    return jnp.where(band, total, 0.0)


def fill_xsend(info, sends, planes, parts, cells_x, cells_z):
    for which, out in enumerate(sends):
        start = pick_side(info[0], cells_x - HA, 0, which)
        for f in range(4):
            for k in range(HA):
                row = (f * HA + k) * cells_z
                out[row : row + cells_z, :] = planes(f, start + k)
        base = 4 * HA * cells_z
        out[base:, :] = parts


def begin_kernel(nsend, info, vel, press, inx, iny, *outs):
    _, cells_x, cells_z, width = vel.shape
    parts = inflow_parts(
        info,
        lambda x: jnp.sum(vel[0, x], axis=0, keepdims=True),
        inx[...],
        iny[...],
        cells_x,
        width,
    )
    outs[0][...] = parts
    planes = lambda f, x: vel[f, x] if f < 3 else press[x]
    fill_xsend(info, outs[1 : 1 + nsend], planes, parts, cells_x, cells_z)


def pack_kernel(peers, capacity, info, kern, owners, lines, turbine, out):
    rows, width = kern.shape
    slots = peers * capacity
    wide = -(-peers // 128) * 128
    owner = owners[...]
    landing = (owner == lanes_of((rows, wide))).astype(F32)
    strict = (lanes_of((rows, rows)) < rows_of((rows, rows))).astype(BF16)
    earlier = jnp.dot(strict, landing.astype(BF16), preferred_element_type=F32)
    slot = jnp.sum(earlier * landing, axis=1, keepdims=True).astype(jnp.int32)
    live = rows_of((rows, 1)) < info[3]
    dest = jnp.where(live, owner * capacity + slot, -1)
    chosen = (dest == lanes_of((rows, slots))).astype(BF16)
    packed = sum(dot0(chosen, part) for part in split3(kern[...]))
    row8 = rows_of((8, rows))
    meta = jnp.where(row8 == 0, lines[...] + 1, jnp.where(row8 == 1, turbine[...], 0)).astype(F32)
    meta = sum(
        jnp.dot(part, chosen, preferred_element_type=F32) for part in split3(meta)[:2]
    )
    block = capacity + 8
    lane = lanes_of((8, 128))
    for peer in range(peers):
        out[peer * block : peer * block + capacity, :] = packed[
            peer * capacity : (peer + 1) * capacity, :
        ]
        at = peer * capacity
        piece = roll(meta[:, at // 128 * 128 : at // 128 * 128 + 128], -(at % 128), 1)
        out[peer * block + capacity : (peer + 1) * block, :] = jnp.where(lane < capacity, piece, 0.0)


def pack_lanes(plane, count, width, depth):
    per = width // depth
    highs, lows = [], []
    for base in range(0, count, per):
        high = low = None
        for k in range(min(per, count - base)):
            value = plane(base + k)
            lane = lanes_of(value.shape) // depth
            if high is None:
                high = low = jnp.zeros_like(value)
            high = jnp.where(lane == k, roll(value, k * depth + depth, 1), high)
            low = jnp.where(lane == k, roll(value, k * depth, 1), low)
        highs.append(high)
        lows.append(low)
    return highs, lows


def unpack_lanes(lower, upper, k, depth):
    width = upper.shape[-1]
    per = width // depth
    at = (k % per) * depth
    lane = lanes_of(upper.shape)
    tile = jnp.where(lane < depth, roll(upper, -at, 1), 0.0)
    return jnp.where(lane >= width - depth, roll(lower, -at - depth, 1), tile)


def total_of(own, received, fold, base):
    if not fold:
        return own
    for r in received:
        own = own + r[base:, :]
    return own


def ext_plane(vel, press, halo, f, xe, cells_x):
    x = xe - HA
    if 0 <= x < cells_x:
        return vel[f, x] if f < 3 else press[x]
    return halo(f, x)


def x_halo(info, count, received, cells_x, cells_z):
    def halo(f, x):
        k = x % cells_x if x >= 0 else x + HA
        k = x - cells_x if x >= 0 else x + HA
        row = (f * HA + k) * cells_z
        pieces = [r[row : row + cells_z, :] for r in received]
        lower, upper = from_sides(info[0], count, pieces, 0.0)
        return upper if x >= 0 else lower

    return halo


def halo_y_kernel(ax, ay, info, vel, press, parts, *refs):
    nx = len(ax.perms)
    xr, outs = refs[:nx], refs[nx:]
    _, cells_x, cells_z, width = vel.shape
    ext = cells_x + 2 * HA
    base = 4 * HA * cells_z
    total = total_of(parts[...], xr, ax.fold, base)
    halo = x_halo(info, ax.count, xr, cells_x, cells_z)
    plane = lambda i: ext_plane(vel, press, halo, i // ext, i % ext, cells_x)
    highs, lows = pack_lanes(plane, 4 * ext, width, HA)
    outs[0][...] = total
    for which in range(len(ay.perms)):
        out = outs[1 + which]
        for i, (high, low) in enumerate(zip(highs, lows)):
            out[i * cells_z : (i + 1) * cells_z, :] = pick_side(info[1], high, low, which)
        out[len(highs) * cells_z :, :] = total


def halo_z_kernel(ax, ay, az, npack, info, vel, press, parts, *refs):
    nx, ny = len(ax.perms), len(ay.perms)
    ncross = 1 if ay.cross else 0
    xr, yr, cross = refs[:nx], refs[nx : nx + ny], refs[nx + ny : nx + ny + ncross]
    outs = refs[nx + ny + ncross :]
    _, cells_x, cells_z, width = vel.shape
    ext = cells_x + 2 * HA
    total = total_of(parts[...], yr, ay.fold, npack * cells_z)
    for c in cross:
        total = total + c[...]
    halo = x_halo(info, ax.count, xr, cells_x, cells_z)
    outs[0][...] = total
    for which in range(len(az.perms)):
        out = outs[1 + which]
        for i in range(4 * ext):
            value = ext_plane(vel, press, halo, i // ext, i % ext, cells_x)
            out[i * HA : (i + 1) * HA, :] = pick_side(
                info[2], value[cells_z - HA :, :], value[:HA, :], which
            )
        row = 4 * ext * HA
        for j in range(ny):
            for i in range(npack):
                value = yr[j][i * cells_z : (i + 1) * cells_z, :]
                out[row : row + HA, :] = pick_side(
                    info[2], value[cells_z - HA :, :], value[:HA, :], which
                )
                row += HA
        pad = out.shape[0] - total.shape[0]
        if pad > row:
            out[row:pad, :] = jnp.zeros((pad - row, width), F32)
        out[pad:, :] = total


def force_field(rows, thrust, total, depth_total, peers, capacity, lines_total):
    turbines = thrust.shape[0]
    width = rows.shape[-1]
    slots = peers * capacity
    block = capacity + 8
    uref = jnp.sum(total, axis=1, keepdims=True) / (BAND * depth_total)
    magnitude = 0.5 * thrust * uref * jnp.abs(uref)
    magnitude = jnp.broadcast_to(magnitude, (turbines, width))
    mag_parts = split3(magnitude)
    force = jnp.zeros((lines_total, width), F32)
    for first in range(0, slots, 128):
        line = jnp.zeros((8, 128), F32)
        values = []
        for at in range(first, min(first + 128, slots), capacity):
            peer = at // capacity
            line = line + roll(
                rows[peer * block + capacity : (peer + 1) * block, :], at - first, 1
            )
            values.append(rows[peer * block : peer * block + capacity, :])
        values = jnp.concatenate(values, axis=0) if len(values) > 1 else values[0]
        used = values.shape[0]
        line = line.astype(jnp.int32)
        turbine = line[1:2, :used]
        line = line[0:1, :used]
        chosen = (rows_of((turbines, used)) == turbine).astype(BF16)
        scale = sum(dot0(chosen, part) for part in mag_parts)
        values = split3(values * scale)
        landing = (rows_of((lines_total, used)) == line - 1).astype(BF16)
        for part in values[:2]:
            force = force + jnp.dot(landing, part, preferred_element_type=F32)
    return force


def star_kernel(ax, ay, az, npack, peers, capacity, info, vel, press, parts, rows, thrust, *refs):
    nx, ny, nz = len(ax.perms), len(ay.perms), len(az.perms)
    ncross = 1 if az.cross else 0
    xr, refs = refs[:nx], refs[nx:]
    yr, refs = refs[:ny], refs[ny:]
    zr, refs = refs[:nz], refs[nz:]
    cross, refs = refs[:ncross], refs[ncross:]
    star, p1, s6, edge = refs[:4]
    sends = refs[4 : 4 + nx]
    field, su, force_ref, ylow, yhigh = refs[4 + nx :]
    _, cells_x, cells_z, width = vel.shape
    ext = cells_x + 2 * HA
    tall = cells_z + 2 * ZP
    zbase = zr[0].shape[0] - parts.shape[0]
    total = total_of(parts[...], zr, az.fold, zbase)
    for c in cross:
        total = total + c[...]
    force_ref[...] = force_field(
        rows, thrust[...], total, cells_z * az.count, peers, capacity, cells_x * cells_z
    )
    halo = x_halo(info, ax.count, xr, cells_x, cells_z)

    def z_rows(row):
        return from_sides(info[2], az.count, [r[row : row + HA, :] for r in zr], 0.0)

    corner = 4 * ext * HA
    ylow[...] = jnp.zeros_like(ylow)
    yhigh[...] = jnp.zeros_like(yhigh)
    for i in range(npack):
        lower, upper = from_sides(
            info[1], ay.count, [r[i * cells_z : (i + 1) * cells_z, :] for r in yr], 0.0
        )
        ylow[i, ZP : ZP + cells_z, :] = lower
        yhigh[i, ZP : ZP + cells_z, :] = upper
        sides = [z_rows(corner + (j * npack + i) * HA) for j in range(ny)]
        for k, rows_at in ((0, slice(ZP - HA, ZP)), (1, slice(ZP + cells_z, ZP + cells_z + HA))):
            lower, upper = from_sides(info[1], ay.count, [s[k] for s in sides], 0.0)
            ylow[i, rows_at, :] = lower
            yhigh[i, rows_at, :] = upper
    per = width // HA
    blank = jnp.zeros((ZP, width), F32)
    for i in range(4 * ext):
        f, xe = i // ext, i % ext
        field[f, xe, :ZP, :width] = blank
        field[f, xe, ZP + cells_z :, :width] = blank
        field[f, xe, ZP : ZP + cells_z, :width] = ext_plane(vel, press, halo, f, xe, cells_x)
        lower, upper = z_rows(i * HA)
        field[f, xe, ZP - HA : ZP, :width] = lower
        field[f, xe, ZP + cells_z : ZP + cells_z + HA, :width] = upper
        field[f, xe, :, width:] = unpack_lanes(ylow[i // per], yhigh[i // per], i, HA)

    rate = TIME_STEP * VISCOSITY

    def around(f, xe):
        mid = field[f, xe]
        total = field[f, xe - 1] + field[f, xe + 1]
        total = total + (roll(mid, 1, 0) + roll(mid, -1, 0))
        return total + (roll(mid, 1, 1) + roll(mid, -1, 1)), mid

    def diffused(f, xe):
        total, mid = around(f, xe)
        return mid + rate * (total - 6.0 * mid)

    own = slice(ZP, ZP + cells_z)

    def u_plane(k, carry):
        su[k] = diffused(0, k + HA - 1)[own, :width]
        return carry

    lax.fori_loop(0, cells_x + 2, u_plane, 0)
    su[0] = jnp.where(info[0] > 0, su[0], 0.0)
    su[cells_x + 1] = jnp.where(info[0] < ax.count - 1, su[cells_x + 1], 0.0)
    lane = lanes_of((cells_z, 2 * width))
    keep_y = ((info[1] > 0) | (lane < width + width // 2)) & (
        (info[1] < ay.count - 1) | (lane < width) | (lane >= width + width // 2)
    )
    row = rows_of((tall, width))
    keep_z = ((info[2] > 0) | (row >= ZP)) & ((info[2] < az.count - 1) | (row < ZP + cells_z))

    def forced(x, carry):
        push = force_ref[pl.ds(pl.multiple_of(x * cells_z, 8), cells_z), :]
        u = su[x + 1] - TIME_STEP * push
        su[x + 1] = u
        star[0, x] = u
        v = jnp.where(keep_y, diffused(1, x + HA)[own, :], 0.0)
        star[1, x] = v[:, :width]
        div = (roll(v, -1, 1) - roll(v, 1, 1))[:, :width]
        w = jnp.where(keep_z, diffused(2, x + HA)[:, :width], 0.0)
        star[2, x] = w[own, :]
        div = div + (roll(w, -1, 0) - roll(w, 1, 0))[own, :]
        s6[x] = div
        return carry

    lax.fori_loop(0, cells_x, forced, 0)

    def first(x, carry):
        source = (s6[x] + (su[x + 2] - su[x])) * (0.5 / 6.0)
        s6[x] = source
        total, _ = around(3, x + HA)
        p1[x] = total[own, :width] * (1.0 / 6.0) - source
        return carry

    lax.fori_loop(0, cells_x, first, 0)
    scale = 0.5 * TIME_STEP / 6.0
    edge[0] = scale * force_ref[:cells_z, :]
    edge[1] = scale * force_ref[(cells_x - 1) * cells_z :, :]
    for which, out in enumerate(sends):
        start = pick_side(info[0], cells_x - HB, 0, which)
        out[:HB] = p1[pl.ds(start, HB)]
        out[HB : 2 * HB] = s6[pl.ds(start, HB)]
        out[2 * HB] = pick_side(info[0], edge[1], edge[0], which)


def deep_y_kernel(ax, ay, info, p1, s6, edge, *refs):
    nx = len(ax.perms)
    xr, refs = refs[:nx], refs[nx:]
    px, sx = refs[:2]
    sends = refs[2:]
    cells_x, cells_z, width = p1.shape
    one_sided = ax.count == 2
    ext = px.shape[0]
    off = jnp.where(info[0] == 0, 0, HB) if one_sided else HB
    px[pl.ds(off, cells_x)] = p1[...]
    sx[pl.ds(off, cells_x)] = s6[...]
    if one_sided:
        away = jnp.where(info[0] == 0, cells_x, 0)
        px[pl.ds(away, HB)] = xr[0][:HB]
        sx[pl.ds(away, HB)] = xr[0][HB : 2 * HB]
        near = [(True, info[0] == 0)]
    else:
        for k in range(HB):
            lower, upper = from_sides(info[0], ax.count, [r[k] for r in xr], 0.0)
            px[k] = lower
            px[HB + cells_x + k] = upper
            lower, upper = from_sides(info[0], ax.count, [r[HB + k] for r in xr], 0.0)
            sx[k] = lower
            sx[HB + cells_x + k] = upper
    lower, upper = from_sides(info[0], ax.count, [r[2 * HB] for r in xr], 0.0)
    has_lower = (info[0] > 0).astype(F32)
    has_upper = (info[0] < ax.count - 1).astype(F32)
    changes = [
        (off, lower),
        (off + cells_x - 1, -upper),
        (jnp.maximum(off - 1, 0), -edge[0] * has_lower),
        (jnp.minimum(off + cells_x, ext - 1), edge[1] * has_upper),
    ]
    for at, change in changes:
        sx[at] = sx[at] + change
        px[at] = px[at] - change
    plane = lambda i: px[i] if i < ext else sx[i - ext]
    highs, lows = pack_lanes(plane, 2 * ext, width, HB)
    for which in range(len(ay.perms)):
        for i, (high, low) in enumerate(zip(highs, lows)):
            sends[which][i * cells_z : (i + 1) * cells_z, :] = pick_side(info[1], high, low, which)


def deep_z_kernel(ay, az, npack, info, px, sx, *refs):
    ny = len(ay.perms)
    yr, sends = refs[:ny], refs[ny:]
    ext, cells_z, width = px.shape
    for which in range(len(az.perms)):
        out = sends[which]
        start = pl.multiple_of(pick_side(info[2], cells_z - HB, 0, which), 8)
        out[:ext] = px[:, pl.ds(start, HB), :]
        out[ext : 2 * ext] = sx[:, pl.ds(start, HB), :]
        for j in range(ny):
            for i in range(npack):
                at = pl.multiple_of(i * cells_z + start, 8)
                out[2 * ext + j * npack + i] = yr[j][pl.ds(at, HB), :]


def sweep_kernel(ax, ay, az, npack, last, info, px, sx, star, inx, iny, *refs):
    ny, nz = len(ay.perms), len(az.perms)
    yr, refs = refs[:ny], refs[ny:]
    zr, refs = refs[:nz], refs[nz:]
    vel, press = refs[:2]
    refs = refs[2:]
    if not last:
        parts, refs = refs[0], refs[1:]
        sends, refs = refs[: len(ax.perms)], refs[len(ax.perms) :]
    pe, se, ylow, yhigh, cref = refs
    ext, cells_z, width = px.shape
    cells_x = press.shape[0]
    one_sided = ax.count == 2
    off = jnp.where(info[0] == 0, 0, HB) if one_sided else HB
    tall = cells_z + 2 * ZP
    own = slice(ZP, ZP + cells_z)

    def z_tile(k):
        return from_sides(info[2], az.count, [r[k] for r in zr], 0.0)

    for i in range(npack):
        lower, upper = from_sides(
            info[1], ay.count, [r[i * cells_z : (i + 1) * cells_z, :] for r in yr], 0.0
        )
        ylow[i, own, :] = lower
        yhigh[i, own, :] = upper
        sides = [z_tile(2 * ext + j * npack + i) for j in range(ny)]
        for k, rows_at in ((0, slice(0, ZP)), (1, slice(ZP + cells_z, tall))):
            lower, upper = from_sides(info[1], ay.count, [s[k] for s in sides], 0.0)
            ylow[i, rows_at, :] = lower
            yhigh[i, rows_at, :] = upper
    per = width // HB
    blank = jnp.zeros((tall, 2 * width), F32)
    pe[0] = blank
    pe[ext + 1] = blank
    for i in range(2 * ext):
        out, at, source = (pe, i + 1, px) if i < ext else (se, i - ext, sx)
        lower, upper = z_tile(i)
        out[at, :ZP, :width] = lower
        out[at, ZP + cells_z :, :width] = upper
        out[at, own, :width] = source[i % ext]
        out[at, :, width:] = unpack_lanes(ylow[i // per], yhigh[i // per], i, HB)
    shape = (tall, 2 * width)
    row, lane = rows_of(shape), lanes_of(shape)
    keep = ((info[2] > 0) | (row >= ZP)) & ((info[2] < az.count - 1) | (row < ZP + cells_z))
    keep &= (lane < width) | ((lane < width + HB) & (info[1] < ay.count - 1)) | (
        (lane >= 2 * width - HB) & (info[1] > 0)
    )
    cref[...] = jnp.where(keep, 1.0 / 6.0, 0.0)

    def around(mid):
        total = roll(mid, 1, 0) + roll(mid, -1, 0)
        return total + (roll(mid, 1, 1) + roll(mid, -1, 1))

    def sweep(number, carry):
        reach = SWEEPS - number
        start = jnp.maximum(off - reach, 0)
        stop = jnp.minimum(off + cells_x + reach, ext)

        def plane(xe, old):
            before, mid = old
            after = pe[xe + 2]
            total = (before + after) + around(mid)
            new = total * cref[...] - se[xe]
            if not one_sided:
                place = info[0] * cells_x + xe - HB
                new = jnp.where((place >= 0) & (place < ax.count * cells_x), new, 0.0)
            pe[xe + 1] = new
            return mid, after

        lax.fori_loop(start, stop, plane, (pe[start], pe[start + 1]))
        return carry

    lax.fori_loop(1, SWEEPS, sweep, 0)

    def gradient(x, carry):
        at = x + off + 1
        mid = pe[at]
        press[x] = mid[own, :width]
        vel[0, x] = star[0, x] - 0.5 * (pe[at + 1] - pe[at - 1])[own, :width]
        vel[1, x] = star[1, x] - 0.5 * (roll(mid, -1, 1) - roll(mid, 1, 1))[own, :width]
        vel[2, x] = star[2, x] - 0.5 * (roll(mid, -1, 0) - roll(mid, 1, 0))[own, :width]
        return carry

    lax.fori_loop(0, cells_x, gradient, 0)
    if not last:
        share = inflow_parts(
            info,
            lambda x: jnp.sum(vel[0, x], axis=0, keepdims=True),
            inx[...],
            iny[...],
            cells_x,
            width,
        )
        parts[...] = share
        planes = lambda f, x: vel[f, x] if f < 3 else press[x]
        fill_xsend(info, sends, planes, share, cells_x, cells_z)


def body(
    velocity, pressure, kernel, owners, lines, point_turbine, row_counts, thrust, inflow_x, inflow_y
):
    _, cells_x, cells_z, width = velocity.shape
    row_total = kernel.shape[0]
    turbines = thrust.shape[0]
    ax, ay, az = Axis("gx"), Axis("gy"), Axis("gz")
    peers = ax.count * ay.count
    capacity = 2 * row_total // peers
    nx, ny, nz = len(ax.perms), len(ay.perms), len(az.perms)
    ext_a = cells_x + 2 * HA
    ext_b = cells_x + (HB if ax.count == 2 else 2 * HB)
    pack_a = -(-4 * ext_a * HA // width)
    pack_b = -(-2 * ext_b * HB // width)
    tall = cells_z + 2 * ZP
    vm = lambda *shape: pltpu.VMEM(shape, F32)
    info = jnp.stack(
        [
            lax.axis_index("gx"),
            lax.axis_index("gy"),
            lax.axis_index("gz"),
            row_counts.reshape(()),
        ]
    ).astype(jnp.int32)
    inx = inflow_x[:, None]
    iny = inflow_y[:, None]
    push = thrust[:, None]
    block = capacity + 8
    (packed,) = call(
        functools.partial(pack_kernel, peers, capacity),
        [(peers * block, width)],
        [info, kernel, owners, lines[None, :], point_turbine[None, :]],
        name="pack_rows",
    )
    rows = lax.all_to_all(
        packed.reshape(peers, block, width), ("gx", "gy"), split_axis=0, concat_axis=0, tiled=True
    ).reshape(peers * block, width)
    xsize = (4 * HA * cells_z + turbines, width)
    vel, press = velocity, pressure
    parts, *xsend = call(
        functools.partial(begin_kernel, nx),
        [(turbines, width)] + [xsize] * nx,
        [info, vel, press, inx, iny],
        name="begin",
    )
    for repeat in range(STEPS):
        last = repeat == STEPS - 1
        if not ax.fold:
            parts = lax.psum(parts, "gx")
        xr = ax.swap(xsend)
        parts, *ysend = call(
            functools.partial(halo_y_kernel, ax, ay),
            [(turbines, width)] + [(pack_a * cells_z + turbines, width)] * ny,
            [info, vel, press, parts, *xr],
            name="halo_y",
        )
        yr = ay.swap(ysend)
        cross = [lax.ppermute(parts, "gy", ay.cross)] if ay.cross else []
        if not ay.fold:
            parts = lax.psum(parts, "gy")
        zrows = 4 * ext_a * HA + ny * pack_a * HA
        zrows = -(-zrows // 8) * 8 + turbines
        parts, *zsend = call(
            functools.partial(halo_z_kernel, ax, ay, az, pack_a),
            [(turbines, width)] + [(zrows, width)] * nz,
            [info, vel, press, parts, *xr, *yr, *cross],
            name="halo_z",
        )
        zr = az.swap(zsend)
        cross = [lax.ppermute(parts, "gz", az.cross)] if az.cross else []
        if not az.fold:
            parts = lax.psum(parts, "gz")
        star, p1, s6, edge, *xsend = call(
            functools.partial(star_kernel, ax, ay, az, pack_a, peers, capacity),
            [
                (3, cells_x, cells_z, width),
                (cells_x, cells_z, width),
                (cells_x, cells_z, width),
                (2, cells_z, width),
            ]
            + [(2 * HB + 1, cells_z, width)] * nx,
            [info, vel, press, parts, rows, push, *xr, *yr, *zr, *cross],
            scratch=[
                vm(4, ext_a, tall, 2 * width),
                vm(cells_x + 2, cells_z, width),
                vm(cells_x * cells_z, width),
                vm(pack_a, tall, width),
                vm(pack_a, tall, width),
            ],
            name="star",
        )
        xr = ax.swap(xsend)
        px, sx, *ysend = call(
            functools.partial(deep_y_kernel, ax, ay),
            [(ext_b, cells_z, width)] * 2 + [(pack_b * cells_z, width)] * ny,
            [info, p1, s6, edge, *xr],
            name="deep_y",
        )
        yr = ay.swap(ysend)
        zsend = call(
            functools.partial(deep_z_kernel, ay, az, pack_b),
            [(2 * ext_b + ny * pack_b, HB, width)] * nz,
            [info, px, sx, *yr],
            name="deep_z",
        )
        zr = az.swap(zsend)
        outs = [(3, cells_x, cells_z, width), (cells_x, cells_z, width)]
        if not last:
            outs = outs + [(turbines, width)] + [xsize] * nx
        results = call(
            functools.partial(sweep_kernel, ax, ay, az, pack_b, last),
            outs,
            [info, px, sx, star, inx, iny, *yr, *zr],
            scratch=[
                vm(ext_b + 2, tall, 2 * width),
                vm(ext_b, tall, 2 * width),
                vm(pack_b, tall, width),
                vm(pack_b, tall, width),
                vm(tall, 2 * width),
            ],
            name="sweeps",
        )
        vel, press = results[:2]
        if not last:
            parts, *xsend = results[2:]
    return (vel, press)


def solution(mesh):
    placed = (
        P(None, "gx", "gz", "gy"),
        P("gx", "gz", "gy"),
        P(("gx", "gy", "gz"), None),
        P(("gx", "gy", "gz"), None),
        P(("gx", "gy", "gz")),
        P(("gx", "gy", "gz")),
        P("gx", "gy", "gz"),
        P(),
        P(),
        P(),
    )
    return jax.shard_map(
        body,
        mesh=mesh,
        in_specs=placed,
        out_specs=(P(None, "gx", "gz", "gy"), P("gx", "gz", "gy")),
        check_vma=False,
    )
```

time: 823 us -> 154 us (0.19); the launches traced: 810 us -> 152 us
  starting transfers between devices: 272 us -> 33.1 us
  waiting for transfers between devices: 233 us -> 46.3 us
  local copies, waits for them, and re-layouts: 137 us -> 4 us
  other arithmetic: 82.1 us -> 0.08 us
  blocking collectives: 79.4 us -> 0 us
  Pallas kernels: 0 us -> 67.2 us
    ppermute x96 -> x24, starting transfers between devices: 259 us -> 28.7 us  [the longest x20 21.8 us: swap(): return [lax.ppermute(s, self.name, p) for s, p in zip(sends, self.perms)]]
    ppermute x96 -> x24, waiting for transfers between devices: 233 us -> 46.3 us  [the longest x20 33.7 us: swap(): return [lax.ppermute(s, self.name, p) for s, p in zip(sends, self.perms)]]
    scatter x3 -> x0, local copies, waits for them, and re-layouts: 94.7 us -> none  [the longest x2 56 us: body(): jnp.zeros((peers, capacity, cells_y), jnp.float32).at[target, slot_index]]
    psum x2 -> x0, blocking collectives: 79.4 us -> none  [body(): total = lax.psum(partial_sum, ('gx', 'gy', 'gz'))]
    pallas_call x0 -> x14, Pallas kernels: none -> 67.2 us  [call(): pl.pallas_call(kernel, out_shape=[jax.ShapeDtypeStruct(o, F32) for o in o...]
    mul x13 -> x0, other arithmetic: 34.8 us -> none  [the longest x8 34.5 us: body(): middle = (neighbours(deeper) - source_wide) / 6.0 * inside]
    slice x44 -> x0, local copies, waits for them, and re-layouts: 24.2 us -> none  [the longest x32 13.3 us: extended(): lax.slice_in_dim(cells, cells.shape[dim] - width, cells.shape[dim], axis=...]
    add x7 -> x0, other arithmetic: 10.9 us -> none  [the longest x2 9.63 us: body(): star = field + time_step * (viscosity * laplace - forcing)]
  transfers between devices with their start and end apart: 99 -> 25, of which waited for: 50 -> 19; matrix products, arithmetic and copies ran while one was open for 19% -> 0% of each run, Pallas kernels for 0% -> 3%
where the time goes in v1:
time: 154 us; the launch traced here: 152 us
  Pallas kernels  67.2 us (44%)
  waiting for transfers between devices  46.3 us (30%)
  starting transfers between devices  33.1 us (21%)
  local copies, waits for them, and re-layouts  4 us (3%)
    pallas_call x14, Pallas kernels, call(): pl.pallas_call(kernel, out_shape=[jax.ShapeDtypeStruct(o, F32) for o in o...  67.2 us
    ppermute x20, waiting for transfers between devices, swap(): return [lax.ppermute(s, self.name, p) for s, p in zip(sends, self.perms)]  33.7 us
    ppermute x20, starting transfers between devices, swap(): return [lax.ppermute(s, self.name, p) for s, p in zip(sends, self.perms)]  21.8 us
    ppermute x2, waiting for transfers between devices, body(): cross = [lax.ppermute(parts, 'gz', az.cross)] if az.cross else []  7.2 us
    ppermute x2, waiting for transfers between devices, body(): cross = [lax.ppermute(parts, 'gy', ay.cross)] if ay.cross else []  5.38 us
    all_to_all x1, starting transfers between devices, body(): lax.all_to_all(packed.reshape(peers, block, width), ('gx', 'gy'), split_a...  4.32 us
    ppermute x2, starting transfers between devices, body(): cross = [lax.ppermute(parts, 'gz', az.cross)] if az.cross else []  3.59 us
    ppermute x2, starting transfers between devices, body(): cross = [lax.ppermute(parts, 'gy', ay.cross)] if ay.cross else []  3.32 us
  transfers between devices with their start and end apart: 25, of which 19 were waited for; matrix products, arithmetic and copies ran while one was open for 0% of the time, Pallas kernels for 3%

profile of v1, /device:TPU:12, one launch (start us, length us, event | category | flops | bytes accessed | tf_op | source)
XLA Modules:
  0.0 152.2 jit_solution(7534064418693537952)
XLA Ops:
  6.2 2.2 %pack_rows.1 = f32[576,128]{1,0:T(8,128)} custom-call(s32[4]{0:T(128)S(1)} %pad_add_fusion.info, f32[256,128]{1,0:T(8,128)S(1)} %copy-done.4, s32[256,1]{1,0:T(8,128)S(1)} %copy.14.owners, s32[1,256]{1,0:T(1,128)S(1)} %bitcast.14, s32[1,256]{1,0:T(1,128)S(1)} %bitcast.15), custom_call_target="tpu_custom_call" | custom-call | flops 429072 | bytes 429072 | tf_op jit(solution)/shard_map/pack_rows/pallas_call | solution.py:28
  8.3 4.3 %all-to-all-start = ((f32[8,72,128]{2,1,0:T(8,128)}), f32[8,72,128]{2,1,0:T(8,128)S(1)}, u32[]{:S(2)}, u32[]{:S(2)}) async-start(f32[8,72,128]{2,1,0:T(8,128)} %bitcast.8), calls=%async_computation | async-start | bytes 589824 | tf_op jit(solution)/shard_map/all_to_all | solution.py:601
  12.7 1.6 %halo_y.2 = (f32[48,128]{1,0:T(8,128)S(1)}, f32[144,128]{1,0:T(8,128)S(1)}, f32[144,128]{1,0:T(8,128)S(1)}) custom-call(s32[4]{0:T(128)S(1)} %pad_add_fusion.info, f32[3,16,48,128]{3,2,1,0:T(8,128)S(1)} %copy-done.1, f32[16,48,128]{2,1,0:T(8,128)S(1)} %copy-done.3, f32[48,128]{1,0:T(8,128)S(1)} %get-tuple-element.42.parts, ...), custom_call_target="tpu_custom_call" | custom-call | flops 1990672 | bytes 1990672 | tf_op jit(solution)/shard_map/halo_y/pallas_call | solution.py:28
  14.3 1.5 %collective-permute-start.1 = (f32[144,128]{1,0:T(8,128)S(1)}, f32[144,128]{1,0:T(8,128)S(1)}, u32[]{:S(2)}, u32[]{:S(2)}) collective-permute-start(f32[144,128]{1,0:T(8,128)S(1)} %get-tuple-element.45), channel_id=1, source_target_pairs={{0,4},{4,0},{8,12},{12,8},{1,5},{5,1},{9,13},{13,9},{2,6},{6,2},{1... | collective-permute-start | bytes 221192 | tf_op jit(solution)/shard_map/ppermute | solution.py:76
  15.9 1.9 %collective-permute-start.3 = (f32[48,128]{1,0:T(8,128)S(1)}, f32[48,128]{1,0:T(8,128)S(1)}, u32[]{:S(2)}, u32[]{:S(2)}) collective-permute-start(f32[48,128]{1,0:T(8,128)S(1)} %get-tuple-element.44.parts), channel_id=1, source_target_pairs={{0,8},{4,12},{8,0},{12,4},{1,9},{5,13},{9,1},{13,5},{2,10},{6,14},... | collective-permute-start | bytes 73736 | tf_op jit(solution)/shard_map/ppermute | solution.py:624
  17.9 2.1 %collective-permute-done.3.refs_3_ = f32[48,128]{1,0:T(8,128)S(1)} collective-permute-done((f32[48,128]{1,0:T(8,128)S(1)}, f32[48,128]{1,0:T(8,128)S(1)}, u32[]{:S(2)}, u32[]{:S(2)}) %collective-permute-start.3) | collective-permute-done | bytes 24608 | tf_op jit(solution)/shard_map/ppermute | solution.py:624
  22.8 2.7 %collective-permute-start.5 = (f32[216,128]{1,0:T(8,128)S(1)}, f32[216,128]{1,0:T(8,128)S(1)}, u32[]{:S(2)}, u32[]{:S(2)}) collective-permute-start(f32[216,128]{1,0:T(8,128)S(1)} %get-tuple-element.49), channel_id=1, source_target_pairs={{1,2},{3,0},{2,1},{0,3},{5,6},{7,4},{6,5},{4,7},{9,10},{11,8},{10,... | collective-permute-start | bytes 331784 | tf_op jit(solution)/shard_map/ppermute | solution.py:76
  26.8 3.9 %collective-permute-done.6.refs_5_ = f32[48,128]{1,0:T(8,128)S(1)} collective-permute-done((f32[48,128]{1,0:T(8,128)S(1)}, f32[48,128]{1,0:T(8,128)S(1)}, u32[]{:S(2)}, u32[]{:S(2)}) %collective-permute-start.6) | collective-permute-done | bytes 24608 | tf_op jit(solution)/shard_map/ppermute | solution.py:636
  31.1 8.7 %star.2 = (f32[3,16,48,128]{3,2,1,0:T(8,128)S(1)}, f32[16,48,128]{2,1,0:T(8,128)S(1)}, f32[16,48,128]{2,1,0:T(8,128)S(1)}, f32[2,48,128]{2,1,0:T(8,128)S(1)}, f32[17,48,128]{2,1,0:T(8,128)S(1)}) custom-call(s32[4]{0:T(128)S(1)} %pad_add_fusion.info, f32[3,16,48,128]{3,2,1,0:T(8,128)S(1)} %copy-done.1, f32[16,48,128]{2,1,0:T(8,128)S(1)} %copy-done.3, ...), custom_call_target="tpu_custom_call" | custom-call | flops 4939984 | bytes 4939984 | tf_op jit(solution)/shard_map/star/pallas_call | solution.py:28
  39.9 1.7 %collective-permute-done.7.refs_0_ = f32[17,48,128]{2,1,0:T(8,128)S(1)} collective-permute-done((f32[17,48,128]{2,1,0:T(8,128)S(1)}, f32[17,48,128]{2,1,0:T(8,128)S(1)}, u32[]{:S(2)}, u32[]{:S(2)}) %collective-permute-start.7) | collective-permute-done | bytes 417824 | tf_op jit(solution)/shard_map/ppermute | solution.py:76
  43.4 2.5 %collective-permute-start.9 = (f32[144,128]{1,0:T(8,128)S(1)}, f32[144,128]{1,0:T(8,128)S(1)}, u32[]{:S(2)}, u32[]{:S(2)}) collective-permute-start(f32[144,128]{1,0:T(8,128)S(1)} %get-tuple-element.58), channel_id=1, source_target_pairs={{4,8},{12,0},{8,4},{0,12},{5,9},{13,1},{9,5},{1,13},{6,10},{14,2},... | collective-permute-start | bytes 221192 | tf_op jit(solution)/shard_map/ppermute | solution.py:76
  45.9 1.7 %collective-permute-done.8.refs_0_ = f32[144,128]{1,0:T(8,128)S(1)} collective-permute-done((f32[144,128]{1,0:T(8,128)S(1)}, f32[144,128]{1,0:T(8,128)S(1)}, u32[]{:S(2)}, u32[]{:S(2)}) %collective-permute-start.8) | collective-permute-done | bytes 73760 | tf_op jit(solution)/shard_map/ppermute | solution.py:76
  47.7 2.1 %collective-permute-done.9.refs_1_ = f32[144,128]{1,0:T(8,128)S(1)} collective-permute-done((f32[144,128]{1,0:T(8,128)S(1)}, f32[144,128]{1,0:T(8,128)S(1)}, u32[]{:S(2)}, u32[]{:S(2)}) %collective-permute-start.9) | collective-permute-done | bytes 73760 | tf_op jit(solution)/shard_map/ppermute | solution.py:76
  50.4 1.8 %collective-permute-start.10 = (f32[54,8,128]{2,1,0:T(8,128)S(1)}, f32[54,8,128]{2,1,0:T(8,128)S(1)}, u32[]{:S(2)}, u32[]{:S(2)}) collective-permute-start(f32[54,8,128]{2,1,0:T(8,128)S(1)} %get-tuple-element.59), channel_id=1, source_target_pairs={{0,1},{1,0},{2,3},{3,2},{4,5},{5,4},{6,7},{7,6},{8,9},{9,8},{10,11... | collective-permute-start | bytes 663560 | tf_op jit(solution)/shard_map/ppermute | solution.py:76
  52.2 1.7 %collective-permute-start.11 = (f32[54,8,128]{2,1,0:T(8,128)S(1)}, f32[54,8,128]{2,1,0:T(8,128)S(1)}, u32[]{:S(2)}, u32[]{:S(2)}) collective-permute-start(f32[54,8,128]{2,1,0:T(8,128)S(1)} %get-tuple-element.60), channel_id=1, source_target_pairs={{1,2},{3,0},{2,1},{0,3},{5,6},{7,4},{6,5},{4,7},{9,10},{11,8},{10,... | collective-permute-start | bytes 663560 | tf_op jit(solution)/shard_map/ppermute | solution.py:76
  53.9 4.8 %collective-permute-done.10.refs_2_ = f32[54,8,128]{2,1,0:T(8,128)S(1)} collective-permute-done((f32[54,8,128]{2,1,0:T(8,128)S(1)}, f32[54,8,128]{2,1,0:T(8,128)S(1)}, u32[]{:S(2)}, u32[]{:S(2)}) %collective-permute-start.10) | collective-permute-done | bytes 221216 | tf_op jit(solution)/shard_map/ppermute | solution.py:76
  58.8 4.2 %collective-permute-done.11.refs_3_ = f32[54,8,128]{2,1,0:T(8,128)S(1)} collective-permute-done((f32[54,8,128]{2,1,0:T(8,128)S(1)}, f32[54,8,128]{2,1,0:T(8,128)S(1)}, u32[]{:S(2)}, u32[]{:S(2)}) %collective-permute-start.11) | collective-permute-done | bytes 221216 | tf_op jit(solution)/shard_map/ppermute | solution.py:76
  63.0 18.8 %sweeps.2 = (f32[3,16,48,128]{3,2,1,0:T(8,128)S(1)}, f32[16,48,128]{2,1,0:T(8,128)S(1)}, f32[48,128]{1,0:T(8,128)S(1)}, f32[432,128]{1,0:T(8,128)S(1)}) custom-call(s32[4]{0:T(128)S(1)} %pad_add_fusion.info, f32[24,48,128]{2,1,0:T(8,128)S(1)} %get-tuple-element.54.px, f32[24,48,128]{2,1,0:T(8,128)S(1)} %get-tuple-element.55.sx, ...), custom_call_target="tpu_custom_call" | custom-call | flops 4768144 | bytes 4768144 | tf_op jit(solution)/shard_map/sweeps/pallas_call | solution.py:28
  81.9 1.5 collective-permute-done.12.refs_0_
  83.4 1.6 %halo_y.3 = (f32[48,128]{1,0:T(8,128)S(1)}, f32[144,128]{1,0:T(8,128)S(1)}, f32[144,128]{1,0:T(8,128)S(1)}) custom-call(s32[4]{0:T(128)S(1)} %pad_add_fusion.info, f32[3,16,48,128]{3,2,1,0:T(8,128)S(1)} %get-tuple-element.61.vel, f32[16,48,128]{2,1,0:T(8,128)S(1)} %get-tuple-element.62.press, f32[48,128]{1,0:T(8,128)S(1)} %get-tuple-element.63.parts, ...), custom_call_target="tpu_custom_call" | custom-call | flops 1990672 | bytes 1990672 | tf_op jit(solution)/shard_map/halo_y/pallas_call | solution.py:28
  88.6 3.2 %collective-permute-done.15.refs_3_ = f32[48,128]{1,0:T(8,128)S(1)} collective-permute-done((f32[48,128]{1,0:T(8,128)S(1)}, f32[48,128]{1,0:T(8,128)S(1)}, u32[]{:S(2)}, u32[]{:S(2)}) %collective-permute-start.15) | collective-permute-done | bytes 24608 | tf_op jit(solution)/shard_map/ppermute | solution.py:624
  94.6 2.4 %collective-permute-start.18 = (f32[48,128]{1,0:T(8,128)S(1)}, f32[48,128]{1,0:T(8,128)S(1)}, u32[]{:S(2)}, u32[]{:S(2)}) collective-permute-start(f32[48,128]{1,0:T(8,128)S(1)} %get-tuple-element.68.parts), channel_id=1, source_target_pairs={{0,2},{1,3},{2,0},{3,1},{4,6},{5,7},{6,4},{7,5},{8,10},{9,11},{10,... | collective-permute-start | bytes 73736 | tf_op jit(solution)/shard_map/ppermute | solution.py:636
  96.9 3.3 %collective-permute-done.18.refs_5_ = f32[48,128]{1,0:T(8,128)S(1)} collective-permute-done((f32[48,128]{1,0:T(8,128)S(1)}, f32[48,128]{1,0:T(8,128)S(1)}, u32[]{:S(2)}, u32[]{:S(2)}) %collective-permute-start.18) | collective-permute-done | bytes 24608 | tf_op jit(solution)/shard_map/ppermute | solution.py:636
  100.4 8.7 %star.3 = (f32[3,16,48,128]{3,2,1,0:T(8,128)S(1)}, f32[16,48,128]{2,1,0:T(8,128)S(1)}, f32[16,48,128]{2,1,0:T(8,128)S(1)}, f32[2,48,128]{2,1,0:T(8,128)S(1)}, f32[17,48,128]{2,1,0:T(8,128)S(1)}) custom-call(s32[4]{0:T(128)S(1)} %pad_add_fusion.info, f32[3,16,48,128]{3,2,1,0:T(8,128)S(1)} %get-tuple-element.61.vel, ...), custom_call_target="tpu_custom_call" | custom-call | flops 4939984 | bytes 4939984 | tf_op jit(solution)/shard_map/star/pallas_call | solution.py:28
  109.2 1.7 %collective-permute-done.19.refs_0_ = f32[17,48,128]{2,1,0:T(8,128)S(1)} collective-permute-done((f32[17,48,128]{2,1,0:T(8,128)S(1)}, f32[17,48,128]{2,1,0:T(8,128)S(1)}, u32[]{:S(2)}, u32[]{:S(2)}) %collective-permute-start.19) | collective-permute-done | bytes 417824 | tf_op jit(solution)/shard_map/ppermute | solution.py:76
  114.9 1.8 %collective-permute-done.20.refs_0_ = f32[144,128]{1,0:T(8,128)S(1)} collective-permute-done((f32[144,128]{1,0:T(8,128)S(1)}, f32[144,128]{1,0:T(8,128)S(1)}, u32[]{:S(2)}, u32[]{:S(2)}) %collective-permute-start.20) | collective-permute-done | bytes 73760 | tf_op jit(solution)/shard_map/ppermute | solution.py:76
  116.8 2.1 %collective-permute-done.21.refs_1_ = f32[144,128]{1,0:T(8,128)S(1)} collective-permute-done((f32[144,128]{1,0:T(8,128)S(1)}, f32[144,128]{1,0:T(8,128)S(1)}, u32[]{:S(2)}, u32[]{:S(2)}) %collective-permute-start.21) | collective-permute-done | bytes 73760 | tf_op jit(solution)/shard_map/ppermute | solution.py:76
  119.4 1.8 %collective-permute-start.22 = (f32[54,8,128]{2,1,0:T(8,128)S(1)}, f32[54,8,128]{2,1,0:T(8,128)S(1)}, u32[]{:S(2)}, u32[]{:S(2)}) collective-permute-start(f32[54,8,128]{2,1,0:T(8,128)S(1)} %get-tuple-element.80), channel_id=1, source_target_pairs={{0,1},{1,0},{2,3},{3,2},{4,5},{5,4},{6,7},{7,6},{8,9},{9,8},{10,11... | collective-permute-start | bytes 663560 | tf_op jit(solution)/shard_map/ppermute | solution.py:76
  121.2 1.4 collective-permute-start.23
  122.7 5.2 %collective-permute-done.22.refs_2_ = f32[54,8,128]{2,1,0:T(8,128)S(1)} collective-permute-done((f32[54,8,128]{2,1,0:T(8,128)S(1)}, f32[54,8,128]{2,1,0:T(8,128)S(1)}, u32[]{:S(2)}, u32[]{:S(2)}) %collective-permute-start.22) | collective-permute-done | bytes 221216 | tf_op jit(solution)/shard_map/ppermute | solution.py:76
  127.8 4.6 %collective-permute-done.23.refs_3_ = f32[54,8,128]{2,1,0:T(8,128)S(1)} collective-permute-done((f32[54,8,128]{2,1,0:T(8,128)S(1)}, f32[54,8,128]{2,1,0:T(8,128)S(1)}, u32[]{:S(2)}, u32[]{:S(2)}) %collective-permute-start.23) | collective-permute-done | bytes 221216 | tf_op jit(solution)/shard_map/ppermute | solution.py:76
  132.4 19.7 %sweeps.3 = (f32[3,16,48,128]{3,2,1,0:T(8,128)}, f32[16,48,128]{2,1,0:T(8,128)}) custom-call(s32[4]{0:T(128)S(1)} %pad_add_fusion.info, f32[24,48,128]{2,1,0:T(8,128)S(1)} %get-tuple-element.75.px, f32[24,48,128]{2,1,0:T(8,128)S(1)} %get-tuple-element.76.sx, f32[3,16,48,128]{3,2,1,0:T(8,128)S(1)} %get-tuple-element.77.star, s32[48,1]{1,0:T(8,128)S(1)} %copy.12.inx, ...), custom_call_target="tpu_custom_call" | custom-call | flops 4522384 | bytes 4522384 | tf_op jit(solution)/shard_map/sweeps/pallas_call | solution.py:28
  (55 shorter events, 23.0 us)
Async XLA Ops:
  0.6 5.3 %copy-start.7 = (s32[256,1]{0,1:T(1,128)S(1)}, s32[256,1]{0,1:T(1,128)}, u32[]{:S(2)}) copy-start(s32[256,1]{0,1:T(1,128)} %param.13) | copy-start | bytes 3076
  0.6 5.5 %copy-start.6 = (s32[256]{0:T(256)S(1)}, s32[256]{0:T(256)}, u32[]{:S(2)}) copy-start(s32[256]{0:T(256)} %param.15) | copy-start | bytes 3076
  0.7 5.5 %copy-start.5 = (s32[256]{0:T(256)S(1)}, s32[256]{0:T(256)}, u32[]{:S(2)}) copy-start(s32[256]{0:T(256)} %param.14) | copy-start | bytes 3076
  2.9 1.3 copy-start
  5.2 7.5 %copy-start.1 = (f32[3,16,48,128]{3,2,1,0:T(8,128)S(1)}, f32[3,16,48,128]{3,2,1,0:T(8,128)}, u32[]{:S(2)}) copy-start(f32[3,16,48,128]{3,2,1,0:T(8,128)} %vel.7) | copy-start | bytes 3538948
  5.2 7.5 %copy-start.3 = (f32[16,48,128]{2,1,0:T(8,128)S(1)}, f32[16,48,128]{2,1,0:T(8,128)}, u32[]{:S(2)}) copy-start(f32[16,48,128]{2,1,0:T(8,128)} %press.7) | copy-start | bytes 1179652
  5.9 6.7 %collective-permute-start = (f32[432,128]{1,0:T(8,128)S(1)}, f32[432,128]{1,0:T(8,128)S(1)}, u32[]{:S(2)}, u32[]{:S(2)}) collective-permute-start(f32[432,128]{1,0:T(8,128)S(1)} %get-tuple-element.43), channel_id=1, source_target_pairs={{0,16},{16,0},{1,17},{17,1},{2,18},{18,2},{3,19},{19,3},{4,20},{20... | collective-permute-start | bytes 663560 | tf_op jit(solution)/shard_map/ppermute | solution.py:76
  8.3 18.5 %all-to-all-start = ((f32[8,72,128]{2,1,0:T(8,128)}), f32[8,72,128]{2,1,0:T(8,128)S(1)}, u32[]{:S(2)}, u32[]{:S(2)}) async-start(f32[8,72,128]{2,1,0:T(8,128)} %bitcast.8), calls=%async_computation | async-start | bytes 589824 | tf_op jit(solution)/shard_map/all_to_all | solution.py:601
  14.3 12.4 %copy-start.8 = (f32[48]{0:T(128)S(1)}, f32[48]{0:T(128)}, u32[]{:S(2)}) copy-start(f32[48]{0:T(128)} %param.17) | copy-start | bytes 580
  14.3 6.3 %collective-permute-start.1 = (f32[144,128]{1,0:T(8,128)S(1)}, f32[144,128]{1,0:T(8,128)S(1)}, u32[]{:S(2)}, u32[]{:S(2)}) collective-permute-start(f32[144,128]{1,0:T(8,128)S(1)} %get-tuple-element.45), channel_id=1, source_target_pairs={{0,4},{4,0},{8,12},{12,8},{1,5},{5,1},{9,13},{13,9},{2,6},{6,2},{1... | collective-permute-start | bytes 221192 | tf_op jit(solution)/shard_map/ppermute | solution.py:76
  15.8 5.8 %collective-permute-start.2 = (f32[144,128]{1,0:T(8,128)S(1)}, f32[144,128]{1,0:T(8,128)S(1)}, u32[]{:S(2)}, u32[]{:S(2)}) collective-permute-start(f32[144,128]{1,0:T(8,128)S(1)} %get-tuple-element.46), channel_id=1, source_target_pairs={{4,8},{12,0},{8,4},{0,12},{5,9},{13,1},{9,5},{1,13},{6,10},{14,2},... | collective-permute-start | bytes 221192 | tf_op jit(solution)/shard_map/ppermute | solution.py:76
  15.9 4.1 %collective-permute-start.3 = (f32[48,128]{1,0:T(8,128)S(1)}, f32[48,128]{1,0:T(8,128)S(1)}, u32[]{:S(2)}, u32[]{:S(2)}) collective-permute-start(f32[48,128]{1,0:T(8,128)S(1)} %get-tuple-element.44.parts), channel_id=1, source_target_pairs={{0,8},{4,12},{8,0},{12,4},{1,9},{5,13},{9,1},{13,5},{2,10},{6,14},... | collective-permute-start | bytes 73736 | tf_op jit(solution)/shard_map/ppermute | solution.py:624
  22.2 8.5 %collective-permute-start.4 = (f32[216,128]{1,0:T(8,128)S(1)}, f32[216,128]{1,0:T(8,128)S(1)}, u32[]{:S(2)}, u32[]{:S(2)}) collective-permute-start(f32[216,128]{1,0:T(8,128)S(1)} %get-tuple-element.48), channel_id=1, source_target_pairs={{0,1},{1,0},{2,3},{3,2},{4,5},{5,4},{6,7},{7,6},{8,9},{9,8},{10,11... | collective-permute-start | bytes 331784 | tf_op jit(solution)/shard_map/ppermute | solution.py:76
  22.8 8.3 %collective-permute-start.5 = (f32[216,128]{1,0:T(8,128)S(1)}, f32[216,128]{1,0:T(8,128)S(1)}, u32[]{:S(2)}, u32[]{:S(2)}) collective-permute-start(f32[216,128]{1,0:T(8,128)S(1)} %get-tuple-element.49), channel_id=1, source_target_pairs={{1,2},{3,0},{2,1},{0,3},{5,6},{7,4},{6,5},{4,7},{9,10},{11,8},{10,... | collective-permute-start | bytes 331784 | tf_op jit(solution)/shard_map/ppermute | solution.py:76
  25.5 5.3 %collective-permute-start.6 = (f32[48,128]{1,0:T(8,128)S(1)}, f32[48,128]{1,0:T(8,128)S(1)}, u32[]{:S(2)}, u32[]{:S(2)}) collective-permute-start(f32[48,128]{1,0:T(8,128)S(1)} %get-tuple-element.47.parts), channel_id=1, source_target_pairs={{0,2},{1,3},{2,0},{3,1},{4,6},{5,7},{6,4},{7,5},{8,10},{9,11},{10,... | collective-permute-start | bytes 73736 | tf_op jit(solution)/shard_map/ppermute | solution.py:636
  39.8 1.8 %collective-permute-start.7 = (f32[17,48,128]{2,1,0:T(8,128)S(1)}, f32[17,48,128]{2,1,0:T(8,128)S(1)}, u32[]{:S(2)}, u32[]{:S(2)}) collective-permute-start(f32[17,48,128]{2,1,0:T(8,128)S(1)} %get-tuple-element.53), channel_id=1, source_target_pairs={{0,16},{16,0},{1,17},{17,1},{2,18},{18,2},{3,19},{19,3},{4,20},{20... | collective-permute-start | bytes 1253384 | tf_op jit(solution)/shard_map/ppermute | solution.py:76
  42.9 4.7 %collective-permute-start.8 = (f32[144,128]{1,0:T(8,128)S(1)}, f32[144,128]{1,0:T(8,128)S(1)}, u32[]{:S(2)}, u32[]{:S(2)}) collective-permute-start(f32[144,128]{1,0:T(8,128)S(1)} %get-tuple-element.57), channel_id=1, source_target_pairs={{0,4},{4,0},{8,12},{12,8},{1,5},{5,1},{9,13},{13,9},{2,6},{6,2},{1... | collective-permute-start | bytes 221192 | tf_op jit(solution)/shard_map/ppermute | solution.py:76
  43.4 6.4 %collective-permute-start.9 = (f32[144,128]{1,0:T(8,128)S(1)}, f32[144,128]{1,0:T(8,128)S(1)}, u32[]{:S(2)}, u32[]{:S(2)}) collective-permute-start(f32[144,128]{1,0:T(8,128)S(1)} %get-tuple-element.58), channel_id=1, source_target_pairs={{4,8},{12,0},{8,4},{0,12},{5,9},{13,1},{9,5},{1,13},{6,10},{14,2},... | collective-permute-start | bytes 221192 | tf_op jit(solution)/shard_map/ppermute | solution.py:76
  50.4 8.4 %collective-permute-start.10 = (f32[54,8,128]{2,1,0:T(8,128)S(1)}, f32[54,8,128]{2,1,0:T(8,128)S(1)}, u32[]{:S(2)}, u32[]{:S(2)}) collective-permute-start(f32[54,8,128]{2,1,0:T(8,128)S(1)} %get-tuple-element.59), channel_id=1, source_target_pairs={{0,1},{1,0},{2,3},{3,2},{4,5},{5,4},{6,7},{7,6},{8,9},{9,8},{10,11... | collective-permute-start | bytes 663560 | tf_op jit(solution)/shard_map/ppermute | solution.py:76
  52.2 10.8 %collective-permute-start.11 = (f32[54,8,128]{2,1,0:T(8,128)S(1)}, f32[54,8,128]{2,1,0:T(8,128)S(1)}, u32[]{:S(2)}, u32[]{:S(2)}) collective-permute-start(f32[54,8,128]{2,1,0:T(8,128)S(1)} %get-tuple-element.60), channel_id=1, source_target_pairs={{1,2},{3,0},{2,1},{0,3},{5,6},{7,4},{6,5},{4,7},{9,10},{11,8},{10,... | collective-permute-start | bytes 663560 | tf_op jit(solution)/shard_map/ppermute | solution.py:76
  81.8 1.5 %collective-permute-start.12 = (f32[432,128]{1,0:T(8,128)S(1)}, f32[432,128]{1,0:T(8,128)S(1)}, u32[]{:S(2)}, u32[]{:S(2)}) collective-permute-start(f32[432,128]{1,0:T(8,128)S(1)} %get-tuple-element.64), channel_id=1, source_target_pairs={{0,16},{16,0},{1,17},{17,1},{2,18},{18,2},{3,19},{19,3},{4,20},{20... | collective-permute-start | bytes 663560 | tf_op jit(solution)/shard_map/ppermute | solution.py:76
  85.0 6.8 %collective-permute-start.13 = (f32[144,128]{1,0:T(8,128)S(1)}, f32[144,128]{1,0:T(8,128)S(1)}, u32[]{:S(2)}, u32[]{:S(2)}) collective-permute-start(f32[144,128]{1,0:T(8,128)S(1)} %get-tuple-element.66), channel_id=1, source_target_pairs={{0,4},{4,0},{8,12},{12,8},{1,5},{5,1},{9,13},{13,9},{2,6},{6,2},{1... | collective-permute-start | bytes 221192 | tf_op jit(solution)/shard_map/ppermute | solution.py:76
  86.4 5.4 %collective-permute-start.14 = (f32[144,128]{1,0:T(8,128)S(1)}, f32[144,128]{1,0:T(8,128)S(1)}, u32[]{:S(2)}, u32[]{:S(2)}) collective-permute-start(f32[144,128]{1,0:T(8,128)S(1)} %get-tuple-element.67), channel_id=1, source_target_pairs={{4,8},{12,0},{8,4},{0,12},{5,9},{13,1},{9,5},{1,13},{6,10},{14,2},... | collective-permute-start | bytes 221192 | tf_op jit(solution)/shard_map/ppermute | solution.py:76
  87.2 4.6 %collective-permute-start.15 = (f32[48,128]{1,0:T(8,128)S(1)}, f32[48,128]{1,0:T(8,128)S(1)}, u32[]{:S(2)}, u32[]{:S(2)}) collective-permute-start(f32[48,128]{1,0:T(8,128)S(1)} %get-tuple-element.65.parts), channel_id=1, source_target_pairs={{0,8},{4,12},{8,0},{12,4},{1,9},{5,13},{9,1},{13,5},{2,10},{6,14},... | collective-permute-start | bytes 73736 | tf_op jit(solution)/shard_map/ppermute | solution.py:624
  92.5 7.7 %collective-permute-start.16 = (f32[216,128]{1,0:T(8,128)S(1)}, f32[216,128]{1,0:T(8,128)S(1)}, u32[]{:S(2)}, u32[]{:S(2)}) collective-permute-start(f32[216,128]{1,0:T(8,128)S(1)} %get-tuple-element.69), channel_id=1, source_target_pairs={{0,1},{1,0},{2,3},{3,2},{4,5},{5,4},{6,7},{7,6},{8,9},{9,8},{10,11... | collective-permute-start | bytes 331784 | tf_op jit(solution)/shard_map/ppermute | solution.py:76
  93.8 6.6 %collective-permute-start.17 = (f32[216,128]{1,0:T(8,128)S(1)}, f32[216,128]{1,0:T(8,128)S(1)}, u32[]{:S(2)}, u32[]{:S(2)}) collective-permute-start(f32[216,128]{1,0:T(8,128)S(1)} %get-tuple-element.70), channel_id=1, source_target_pairs={{1,2},{3,0},{2,1},{0,3},{5,6},{7,4},{6,5},{4,7},{9,10},{11,8},{10,... | collective-permute-start | bytes 331784 | tf_op jit(solution)/shard_map/ppermute | solution.py:76
  94.6 5.6 %collective-permute-start.18 = (f32[48,128]{1,0:T(8,128)S(1)}, f32[48,128]{1,0:T(8,128)S(1)}, u32[]{:S(2)}, u32[]{:S(2)}) collective-permute-start(f32[48,128]{1,0:T(8,128)S(1)} %get-tuple-element.68.parts), channel_id=1, source_target_pairs={{0,2},{1,3},{2,0},{3,1},{4,6},{5,7},{6,4},{7,5},{8,10},{9,11},{10,... | collective-permute-start | bytes 73736 | tf_op jit(solution)/shard_map/ppermute | solution.py:636
  109.1 1.8 %collective-permute-start.19 = (f32[17,48,128]{2,1,0:T(8,128)S(1)}, f32[17,48,128]{2,1,0:T(8,128)S(1)}, u32[]{:S(2)}, u32[]{:S(2)}) collective-permute-start(f32[17,48,128]{2,1,0:T(8,128)S(1)} %get-tuple-element.74), channel_id=1, source_target_pairs={{0,16},{16,0},{1,17},{17,1},{2,18},{18,2},{3,19},{19,3},{4,20},{20... | collective-permute-start | bytes 1253384 | tf_op jit(solution)/shard_map/ppermute | solution.py:76
  112.3 4.5 %collective-permute-start.20 = (f32[144,128]{1,0:T(8,128)S(1)}, f32[144,128]{1,0:T(8,128)S(1)}, u32[]{:S(2)}, u32[]{:S(2)}) collective-permute-start(f32[144,128]{1,0:T(8,128)S(1)} %get-tuple-element.78), channel_id=1, source_target_pairs={{0,4},{4,0},{8,12},{12,8},{1,5},{5,1},{9,13},{13,9},{2,6},{6,2},{1... | collective-permute-start | bytes 221192 | tf_op jit(solution)/shard_map/ppermute | solution.py:76
  113.6 5.3 %collective-permute-start.21 = (f32[144,128]{1,0:T(8,128)S(1)}, f32[144,128]{1,0:T(8,128)S(1)}, u32[]{:S(2)}, u32[]{:S(2)}) collective-permute-start(f32[144,128]{1,0:T(8,128)S(1)} %get-tuple-element.79), channel_id=1, source_target_pairs={{4,8},{12,0},{8,4},{0,12},{5,9},{13,1},{9,5},{1,13},{6,10},{14,2},... | collective-permute-start | bytes 221192 | tf_op jit(solution)/shard_map/ppermute | solution.py:76
  119.4 8.4 %collective-permute-start.22 = (f32[54,8,128]{2,1,0:T(8,128)S(1)}, f32[54,8,128]{2,1,0:T(8,128)S(1)}, u32[]{:S(2)}, u32[]{:S(2)}) collective-permute-start(f32[54,8,128]{2,1,0:T(8,128)S(1)} %get-tuple-element.80), channel_id=1, source_target_pairs={{0,1},{1,0},{2,3},{3,2},{4,5},{5,4},{6,7},{7,6},{8,9},{9,8},{10,11... | collective-permute-start | bytes 663560 | tf_op jit(solution)/shard_map/ppermute | solution.py:76
  121.2 11.2 %collective-permute-start.23 = (f32[54,8,128]{2,1,0:T(8,128)S(1)}, f32[54,8,128]{2,1,0:T(8,128)S(1)}, u32[]{:S(2)}, u32[]{:S(2)}) collective-permute-start(f32[54,8,128]{2,1,0:T(8,128)S(1)} %get-tuple-element.81), channel_id=1, source_target_pairs={{1,2},{3,0},{2,1},{0,3},{5,6},{7,4},{6,5},{4,7},{9,10},{11,8},{10,... | collective-permute-start | bytes 663560 | tf_op jit(solution)/shard_map/ppermute | solution.py:76
  (2 other events, 2.0 us)

commit v2 on v1

v2 whole, which is shorter than its diff:
```python
import functools
import math

import jax
import jax.numpy as jnp
from jax import lax
from jax.experimental import pallas as pl
from jax.experimental.pallas import tpu as pltpu
from jax.sharding import PartitionSpec as P

BAND = 32
STEPS = 2
SWEEPS = 8
TIME_STEP = 0.4
VISCOSITY = 0.05
HA = 2
HB = SWEEPS
ZP = 8
ZO = 16
F32 = jnp.float32
BF16 = jnp.bfloat16


def call(kernel, outs, args, smem=(0,), scratch=(), name=None):
    specs = [
        pl.BlockSpec(memory_space=pltpu.SMEM if i in smem else pltpu.VMEM) for i in range(len(args))
    ]
    size = sum(a.size * 4 for a in args) + sum(math.prod(o) * 4 for o in outs)
    return pl.pallas_call(
        kernel,
        out_shape=[jax.ShapeDtypeStruct(o, F32) for o in outs],
        in_specs=specs,
        out_specs=[pl.BlockSpec(memory_space=pltpu.VMEM)] * len(outs),
        scratch_shapes=list(scratch),
        name=name,
        cost_estimate=pl.CostEstimate(flops=size, bytes_accessed=size, transcendentals=0),
        compiler_params=pltpu.CompilerParams(vmem_limit_bytes=48 << 20),
    )(*args)


def lanes_of(shape):
    return lax.broadcasted_iota(jnp.int32, shape, len(shape) - 1)


def rows_of(shape):
    return lax.broadcasted_iota(jnp.int32, shape, len(shape) - 2)


def roll(value, shift, axis):
    shift = shift % value.shape[axis]
    return pltpu.roll(value, shift, axis) if shift else value


def split3(value):
    high = value.astype(BF16)
    rest = value - high.astype(F32)
    middle = rest.astype(BF16)
    return high, middle, (rest - middle.astype(F32)).astype(BF16)


def dot0(left, right):
    return lax.dot_general(left, right, (((0,), (0,)), ((), ())), preferred_element_type=F32)


class Axis:
    def __init__(self, name):
        self.name = name
        self.count = n = lax.axis_size(name)
        self.first = [(i, i ^ 1) for i in range(n)]
        self.second = [((2 * i + 1) % n, (2 * i + 2) % n) for i in range(n // 2)]
        self.second = self.second + [(b, a) for a, b in self.second]
        self.perms = [self.first] if n == 2 else [self.first, self.second]
        self.inner = [(i, j) for i, j in self.second if abs(i - j) == 1]
        self.fold = n in (2, 4)
        self.cross = [(i, i ^ 2) for i in range(n)] if n == 4 else None

    def swap(self, sends, wide=False):
        perms = [self.first, self.inner] if wide else self.perms
        return [lax.ppermute(s, self.name, p) for s, p in zip(sends, perms)]


def roll_by(value, shift):
    return pltpu.roll(value, shift, 1)


def pick_side(index, high, low, which):
    even = (index % 2) == 0
    return jnp.where(even == (which == 0), high, low)


def from_sides(index, count, received, zero):
    even = (index % 2) == 0
    other = received[1] if len(received) > 1 else received[0]
    upper = jnp.where(even, received[0], other)
    lower = jnp.where(even, other, received[0])
    lower = jnp.where(index > 0, lower, zero)
    upper = jnp.where(index < count - 1, upper, zero)
    return lower, upper


def row_of(column):
    wide = jnp.broadcast_to(column, (column.shape[0], 128))
    row = jnp.sum(jnp.where(rows_of(wide.shape) == lanes_of(wide.shape), wide, 0.0), axis=0)
    return jnp.where(rows_of((8, 128)) == 0, row[None, :], 0.0)


def column_of(tile, count):
    wide = jnp.broadcast_to(tile[0:1, :], (count, 128))
    keep = rows_of(wide.shape) == lanes_of(wide.shape)
    return jnp.sum(jnp.where(keep, wide, 0.0), axis=1, keepdims=True)


def inflow_parts(info, column_at, inflow_x, inflow_y, turbines, cells_x, width):
    where_x = column_of(inflow_x.astype(F32), turbines).astype(jnp.int32) - info[0] * cells_x
    inflow_y = column_of(inflow_y.astype(F32), turbines).astype(jnp.int32)
    place = lanes_of((turbines, width)) + info[1] * width
    band = (place >= inflow_y) & (place < inflow_y + BAND)
    total = jnp.zeros((turbines, width), F32)
    for x in range(cells_x):
        total = jnp.where(where_x == x, column_at(x), total)
    return row_of(jnp.sum(jnp.where(band, total, 0.0), axis=1, keepdims=True))


def fill_xsend(info, sends, planes, parts, cells_x, cells_z):
    for which, out in enumerate(sends):
        start = pick_side(info[0], cells_x - HA, 0, which)
        for f in range(4):
            for k in range(HA):
                row = (f * HA + k) * cells_z
                out[row : row + cells_z, :] = planes(f, start + k)
        out[4 * HA * cells_z :, :] = parts


def begin_kernel(nsend, turbines, info, vel, press, inx, iny, *outs):
    _, cells_x, cells_z, width = vel.shape
    column = lambda x: jnp.sum(vel[0, x], axis=0, keepdims=True)
    parts = inflow_parts(info, column, inx[...], iny[...], turbines, cells_x, width)
    outs[0][...] = parts
    planes = lambda f, x: vel[f, x] if f < 3 else press[x]
    fill_xsend(info, outs[1 : 1 + nsend], planes, parts, cells_x, cells_z)


def pack_kernel(peers, capacity, info, kern, owners, lines, turbine, out):
    rows, width = kern.shape
    slots = peers * capacity
    wide = -(-peers // 128) * 128
    owner = owners[...]
    landing = (owner == lanes_of((rows, wide))).astype(F32)
    strict = (lanes_of((rows, rows)) < rows_of((rows, rows))).astype(BF16)
    earlier = jnp.dot(strict, landing.astype(BF16), preferred_element_type=F32)
    slot = jnp.sum(earlier * landing, axis=1, keepdims=True).astype(jnp.int32)
    live = rows_of((rows, 1)) < info[3]
    dest = jnp.where(live, owner * capacity + slot, -1)
    chosen = (dest == lanes_of((rows, slots))).astype(BF16)
    packed = sum(dot0(chosen, part) for part in split3(kern[...]))
    row8 = rows_of((8, rows))
    meta = jnp.where(row8 == 0, lines[...] + 1, jnp.where(row8 == 1, turbine[...], 0)).astype(F32)
    meta = sum(
        jnp.dot(part, chosen, preferred_element_type=F32) for part in split3(meta)[:2]
    )
    block = capacity + 8
    lane = lanes_of((8, 128))
    for peer in range(peers):
        out[peer * block : peer * block + capacity, :] = packed[
            peer * capacity : (peer + 1) * capacity, :
        ]
        at = peer * capacity
        piece = roll(meta[:, at // 128 * 128 : at // 128 * 128 + 128], -(at % 128), 1)
        out[peer * block + capacity : (peer + 1) * block, :] = jnp.where(lane < capacity, piece, 0.0)


def pack_edges(plane, count, depth):
    slot = 2 * depth
    groups = []
    for base in range(0, count, 128 // slot):
        packed = None
        for k in range(min(128 // slot, count - base)):
            value = plane(base + k)
            lane = lanes_of(value.shape) // slot
            packed = jnp.zeros_like(value) if packed is None else packed
            packed = jnp.where(lane == k, roll(value, k * slot + depth, 1), packed)
        groups.append(packed)
    return groups


def merge_edges(one, two, depth):
    half = lanes_of(one.shape) % (2 * depth) < depth
    return jnp.where(half, one, roll(two, depth, 1)), jnp.where(half, roll(two, -depth, 1), one)


def split_edges(lower, upper, depth):
    half = lanes_of(lower.shape) % (2 * depth) < depth
    return (
        jnp.where(half, lower, upper),
        jnp.where(half, roll(lower, -depth, 1), roll(upper, depth, 1)),
    )


def total_of(own, received, fold, base):
    if not fold:
        return own
    for r in received:
        own = own + r[base : base + 8, :]
    return own


def ext_plane(vel, press, halo, f, xe, cells_x):
    x = xe - HA
    if 0 <= x < cells_x:
        return vel[f, x] if f < 3 else press[x]
    return halo(f, x)


def x_halo(info, count, received, cells_x, cells_z):
    def halo(f, x):
        k = x - cells_x if x >= 0 else x + HA
        row = (f * HA + k) * cells_z
        pieces = [r[row : row + cells_z, :] for r in received]
        lower, upper = from_sides(info[0], count, pieces, 0.0)
        return upper if x >= 0 else lower

    return halo


def z_table(cells_x):
    table, row = [], 0
    for f, first, planes, depth in ((0, 1, 2, 1), (1, 2, 0, 1), (2, 1, 2, 2), (3, 2, 0, 1)):
        for xe in range(first, first + cells_x + planes):
            table.append((f, xe, depth, row))
            row += depth
    return table, row


def halo_y_kernel(ax, ay, info, vel, press, parts, *refs):
    nx = len(ax.perms)
    xr, outs = refs[:nx], refs[nx:]
    _, cells_x, cells_z, width = vel.shape
    ext = cells_x + 2 * HA
    total = total_of(parts[...], xr, ax.fold, 4 * HA * cells_z)
    halo = x_halo(info, ax.count, xr, cells_x, cells_z)
    packs = []
    for f in range(4):
        packs.append(
            pack_edges(lambda xe: ext_plane(vel, press, halo, f, xe, cells_x), ext, HA)[0]
        )
    outs[0][...] = total
    outs[1][...] = packs[1]
    for i in range(2):
        high, low = merge_edges(packs[2 * i], packs[2 * i + 1], HA)
        for which in range(len(ay.perms)):
            outs[2 + which][i * cells_z : (i + 1) * cells_z, :] = pick_side(
                info[1], high, low, which
            )
    for which in range(len(ay.perms)):
        outs[2 + which][2 * cells_z :, :] = total


def halo_z_kernel(ax, ay, az, info, vel, press, parts, *refs):
    nx, ny = len(ax.perms), len(ay.perms)
    ncross = 1 if ay.cross else 0
    xr, yr, cross = refs[:nx], refs[nx : nx + ny], refs[nx + ny : nx + ny + ncross]
    outs = refs[nx + ny + ncross :]
    _, cells_x, cells_z, width = vel.shape
    total = total_of(parts[...], yr, ay.fold, 2 * cells_z)
    for c in cross:
        total = total + c[...]
    halo = x_halo(info, ax.count, xr, cells_x, cells_z)
    outs[0][...] = total
    sends = outs[1:]

    def put(row, depth, value):
        high, low = value[cells_z - depth :, :], value[:depth, :]
        for which, out in enumerate(sends):
            out[row : row + depth, :] = pick_side(info[2], high, low, which)

    table, row = z_table(cells_x)
    for f, xe, depth, at in table:
        put(at, depth, ext_plane(vel, press, halo, f, xe, cells_x))
    for j in range(ny):
        for i in range(2):
            put(row, HA, yr[j][i * cells_z : (i + 1) * cells_z, :])
            row += HA
    for out in sends:
        pad = out.shape[0] - 8
        if pad > row:
            out[row:pad, :] = jnp.zeros((pad - row, width), F32)
        out[pad:, :] = total


def force_field(rows, thrust, total, depth_total, peers, capacity, lines_total):
    turbines = thrust.shape[0]
    width = rows.shape[-1]
    slots = peers * capacity
    block = capacity + 8
    uref = total / (BAND * depth_total)
    magnitude = 0.5 * thrust * uref * jnp.abs(uref)
    magnitude = jnp.broadcast_to(magnitude, (turbines, width))
    mag_parts = split3(magnitude)
    force = jnp.zeros((lines_total, width), F32)
    for first in range(0, slots, 128):
        line = jnp.zeros((8, 128), F32)
        values = []
        for at in range(first, min(first + 128, slots), capacity):
            peer = at // capacity
            line = line + roll(
                rows[peer * block + capacity : (peer + 1) * block, :], at - first, 1
            )
            values.append(rows[peer * block : peer * block + capacity, :])
        values = jnp.concatenate(values, axis=0) if len(values) > 1 else values[0]
        used = values.shape[0]
        line = line.astype(jnp.int32)
        turbine = line[1:2, :used]
        line = line[0:1, :used]
        chosen = (rows_of((turbines, used)) == turbine).astype(BF16)
        scale = sum(dot0(chosen, part) for part in mag_parts)
        values = split3(values * scale)
        landing = (rows_of((lines_total, used)) == line - 1).astype(BF16)
        for part in values[:2]:
            force = force + jnp.dot(landing, part, preferred_element_type=F32)
    return force


def star_kernel(ax, ay, az, peers, capacity, turbines, info, vel, press, parts, rows, thrust, own_v, *refs):
    nx, ny, nz = len(ax.perms), len(ay.perms), len(az.perms)
    ncross = 1 if az.cross else 0
    xr, refs = refs[:nx], refs[nx:]
    yr, refs = refs[:ny], refs[ny:]
    zr, refs = refs[:nz], refs[nz:]
    cross, refs = refs[:ncross], refs[ncross:]
    star, p1, s6, edge = refs[:4]
    sends = refs[4 : 4 + nx]
    fm, hm, su, svh, sw, force_ref = refs[4 + nx :]
    _, cells_x, cells_z, width = vel.shape
    ext = cells_x + 2 * HA
    total = total_of(parts[...], zr, az.fold, zr[0].shape[0] - 8)
    for c in cross:
        total = total + c[...]
    force_ref[...] = force_field(
        rows,
        column_of(thrust[...], turbines),
        column_of(total, turbines),
        cells_z * az.count,
        peers,
        capacity,
        cells_x * cells_z,
    )
    halo = x_halo(info, ax.count, xr, cells_x, cells_z)
    end = ZO + cells_z
    for f in range(4):
        for xe in range(ext):
            if f == 0 or 0 < xe < ext - 1:
                fm[f, xe, ZO:end, :] = ext_plane(vel, press, halo, f, xe, cells_x)
    table, corner = z_table(cells_x)
    for f, xe, depth, at in table:
        lower, upper = from_sides(info[2], az.count, [r[at : at + depth, :] for r in zr], 0.0)
        fm[f, xe, ZO - depth : ZO, :] = lower
        fm[f, xe, end : end + depth, :] = upper
    for i in range(2):
        zs = [
            from_sides(
                info[2],
                az.count,
                [r[corner + (2 * j + i) * HA : corner + (2 * j + i + 1) * HA, :] for r in zr],
                0.0,
            )
            for j in range(ny)
        ]
        for rows_at, pieces in (
            (slice(ZO, end), [r[i * cells_z : (i + 1) * cells_z, :] for r in yr]),
            (slice(ZO - HA, ZO), [z[0] for z in zs]),
            (slice(end, end + HA), [z[1] for z in zs]),
        ):
            lower, upper = from_sides(info[1], ay.count, pieces, 0.0)
            one, two = split_edges(lower, upper, HA)
            hm[2 * i, rows_at, :] = one
            hm[2 * i + 1, rows_at, :] = two

    rate = TIME_STEP * VISCOSITY
    lane = lanes_of((8, width))
    slot = 2 * HA

    def turn(xe):
        return (width - HA) - slot * xe + jnp.where(slot * xe + HA > width, width, 0)

    def around(f, xe, r):
        mid = fm[f, xe, r : r + 8, :]
        far = roll_by(hm[f, r : r + 8, :], turn(xe))
        total = fm[f, xe - 1, r : r + 8, :] + fm[f, xe + 1, r : r + 8, :]
        total = total + (fm[f, xe, r - 1 : r + 7, :] + fm[f, xe, r + 1 : r + 9, :])
        left = roll(jnp.where(lane == width - 1, far, mid), 1, 1)
        right = roll(jnp.where(lane == 0, far, mid), -1, 1)
        return total + (left + right), mid

    def diffused(f, xe, r):
        total, mid = around(f, xe, r)
        return mid + rate * (total - 6.0 * mid)

    def u_plane(k, carry):
        for t in range(0, cells_z, 8):
            su[k, t : t + 8, :] = diffused(0, k + 1, ZO + t)
        return carry

    lax.fori_loop(0, cells_x + 2, u_plane, 0)
    su[0] = jnp.where(info[0] > 0, su[0], 0.0)
    su[cells_x + 1] = jnp.where(info[0] < ax.count - 1, su[cells_x + 1], 0.0)
    place = lane % slot
    keep_y = ((place >= HA) | (info[1] > 0)) & ((place < HA) | (info[1] < ay.count - 1))
    for t in range(0, cells_z, 8):
        r = ZO + t
        mid = hm[1, r : r + 8, :]
        inner = own_v[t : t + 8, :]
        total = roll(mid, slot, 1) + roll(mid, -slot, 1)
        total = total + (hm[1, r - 1 : r + 7, :] + hm[1, r + 1 : r + 9, :])
        total = total + roll(jnp.where(place == HA - 1, inner, mid), 1, 1)
        total = total + roll(jnp.where(place == HA, inner, mid), -1, 1)
        svh[t : t + 8, :] = jnp.where(keep_y, mid + rate * (total - 6.0 * mid), 0.0)

    def forced(x, carry):
        xe = x + HA
        for t in range(0, cells_z, 8):
            push = force_ref[pl.ds(pl.multiple_of(x * cells_z + t, 8), 8), :]
            u = su[x + 1, t : t + 8, :] - TIME_STEP * push
            su[x + 1, t : t + 8, :] = u
            star[0, x, t : t + 8, :] = u
        for t in range(-8, cells_z + 8, 8):
            w = diffused(2, xe, ZO + t)
            if t < 0:
                w = jnp.where(info[2] > 0, w, 0.0)
            elif t >= cells_z:
                w = jnp.where(info[2] < az.count - 1, w, 0.0)
            else:
                star[2, x, t : t + 8, :] = w
            sw[x, t + 8 : t + 16, :] = w
        for t in range(0, cells_z, 8):
            v = diffused(1, xe, ZO + t)
            star[1, x, t : t + 8, :] = v
            far = roll_by(svh[t : t + 8, :], turn(xe))
            left = roll(jnp.where(lane == width - 1, far, v), 1, 1)
            right = roll(jnp.where(lane == 0, far, v), -1, 1)
            s6[x, t : t + 8, :] = right - left
        return carry

    lax.fori_loop(0, cells_x, forced, 0)

    def first(x, carry):
        for t in range(0, cells_z, 8):
            source = s6[x, t : t + 8, :] + (sw[x, t + 9 : t + 17, :] - sw[x, t + 7 : t + 15, :])
            source = source + (su[x + 2, t : t + 8, :] - su[x, t : t + 8, :])
            source = source * (0.5 / 6.0)
            s6[x, t : t + 8, :] = source
            total, _ = around(3, x + HA, ZO + t)
            p1[x, t : t + 8, :] = total * (1.0 / 6.0) - source
        return carry

    lax.fori_loop(0, cells_x, first, 0)
    scale = 0.5 * TIME_STEP / 6.0
    edge[0] = scale * force_ref[:cells_z, :]
    edge[1] = scale * force_ref[(cells_x - 1) * cells_z :, :]
    for which, out in enumerate(sends):
        start = pick_side(info[0], cells_x - HB, 0, which)
        out[:HB] = p1[pl.ds(start, HB)]
        out[HB : 2 * HB] = s6[pl.ds(start, HB)]
        out[2 * HB] = pick_side(info[0], edge[1], edge[0], which)


def deep_y_kernel(ax, ay, info, p1, s6, edge, *refs):
    nx = len(ax.perms)
    xr, refs = refs[:nx], refs[nx:]
    px, sx = refs[:2]
    sends = refs[2:]
    cells_x, cells_z, width = p1.shape
    one_sided = ax.count == 2
    ext = px.shape[0]
    off = jnp.where(info[0] == 0, 0, HB) if one_sided else HB
    px[pl.ds(off, cells_x)] = p1[...]
    sx[pl.ds(off, cells_x)] = s6[...]
    if one_sided:
        away = jnp.where(info[0] == 0, cells_x, 0)
        px[pl.ds(away, HB)] = xr[0][:HB]
        sx[pl.ds(away, HB)] = xr[0][HB : 2 * HB]
        near = [(True, info[0] == 0)]
    else:
        for k in range(HB):
            lower, upper = from_sides(info[0], ax.count, [r[k] for r in xr], 0.0)
            px[k] = lower
            px[HB + cells_x + k] = upper
            lower, upper = from_sides(info[0], ax.count, [r[HB + k] for r in xr], 0.0)
            sx[k] = lower
            sx[HB + cells_x + k] = upper
    lower, upper = from_sides(info[0], ax.count, [r[2 * HB] for r in xr], 0.0)
    has_lower = (info[0] > 0).astype(F32)
    has_upper = (info[0] < ax.count - 1).astype(F32)
    changes = [
        (off, lower),
        (off + cells_x - 1, -upper),
        (jnp.maximum(off - 1, 0), -edge[0] * has_lower),
        (jnp.minimum(off + cells_x, ext - 1), edge[1] * has_upper),
    ]
    for at, change in changes:
        sx[at] = sx[at] + change
        px[at] = px[at] - change
    packs_p = pack_edges(lambda x: px[x], ext, HB)
    packs_s = pack_edges(lambda x: sx[x], ext, HB)
    for i, (one, two) in enumerate(zip(packs_p, packs_s)):
        high, low = merge_edges(one, two, HB)
        for which in range(len(ay.perms)):
            sends[which][i * cells_z : (i + 1) * cells_z, :] = pick_side(info[1], high, low, which)


def deep_z_kernel(ay, az, npack, info, px, sx, *refs):
    ny = len(ay.perms)
    yr, sends = refs[:ny], refs[ny:]
    ext, cells_z, width = px.shape
    for which in range(len(az.perms)):
        out = sends[which]
        start = pl.multiple_of(pick_side(info[2], cells_z - HB, 0, which), 8)
        out[:ext] = px[:, pl.ds(start, HB), :]
        out[ext : 2 * ext] = sx[:, pl.ds(start, HB), :]
        for j in range(ny):
            for i in range(npack):
                at = pl.multiple_of(i * cells_z + start, 8)
                out[2 * ext + j * npack + i] = yr[j][pl.ds(at, HB), :]


def sweep_kernel(ax, ay, az, npack, last, turbines, info, px, sx, star, inx, iny, *refs):
    ny, nz = len(ay.perms), len(az.perms)
    yr, refs = refs[:ny], refs[ny:]
    zr, refs = refs[:nz], refs[nz:]
    vel, press = refs[:2]
    refs = refs[2:]
    if not last:
        parts, refs = refs[0], refs[1:]
        sends, refs = refs[: len(ax.perms)], refs[len(ax.perms) :]
    pm, sm, ph, sh = refs
    ext, cells_z, width = px.shape
    cells_x = press.shape[0]
    one_sided = ax.count == 2
    off = jnp.where(info[0] == 0, 0, HB) if one_sided else HB
    slot = 2 * HB
    per = width // slot
    low, end = ZO - ZP, ZO + cells_z
    blank = jnp.zeros((end + 2 * ZP, width), F32)
    for b in range(2):
        pm[b, 0] = blank
        pm[b, ext + 1] = blank
        ph[b, 0] = blank
        ph[b, npack + 1] = blank
        for x in range(ext):
            pm[b, x + 1, :low, :] = blank[:low]
            pm[b, x + 1, end + ZP :, :] = blank[:low]
        for g in range(npack):
            ph[b, g + 1, :low, :] = blank[:low]
            ph[b, g + 1, end + ZP :, :] = blank[:low]

    def z_tile(k):
        return from_sides(info[2], az.count, [r[k] for r in zr], 0.0)

    for x in range(ext):
        lower, upper = z_tile(x)
        pm[0, x + 1, low:ZO, :] = lower
        pm[0, x + 1, end : end + ZP, :] = upper
        pm[0, x + 1, ZO:end, :] = px[x]
        lower, upper = z_tile(ext + x)
        sm[x, :ZP, :] = lower
        sm[x, ZP + cells_z :, :] = upper
        sm[x, ZP : ZP + cells_z, :] = sx[x]
    for i in range(npack):
        zs = [z_tile(2 * ext + j * npack + i) for j in range(ny)]
        for start, stop, pieces in (
            (ZO, end, [r[i * cells_z : (i + 1) * cells_z, :] for r in yr]),
            (low, ZO, [z[0] for z in zs]),
            (end, end + ZP, [z[1] for z in zs]),
        ):
            lower, upper = from_sides(info[1], ay.count, pieces, 0.0)
            one, two = split_edges(lower, upper, HB)
            ph[0, i + 1, start:stop, :] = one
            sh[i, start - low : stop - low, :] = two

    lane = lanes_of((8, width))
    place = lane % slot
    keep_y = ((place >= HB) | (info[1] > 0)) & ((place < HB) | (info[1] < ay.count - 1))
    sixth = 1.0 / 6.0
    weight_y = jnp.where(keep_y, sixth, 0.0)
    first_lane, last_lane = lane == 0, lane == width - 1

    def sweep(number, carry):
        now, then = number % 2, 1 - number % 2

        def group(g, carry):
            scale = 1.0
            if not one_sided:
                outside = (g == 0) & (info[0] == 0)
                outside |= (g == npack - 1) & (info[0] == ax.count - 1)
                scale = jnp.where(outside, 0.0, 1.0)
            for t in range(0, cells_z + 2 * ZP, 8):
                r = low + t
                weight = scale
                if t < ZP:
                    weight = weight * jnp.where(info[2] > 0, 1.0, 0.0)
                elif t >= ZP + cells_z:
                    weight = weight * jnp.where(info[2] < az.count - 1, 1.0, 0.0)
                halo = ph[now, g + 1, r : r + 8, :]
                edges = halo
                for k in range(per):
                    x = g * per + k
                    mid = pm[now, x + 1, r : r + 8, :]
                    far = roll(halo, -(slot * k + HB), 1)
                    edges = jnp.where(lane // slot == k, roll(mid, slot * k + HB, 1), edges)
                    total = pm[now, x, r : r + 8, :] + pm[now, x + 2, r : r + 8, :]
                    total = total + (
                        pm[now, x + 1, r - 1 : r + 7, :] + pm[now, x + 1, r + 1 : r + 9, :]
                    )
                    left = roll(jnp.where(last_lane, far, mid), 1, 1)
                    right = roll(jnp.where(first_lane, far, mid), -1, 1)
                    total = total + (left + right)
                    pm[then, x + 1, r : r + 8, :] = (
                        total * (sixth * weight) - sm[x, t : t + 8, :]
                    )
                total = ph[now, g + 1, r - 1 : r + 7, :] + ph[now, g + 1, r + 1 : r + 9, :]
                total = total + roll(jnp.where(place == HB - 1, edges, halo), 1, 1)
                total = total + roll(jnp.where(place == HB, edges, halo), -1, 1)
                before = jnp.where(lane >= width - slot, ph[now, g, r : r + 8, :], halo)
                after = jnp.where(lane < slot, ph[now, g + 2, r : r + 8, :], halo)
                total = total + (roll(before, slot, 1) + roll(after, -slot, 1))
                ph[then, g + 1, r : r + 8, :] = total * (weight_y * weight) - sh[g, t : t + 8, :]
            return carry

        return lax.fori_loop(0, npack, group, carry)

    lax.fori_loop(0, SWEEPS - 1, sweep, 0)
    done = (SWEEPS - 1) % 2
    first_group = off // per

    def gradient(q, carry):
        g = first_group + q
        for k in range(per):
            x = q * per + k
            at = g * per + k + 1
            for t in range(0, cells_z, 8):
                r = ZO + t
                mid = pm[done, at, r : r + 8, :]
                far = roll(ph[done, g + 1, r : r + 8, :], -(slot * k + HB), 1)
                left = roll(jnp.where(last_lane, far, mid), 1, 1)
                right = roll(jnp.where(first_lane, far, mid), -1, 1)
                press[x, t : t + 8, :] = mid
                gx = pm[done, at + 1, r : r + 8, :] - pm[done, at - 1, r : r + 8, :]
                gz = pm[done, at, r + 1 : r + 9, :] - pm[done, at, r - 1 : r + 7, :]
                vel[0, x, t : t + 8, :] = star[0, x, t : t + 8, :] - 0.5 * gx
                vel[1, x, t : t + 8, :] = star[1, x, t : t + 8, :] - 0.5 * (right - left)
                vel[2, x, t : t + 8, :] = star[2, x, t : t + 8, :] - 0.5 * gz
        return carry

    lax.fori_loop(0, cells_x // per, gradient, 0)
    if not last:
        column = lambda x: jnp.sum(vel[0, x], axis=0, keepdims=True)
        share = inflow_parts(info, column, inx[...], iny[...], turbines, cells_x, width)
        parts[...] = share
        planes = lambda f, x: vel[f, x] if f < 3 else press[x]
        fill_xsend(info, sends, planes, share, cells_x, cells_z)


def body(
    velocity, pressure, kernel, owners, lines, point_turbine, row_counts, thrust, inflow_x, inflow_y
):
    _, cells_x, cells_z, width = velocity.shape
    row_total = kernel.shape[0]
    turbines = thrust.shape[0]
    ax, ay, az = Axis("gx"), Axis("gy"), Axis("gz")
    peers = ax.count * ay.count
    capacity = 2 * row_total // peers
    nx, ny, nz = len(ax.perms), len(ay.perms), len(az.perms)
    ext_a = cells_x + 2 * HA
    ext_b = cells_x + (HB if ax.count == 2 else 2 * HB)
    pack_b = ext_b * 2 * HB // width
    tall = cells_z + 2 * ZO
    vm = lambda *shape: pltpu.VMEM(shape, F32)
    info = jnp.stack(
        [
            lax.axis_index("gx"),
            lax.axis_index("gy"),
            lax.axis_index("gz"),
            row_counts.reshape(()),
        ]
    ).astype(jnp.int32)
    inx = inflow_x[None, :]
    iny = inflow_y[None, :]
    push = jnp.pad(thrust[None, :], ((0, 0), (0, 128 - turbines)))
    wide = lambda row: jnp.pad(row, ((0, 0), (0, 128 - turbines)))
    inx, iny = wide(inx), wide(iny)
    block = capacity + 8
    (packed,) = call(
        functools.partial(pack_kernel, peers, capacity),
        [(peers * block, width)],
        [info, kernel, owners, lines[None, :], point_turbine[None, :]],
        name="pack_rows",
    )
    rows = lax.all_to_all(
        packed.reshape(peers, block, width), ("gx", "gy"), split_axis=0, concat_axis=0, tiled=True
    ).reshape(peers * block, width)
    xsize = (4 * HA * cells_z + 8, width)
    vel, press = velocity, pressure
    parts, *xsend = call(
        functools.partial(begin_kernel, nx, turbines),
        [(8, width)] + [xsize] * nx,
        [info, vel, press, inx, iny],
        name="begin",
    )
    zrows = z_table(cells_x)[1] + ny * 2 * HA
    zrows = -(-zrows // 8) * 8 + 8
    for repeat in range(STEPS):
        last = repeat == STEPS - 1
        if not ax.fold:
            parts = lax.psum(parts, "gx")
        xr = ax.swap(xsend)
        parts, own_v, *ysend = call(
            functools.partial(halo_y_kernel, ax, ay),
            [(8, width), (cells_z, width)] + [(2 * cells_z + 8, width)] * ny,
            [info, vel, press, parts, *xr],
            name="halo_y",
        )
        yr = ay.swap(ysend)
        cross = [lax.ppermute(parts, "gy", ay.cross)] if ay.cross else []
        if not ay.fold:
            parts = lax.psum(parts, "gy")
        parts, *zsend = call(
            functools.partial(halo_z_kernel, ax, ay, az),
            [(8, width)] + [(zrows, width)] * nz,
            [info, vel, press, parts, *xr, *yr, *cross],
            name="halo_z",
        )
        zr = az.swap(zsend)
        cross = [lax.ppermute(parts, "gz", az.cross)] if az.cross else []
        if not az.fold:
            parts = lax.psum(parts, "gz")
        star, p1, s6, edge, *xsend = call(
            functools.partial(star_kernel, ax, ay, az, peers, capacity, turbines),
            [
                (3, cells_x, cells_z, width),
                (cells_x, cells_z, width),
                (cells_x, cells_z, width),
                (2, cells_z, width),
            ]
            + [(2 * HB + 1, cells_z, width)] * nx,
            [info, vel, press, parts, rows, push, own_v, *xr, *yr, *zr, *cross],
            scratch=[
                vm(4, ext_a, tall, width),
                vm(4, tall, width),
                vm(cells_x + 2, cells_z, width),
                vm(cells_z, width),
                vm(cells_x, cells_z + 2 * ZP, width),
                vm(cells_x * cells_z, width),
            ],
            name="star",
        )
        xr = ax.swap(xsend)
        px, sx, *ysend = call(
            functools.partial(deep_y_kernel, ax, ay),
            [(ext_b, cells_z, width)] * 2 + [(pack_b * cells_z, width)] * ny,
            [info, p1, s6, edge, *xr],
            name="deep_y",
        )
        yr = ay.swap(ysend)
        zsend = call(
            functools.partial(deep_z_kernel, ay, az, pack_b),
            [(2 * ext_b + ny * pack_b, HB, width)] * nz,
            [info, px, sx, *yr],
            name="deep_z",
        )
        zr = az.swap(zsend, wide=True)
        outs = [(3, cells_x, cells_z, width), (cells_x, cells_z, width)]
        if not last:
            outs = outs + [(8, width)] + [xsize] * nx
        results = call(
            functools.partial(sweep_kernel, ax, ay, az, pack_b, last, turbines),
            outs,
            [info, px, sx, star, inx, iny, *yr, *zr],
            scratch=[
                vm(2, ext_b + 2, tall, width),
                vm(ext_b, cells_z + 2 * ZP, width),
                vm(2, pack_b + 2, tall, width),
                vm(pack_b, cells_z + 2 * ZP, width),
            ],
            name="sweeps",
        )
        vel, press = results[:2]
        if not last:
            parts, *xsend = results[2:]
    return (vel, press)


def solution(mesh):
    placed = (
        P(None, "gx", "gz", "gy"),
        P("gx", "gz", "gy"),
        P(("gx", "gy", "gz"), None),
        P(("gx", "gy", "gz"), None),
        P(("gx", "gy", "gz")),
        P(("gx", "gy", "gz")),
        P("gx", "gy", "gz"),
        P(),
        P(),
        P(),
    )
    return jax.shard_map(
        body,
        mesh=mesh,
        in_specs=placed,
        out_specs=(P(None, "gx", "gz", "gy"), P("gx", "gz", "gy")),
        check_vma=False,
    )
```

time: 154 us -> 358 us (2.32)
  Pallas kernels: 67.2 us -> 282 us
  waiting for transfers between devices: 46.3 us -> 34.6 us
    pallas_call x14, Pallas kernels: 67.2 us -> 282 us  [call(): pl.pallas_call(kernel, out_shape=[jax.ShapeDtypeStruct(o, F32) for o in o...]
    ppermute x20, waiting for transfers between devices: 33.7 us -> 24.8 us  [swap(): return [lax.ppermute(s, self.name, p) for s, p in zip(sends, perms)]]
  transfers between devices with their start and end apart: 25 -> 25, of which waited for: 19 -> 17; matrix products, arithmetic and copies ran while one was open for 0% -> 0% of each run, Pallas kernels for 3% -> 1%
where the time goes in v2:
time: 358 us; the launch traced here: 357 us
  Pallas kernels  282 us (79%)
  starting transfers between devices  34.8 us (10%)
  waiting for transfers between devices  34.6 us (10%)
  local copies, waits for them, and re-layouts  3.76 us (1%)
    pallas_call x14, Pallas kernels, call(): pl.pallas_call(kernel, out_shape=[jax.ShapeDtypeStruct(o, F32) for o in o...  282 us
    ppermute x20, waiting for transfers between devices, swap(): return [lax.ppermute(s, self.name, p) for s, p in zip(sends, perms)]  24.8 us
    ppermute x20, starting transfers between devices, swap(): return [lax.ppermute(s, self.name, p) for s, p in zip(sends, perms)]  22.5 us
  transfers between devices with their start and end apart: 25, of which 17 were waited for; matrix products, arithmetic and copies ran while one was open for 0% of the time, Pallas kernels for 1%

profile of v2, /device:TPU:12, one launch (start us, length us, event | category | flops | bytes accessed | tf_op | source)
XLA Modules:
  0.0 356.6 jit_solution(88482903491915427)
XLA Ops:
  6.0 2.2 pack_rows.1
  8.2 4.3 %all-to-all-start = ((f32[8,72,128]{2,1,0:T(8,128)}), f32[8,72,128]{2,1,0:T(8,128)S(1)}, u32[]{:S(2)}, u32[]{:S(2)}) async-start(f32[8,72,128]{2,1,0:T(8,128)} %bitcast.8), calls=%async_computation | async-start | bytes 589824 | tf_op jit(solution)/shard_map/all_to_all | solution.py:697
  13.7 1.5 collective-permute-start.1
  15.3 1.9 collective-permute-start.3
  17.3 1.7 collective-permute-done.3.refs_3_
  21.7 2.7 collective-permute-start.5
  25.6 3.3 collective-permute-done.6.refs_5_
  28.9 11.3 %star.2 = (f32[3,16,48,128]{3,2,1,0:T(8,128)S(1)}, f32[16,48,128]{2,1,0:T(8,128)S(1)}, f32[16,48,128]{2,1,0:T(8,128)S(1)}, f32[2,48,128]{2,1,0:T(8,128)S(1)}, f32[17,48,128]{2,1,0:T(8,128)S(1)}) custom-call(s32[4]{0:T(128)S(1)} %pad_add_fusion.info, f32[3,16,48,128]{3,2,1,0:T(8,128)S(1)} %copy-done.1, f32[16,48,128]{2,1,0:T(8,128)S(1)} %copy-done.3, ...), custom_call_target="tpu_custom_call" | custom-call | flops 4747792 | bytes 4747792 | tf_op jit(solution)/shard_map/star/pallas_call | solution.py:29
  40.3 1.7 collective-permute-done.7.refs_0_
  43.6 2.5 collective-permute-start.9
  46.1 1.8 collective-permute-done.8.refs_0_
  47.9 2.1 collective-permute-done.9.refs_1_
  50.6 1.4 collective-permute-start.10
  52.0 2.5 collective-permute-start.11
  54.5 2.5 collective-permute-done.10.refs_2_
  56.9 2.9 collective-permute-done.11.refs_3_
  59.9 124.3 %sweeps.2 = (f32[3,16,48,128]{3,2,1,0:T(8,128)S(1)}, f32[16,48,128]{2,1,0:T(8,128)S(1)}, f32[8,128]{1,0:T(8,128)S(1)}, f32[392,128]{1,0:T(8,128)S(1)}) custom-call(s32[4]{0:T(128)S(1)} %pad_add_fusion.info, f32[24,48,128]{2,1,0:T(8,128)S(1)} %get-tuple-element.57.px, f32[24,48,128]{2,1,0:T(8,128)S(1)} %get-tuple-element.58.sx, ...), custom_call_target="tpu_custom_call" | custom-call | flops 4727824 | bytes 4727824 | tf_op jit(solution)/shard_map/sweeps/pallas_call | solution.py:29
  184.2 1.4 collective-permute-done.12.refs_0_
  188.1 1.3 collective-permute-start.14
  190.4 2.8 collective-permute-done.15.refs_3_
  194.6 3.7 %collective-permute-start.18 = (f32[8,128]{1,0:T(8,128)S(1)}, f32[8,128]{1,0:T(8,128)S(1)}, u32[]{:S(2)}, u32[]{:S(2)}) collective-permute-start(f32[8,128]{1,0:T(8,128)S(1)} %get-tuple-element.71.parts), channel_id=1, source_target_pairs={{0,2},{1,3},{2,0},{3,1},{4,6},{5,7},{6,4},{7,5},{8,10},{9,11},{10,... | collective-permute-start | bytes 12296 | tf_op jit(solution)/shard_map/ppermute | solution.py:732
  198.3 2.2 collective-permute-done.18.refs_5_
  200.4 11.3 %star.3 = (f32[3,16,48,128]{3,2,1,0:T(8,128)S(1)}, f32[16,48,128]{2,1,0:T(8,128)S(1)}, f32[16,48,128]{2,1,0:T(8,128)S(1)}, f32[2,48,128]{2,1,0:T(8,128)S(1)}, f32[17,48,128]{2,1,0:T(8,128)S(1)}) custom-call(s32[4]{0:T(128)S(1)} %pad_add_fusion.info, f32[3,16,48,128]{3,2,1,0:T(8,128)S(1)} %get-tuple-element.64.vel, ...), custom_call_target="tpu_custom_call" | custom-call | flops 4747792 | bytes 4747792 | tf_op jit(solution)/shard_map/star/pallas_call | solution.py:29
  211.8 1.7 collective-permute-done.19.refs_0_
  215.6 1.5 collective-permute-start.21
  217.0 2.5 collective-permute-done.20.refs_0_
  219.5 1.4 collective-permute-done.21.refs_1_
  221.5 1.6 collective-permute-start.22
  223.1 3.3 collective-permute-start.23
  226.4 1.9 collective-permute-done.22.refs_2_
  228.3 3.1 collective-permute-done.23.refs_3_
  231.4 125.1 %sweeps.3 = (f32[3,16,48,128]{3,2,1,0:T(8,128)}, f32[16,48,128]{2,1,0:T(8,128)}) custom-call(s32[4]{0:T(128)S(1)} %pad_add_fusion.info, f32[24,48,128]{2,1,0:T(8,128)S(1)} %get-tuple-element.79.px, f32[24,48,128]{2,1,0:T(8,128)S(1)} %get-tuple-element.80.sx, f32[3,16,48,128]{3,2,1,0:T(8,128)S(1)} %get-tuple-element.81.star, s32[1,128]{1,0:T(1,128)S(1)} %pad.11.inx, ...), custom_call_target="tpu_custom_call" | custom-call | flops 4523024 | bytes 4523024 | tf_op jit(solution)/shard_map/sweeps/pallas_call | solution.py:29
  (55 shorter events, 19.6 us)
Async XLA Ops:
  0.6 5.2 %copy-start.7 = (s32[256,1]{0,1:T(1,128)S(1)}, s32[256,1]{0,1:T(1,128)}, u32[]{:S(2)}) copy-start(s32[256,1]{0,1:T(1,128)} %param.13) | copy-start | bytes 3076
  0.6 5.3 %copy-start.6 = (s32[256]{0:T(256)S(1)}, s32[256]{0:T(256)}, u32[]{:S(2)}) copy-start(s32[256]{0:T(256)} %param.15) | copy-start | bytes 3076
  0.7 5.3 %copy-start.5 = (s32[256]{0:T(256)S(1)}, s32[256]{0:T(256)}, u32[]{:S(2)}) copy-start(s32[256]{0:T(256)} %param.14) | copy-start | bytes 3076
  2.7 1.3 copy-start
  5.0 7.5 %copy-start.1 = (f32[3,16,48,128]{3,2,1,0:T(8,128)S(1)}, f32[3,16,48,128]{3,2,1,0:T(8,128)}, u32[]{:S(2)}) copy-start(f32[3,16,48,128]{3,2,1,0:T(8,128)} %vel.7) | copy-start | bytes 3538948
  5.0 7.5 %copy-start.3 = (f32[16,48,128]{2,1,0:T(8,128)S(1)}, f32[16,48,128]{2,1,0:T(8,128)}, u32[]{:S(2)}) copy-start(f32[16,48,128]{2,1,0:T(8,128)} %press.7) | copy-start | bytes 1179652
  5.7 6.7 %collective-permute-start = (f32[392,128]{1,0:T(8,128)S(1)}, f32[392,128]{1,0:T(8,128)S(1)}, u32[]{:S(2)}, u32[]{:S(2)}) collective-permute-start(f32[392,128]{1,0:T(8,128)S(1)} %get-tuple-element.45), channel_id=1, source_target_pairs={{0,16},{16,0},{1,17},{17,1},{2,18},{18,2},{3,19},{19,3},{4,20},{20... | collective-permute-start | bytes 602120 | tf_op jit(solution)/shard_map/ppermute | solution.py:79
  8.2 17.5 %all-to-all-start = ((f32[8,72,128]{2,1,0:T(8,128)}), f32[8,72,128]{2,1,0:T(8,128)S(1)}, u32[]{:S(2)}, u32[]{:S(2)}) async-start(f32[8,72,128]{2,1,0:T(8,128)} %bitcast.8), calls=%async_computation | async-start | bytes 589824 | tf_op jit(solution)/shard_map/all_to_all | solution.py:697
  13.7 11.9 %copy-start.8 = (f32[48]{0:T(128)S(1)}, f32[48]{0:T(128)}, u32[]{:S(2)}) copy-start(f32[48]{0:T(128)} %param.17) | copy-start | bytes 580
  13.7 6.3 %collective-permute-start.1 = (f32[104,128]{1,0:T(8,128)S(1)}, f32[104,128]{1,0:T(8,128)S(1)}, u32[]{:S(2)}, u32[]{:S(2)}) collective-permute-start(f32[104,128]{1,0:T(8,128)S(1)} %get-tuple-element.47), channel_id=1, source_target_pairs={{0,4},{4,0},{8,12},{12,8},{1,5},{5,1},{9,13},{13,9},{2,6},{6,2},{1... | collective-permute-start | bytes 159752 | tf_op jit(solution)/shard_map/ppermute | solution.py:79
  15.2 5.3 %collective-permute-start.2 = (f32[104,128]{1,0:T(8,128)S(1)}, f32[104,128]{1,0:T(8,128)S(1)}, u32[]{:S(2)}, u32[]{:S(2)}) collective-permute-start(f32[104,128]{1,0:T(8,128)S(1)} %get-tuple-element.48), channel_id=1, source_target_pairs={{4,8},{12,0},{8,4},{0,12},{5,9},{13,1},{9,5},{1,13},{6,10},{14,2},... | collective-permute-start | bytes 159752 | tf_op jit(solution)/shard_map/ppermute | solution.py:79
  15.3 3.6 %collective-permute-start.3 = (f32[8,128]{1,0:T(8,128)S(1)}, f32[8,128]{1,0:T(8,128)S(1)}, u32[]{:S(2)}, u32[]{:S(2)}) collective-permute-start(f32[8,128]{1,0:T(8,128)S(1)} %get-tuple-element.46.parts), channel_id=1, source_target_pairs={{0,8},{4,12},{8,0},{12,4},{1,9},{5,13},{9,1},{13,5},{2,10},{6,14},... | collective-permute-start | bytes 12296 | tf_op jit(solution)/shard_map/ppermute | solution.py:722
  21.2 7.7 %collective-permute-start.4 = (f32[104,128]{1,0:T(8,128)S(1)}, f32[104,128]{1,0:T(8,128)S(1)}, u32[]{:S(2)}, u32[]{:S(2)}) collective-permute-start(f32[104,128]{1,0:T(8,128)S(1)} %get-tuple-element.51), channel_id=1, source_target_pairs={{0,1},{1,0},{2,3},{3,2},{4,5},{5,4},{6,7},{7,6},{8,9},{9,8},{10,11... | collective-permute-start | bytes 159752 | tf_op jit(solution)/shard_map/ppermute | solution.py:79
  21.7 7.2 %collective-permute-start.5 = (f32[104,128]{1,0:T(8,128)S(1)}, f32[104,128]{1,0:T(8,128)S(1)}, u32[]{:S(2)}, u32[]{:S(2)}) collective-permute-start(f32[104,128]{1,0:T(8,128)S(1)} %get-tuple-element.52), channel_id=1, source_target_pairs={{1,2},{3,0},{2,1},{0,3},{5,6},{7,4},{6,5},{4,7},{9,10},{11,8},{10,... | collective-permute-start | bytes 159752 | tf_op jit(solution)/shard_map/ppermute | solution.py:79
  24.4 4.5 %collective-permute-start.6 = (f32[8,128]{1,0:T(8,128)S(1)}, f32[8,128]{1,0:T(8,128)S(1)}, u32[]{:S(2)}, u32[]{:S(2)}) collective-permute-start(f32[8,128]{1,0:T(8,128)S(1)} %get-tuple-element.49.parts), channel_id=1, source_target_pairs={{0,2},{1,3},{2,0},{3,1},{4,6},{5,7},{6,4},{7,5},{8,10},{9,11},{10,... | collective-permute-start | bytes 12296 | tf_op jit(solution)/shard_map/ppermute | solution.py:732
  40.2 1.8 collective-permute-start.7
  43.1 4.8 %collective-permute-start.8 = (f32[144,128]{1,0:T(8,128)S(1)}, f32[144,128]{1,0:T(8,128)S(1)}, u32[]{:S(2)}, u32[]{:S(2)}) collective-permute-start(f32[144,128]{1,0:T(8,128)S(1)} %get-tuple-element.60), channel_id=1, source_target_pairs={{0,4},{4,0},{8,12},{12,8},{1,5},{5,1},{9,13},{13,9},{2,6},{6,2},{1... | collective-permute-start | bytes 221192 | tf_op jit(solution)/shard_map/ppermute | solution.py:79
  43.6 6.3 %collective-permute-start.9 = (f32[144,128]{1,0:T(8,128)S(1)}, f32[144,128]{1,0:T(8,128)S(1)}, u32[]{:S(2)}, u32[]{:S(2)}) collective-permute-start(f32[144,128]{1,0:T(8,128)S(1)} %get-tuple-element.61), channel_id=1, source_target_pairs={{4,8},{12,0},{8,4},{0,12},{5,9},{13,1},{9,5},{1,13},{6,10},{14,2},... | collective-permute-start | bytes 221192 | tf_op jit(solution)/shard_map/ppermute | solution.py:79
  50.6 6.4 %collective-permute-start.10 = (f32[54,8,128]{2,1,0:T(8,128)S(1)}, f32[54,8,128]{2,1,0:T(8,128)S(1)}, u32[]{:S(2)}, u32[]{:S(2)}) collective-permute-start(f32[54,8,128]{2,1,0:T(8,128)S(1)} %get-tuple-element.62), channel_id=1, source_target_pairs={{0,1},{1,0},{2,3},{3,2},{4,5},{5,4},{6,7},{7,6},{8,9},{9,8},{10,11... | collective-permute-start | bytes 663560 | tf_op jit(solution)/shard_map/ppermute | solution.py:79
  52.0 7.9 %collective-permute-start.11 = (f32[54,8,128]{2,1,0:T(8,128)S(1)}, f32[54,8,128]{2,1,0:T(8,128)S(1)}, u32[]{:S(2)}, u32[]{:S(2)}) collective-permute-start(f32[54,8,128]{2,1,0:T(8,128)S(1)} %get-tuple-element.63), channel_id=1, source_target_pairs={{1,2},{2,1},{5,6},{6,5},{9,10},{10,9},{13,14},{14,13},{17,18},{18,... | collective-permute-start | bytes 663560 | tf_op jit(solution)/shard_map/ppermute | solution.py:79
  184.2 1.5 collective-permute-start.12
  186.9 6.3 %collective-permute-start.13 = (f32[104,128]{1,0:T(8,128)S(1)}, f32[104,128]{1,0:T(8,128)S(1)}, u32[]{:S(2)}, u32[]{:S(2)}) collective-permute-start(f32[104,128]{1,0:T(8,128)S(1)} %get-tuple-element.69), channel_id=1, source_target_pairs={{0,4},{4,0},{8,12},{12,8},{1,5},{5,1},{9,13},{13,9},{2,6},{6,2},{1... | collective-permute-start | bytes 159752 | tf_op jit(solution)/shard_map/ppermute | solution.py:79
  188.1 5.1 %collective-permute-start.14 = (f32[104,128]{1,0:T(8,128)S(1)}, f32[104,128]{1,0:T(8,128)S(1)}, u32[]{:S(2)}, u32[]{:S(2)}) collective-permute-start(f32[104,128]{1,0:T(8,128)S(1)} %get-tuple-element.70), channel_id=1, source_target_pairs={{4,8},{12,0},{8,4},{0,12},{5,9},{13,1},{9,5},{1,13},{6,10},{14,2},... | collective-permute-start | bytes 159752 | tf_op jit(solution)/shard_map/ppermute | solution.py:79
  189.4 3.8 %collective-permute-start.15 = (f32[8,128]{1,0:T(8,128)S(1)}, f32[8,128]{1,0:T(8,128)S(1)}, u32[]{:S(2)}, u32[]{:S(2)}) collective-permute-start(f32[8,128]{1,0:T(8,128)S(1)} %get-tuple-element.68.parts), channel_id=1, source_target_pairs={{0,8},{4,12},{8,0},{12,4},{1,9},{5,13},{9,1},{13,5},{2,10},{6,14},... | collective-permute-start | bytes 12296 | tf_op jit(solution)/shard_map/ppermute | solution.py:722
  193.8 6.6 %collective-permute-start.16 = (f32[104,128]{1,0:T(8,128)S(1)}, f32[104,128]{1,0:T(8,128)S(1)}, u32[]{:S(2)}, u32[]{:S(2)}) collective-permute-start(f32[104,128]{1,0:T(8,128)S(1)} %get-tuple-element.73), channel_id=1, source_target_pairs={{0,1},{1,0},{2,3},{3,2},{4,5},{5,4},{6,7},{7,6},{8,9},{9,8},{10,11... | collective-permute-start | bytes 159752 | tf_op jit(solution)/shard_map/ppermute | solution.py:79
  193.9 6.5 %collective-permute-start.17 = (f32[104,128]{1,0:T(8,128)S(1)}, f32[104,128]{1,0:T(8,128)S(1)}, u32[]{:S(2)}, u32[]{:S(2)}) collective-permute-start(f32[104,128]{1,0:T(8,128)S(1)} %get-tuple-element.74), channel_id=1, source_target_pairs={{1,2},{3,0},{2,1},{0,3},{5,6},{7,4},{6,5},{4,7},{9,10},{11,8},{10,... | collective-permute-start | bytes 159752 | tf_op jit(solution)/shard_map/ppermute | solution.py:79
  194.6 5.8 %collective-permute-start.18 = (f32[8,128]{1,0:T(8,128)S(1)}, f32[8,128]{1,0:T(8,128)S(1)}, u32[]{:S(2)}, u32[]{:S(2)}) collective-permute-start(f32[8,128]{1,0:T(8,128)S(1)} %get-tuple-element.71.parts), channel_id=1, source_target_pairs={{0,2},{1,3},{2,0},{3,1},{4,6},{5,7},{6,4},{7,5},{8,10},{9,11},{10,... | collective-permute-start | bytes 12296 | tf_op jit(solution)/shard_map/ppermute | solution.py:732
  211.7 1.8 collective-permute-start.19
  214.6 4.9 %collective-permute-start.20 = (f32[144,128]{1,0:T(8,128)S(1)}, f32[144,128]{1,0:T(8,128)S(1)}, u32[]{:S(2)}, u32[]{:S(2)}) collective-permute-start(f32[144,128]{1,0:T(8,128)S(1)} %get-tuple-element.82), channel_id=1, source_target_pairs={{0,4},{4,0},{8,12},{12,8},{1,5},{5,1},{9,13},{13,9},{2,6},{6,2},{1... | collective-permute-start | bytes 221192 | tf_op jit(solution)/shard_map/ppermute | solution.py:79
  215.6 5.4 %collective-permute-start.21 = (f32[144,128]{1,0:T(8,128)S(1)}, f32[144,128]{1,0:T(8,128)S(1)}, u32[]{:S(2)}, u32[]{:S(2)}) collective-permute-start(f32[144,128]{1,0:T(8,128)S(1)} %get-tuple-element.83), channel_id=1, source_target_pairs={{4,8},{12,0},{8,4},{0,12},{5,9},{13,1},{9,5},{1,13},{6,10},{14,2},... | collective-permute-start | bytes 221192 | tf_op jit(solution)/shard_map/ppermute | solution.py:79
  221.5 6.8 %collective-permute-start.22 = (f32[54,8,128]{2,1,0:T(8,128)S(1)}, f32[54,8,128]{2,1,0:T(8,128)S(1)}, u32[]{:S(2)}, u32[]{:S(2)}) collective-permute-start(f32[54,8,128]{2,1,0:T(8,128)S(1)} %get-tuple-element.84), channel_id=1, source_target_pairs={{0,1},{1,0},{2,3},{3,2},{4,5},{5,4},{6,7},{7,6},{8,9},{9,8},{10,11... | collective-permute-start | bytes 663560 | tf_op jit(solution)/shard_map/ppermute | solution.py:79
  223.1 8.4 %collective-permute-start.23 = (f32[54,8,128]{2,1,0:T(8,128)S(1)}, f32[54,8,128]{2,1,0:T(8,128)S(1)}, u32[]{:S(2)}, u32[]{:S(2)}) collective-permute-start(f32[54,8,128]{2,1,0:T(8,128)S(1)} %get-tuple-element.85), channel_id=1, source_target_pairs={{1,2},{2,1},{5,6},{6,5},{9,10},{10,9},{13,14},{14,13},{17,18},{18,... | collective-permute-start | bytes 663560 | tf_op jit(solution)/shard_map/ppermute | solution.py:79
  (2 other events, 2.0 us)

commit v3 on v2

--- a/solution.py
+++ b/solution.py
@@ -77,6 +77,18 @@
     def swap(self, sends, wide=False):
         perms = [self.first, self.inner] if wide else self.perms
         return [lax.ppermute(s, self.name, p) for s, p in zip(sends, perms)]
+
+
+def loop(count, step, unroll):
+    while count % unroll:
+        unroll -= 1
+
+    def turn(i, carry):
+        for j in range(unroll):
+            step(i * unroll + j)
+        return carry
+
+    lax.fori_loop(0, count // unroll, turn, 0)
 
 
 def roll_by(value, shift):
@@ -395,12 +407,11 @@
         total, mid = around(f, xe, r)
         return mid + rate * (total - 6.0 * mid)
 
-    def u_plane(k, carry):
+    def u_plane(k):
         for t in range(0, cells_z, 8):
             su[k, t : t + 8, :] = diffused(0, k + 1, ZO + t)
-        return carry
-
-    lax.fori_loop(0, cells_x + 2, u_plane, 0)
+
+    loop(cells_x + 2, u_plane, 3)
     su[0] = jnp.where(info[0] > 0, su[0], 0.0)
     su[cells_x + 1] = jnp.where(info[0] < ax.count - 1, su[cells_x + 1], 0.0)
     place = lane % slot
@@ -415,7 +426,7 @@
         total = total + roll(jnp.where(place == HA, inner, mid), -1, 1)
         svh[t : t + 8, :] = jnp.where(keep_y, mid + rate * (total - 6.0 * mid), 0.0)
 
-    def forced(x, carry):
+    def forced(x):
         xe = x + HA
         for t in range(0, cells_z, 8):
             push = force_ref[pl.ds(pl.multiple_of(x * cells_z + t, 8), 8), :]
@@ -438,11 +449,10 @@
             left = roll(jnp.where(lane == width - 1, far, v), 1, 1)
             right = roll(jnp.where(lane == 0, far, v), -1, 1)
             s6[x, t : t + 8, :] = right - left
-        return carry
-
-    lax.fori_loop(0, cells_x, forced, 0)
-
-    def first(x, carry):
+
+    loop(cells_x, forced, 2)
+
+    def first(x):
         for t in range(0, cells_z, 8):
             source = s6[x, t : t + 8, :] + (sw[x, t + 9 : t + 17, :] - sw[x, t + 7 : t + 15, :])
             source = source + (su[x + 2, t : t + 8, :] - su[x, t : t + 8, :])
@@ -450,9 +460,8 @@
             s6[x, t : t + 8, :] = source
             total, _ = around(3, x + HA, ZO + t)
             p1[x, t : t + 8, :] = total * (1.0 / 6.0) - source
-        return carry
-
-    lax.fori_loop(0, cells_x, first, 0)
+
+    loop(cells_x, first, 4)
     scale = 0.5 * TIME_STEP / 6.0
     edge[0] = scale * force_ref[:cells_z, :]
     edge[1] = scale * force_ref[(cells_x - 1) * cells_z :, :]
@@ -531,7 +540,9 @@
     if not last:
         parts, refs = refs[0], refs[1:]
         sends, refs = refs[: len(ax.perms)], refs[len(ax.perms) :]
-    pm, sm, ph, sh = refs
+    pms, pts = refs[:2], refs[2:4]
+    sm, st, ph, sh = refs[4:]
+    pm, pt = pms[0], pts[0]
     ext, cells_z, width = px.shape
     cells_x = press.shape[0]
     one_sided = ax.count == 2
@@ -540,26 +551,21 @@
     per = width // slot
     low, end = ZO - ZP, ZO + cells_z
     blank = jnp.zeros((end + 2 * ZP, width), F32)
-    for b in range(2):
-        pm[b, 0] = blank
-        pm[b, ext + 1] = blank
-        ph[b, 0] = blank
-        ph[b, npack + 1] = blank
+    for planes in pms + pts:
+        planes[0] = blank
+        planes[ext + 1] = blank
         for x in range(ext):
-            pm[b, x + 1, :low, :] = blank[:low]
-            pm[b, x + 1, end + ZP :, :] = blank[:low]
-        for g in range(npack):
-            ph[b, g + 1, :low, :] = blank[:low]
-            ph[b, g + 1, end + ZP :, :] = blank[:low]
+            planes[x + 1, :low, :] = blank[:low]
+            planes[x + 1, end + ZP :, :] = blank[:low]
 
     def z_tile(k):
         return from_sides(info[2], az.count, [r[k] for r in zr], 0.0)
 
     for x in range(ext):
         lower, upper = z_tile(x)
-        pm[0, x + 1, low:ZO, :] = lower
-        pm[0, x + 1, end : end + ZP, :] = upper
-        pm[0, x + 1, ZO:end, :] = px[x]
+        pm[x + 1, low:ZO, :] = lower
+        pm[x + 1, end : end + ZP, :] = upper
+        pm[x + 1, ZO:end, :] = px[x]
         lower, upper = z_tile(ext + x)
         sm[x, :ZP, :] = lower
         sm[x, ZP + cells_z :, :] = upper
@@ -573,84 +579,89 @@
         ):
             lower, upper = from_sides(info[1], ay.count, pieces, 0.0)
             one, two = split_edges(lower, upper, HB)
-            ph[0, i + 1, start:stop, :] = one
+            ph[i, start - low : stop - low, :] = one
             sh[i, start - low : stop - low, :] = two
 
+    for k in range(per):
+        for x in range(k, ext, per):
+            pt[x + 1, low : end + ZP, :] = roll(ph[x // per], -(slot * k + HB), 1)
+            st[x] = roll(sh[x // per], -(slot * k + HB), 1)
+
     lane = lanes_of((8, width))
-    place = lane % slot
-    keep_y = ((place >= HB) | (info[1] > 0)) & ((place < HB) | (info[1] < ay.count - 1))
+    keep_y = ((lane < HB) & (info[1] < ay.count - 1)) | ((lane >= width - HB) & (info[1] > 0))
     sixth = 1.0 / 6.0
     weight_y = jnp.where(keep_y, sixth, 0.0)
     first_lane, last_lane = lane == 0, lane == width - 1
 
-    def sweep(number, carry):
-        now, then = number % 2, 1 - number % 2
-
-        def group(g, carry):
-            scale = 1.0
-            if not one_sided:
-                outside = (g == 0) & (info[0] == 0)
-                outside |= (g == npack - 1) & (info[0] == ax.count - 1)
-                scale = jnp.where(outside, 0.0, 1.0)
-            for t in range(0, cells_z + 2 * ZP, 8):
-                r = low + t
-                weight = scale
-                if t < ZP:
-                    weight = weight * jnp.where(info[2] > 0, 1.0, 0.0)
-                elif t >= ZP + cells_z:
-                    weight = weight * jnp.where(info[2] < az.count - 1, 1.0, 0.0)
-                halo = ph[now, g + 1, r : r + 8, :]
-                edges = halo
-                for k in range(per):
-                    x = g * per + k
-                    mid = pm[now, x + 1, r : r + 8, :]
-                    far = roll(halo, -(slot * k + HB), 1)
-                    edges = jnp.where(lane // slot == k, roll(mid, slot * k + HB, 1), edges)
-                    total = pm[now, x, r : r + 8, :] + pm[now, x + 2, r : r + 8, :]
-                    total = total + (
-                        pm[now, x + 1, r - 1 : r + 7, :] + pm[now, x + 1, r + 1 : r + 9, :]
-                    )
-                    left = roll(jnp.where(last_lane, far, mid), 1, 1)
-                    right = roll(jnp.where(first_lane, far, mid), -1, 1)
-                    total = total + (left + right)
-                    pm[then, x + 1, r : r + 8, :] = (
-                        total * (sixth * weight) - sm[x, t : t + 8, :]
-                    )
-                total = ph[now, g + 1, r - 1 : r + 7, :] + ph[now, g + 1, r + 1 : r + 9, :]
-                total = total + roll(jnp.where(place == HB - 1, edges, halo), 1, 1)
-                total = total + roll(jnp.where(place == HB, edges, halo), -1, 1)
-                before = jnp.where(lane >= width - slot, ph[now, g, r : r + 8, :], halo)
-                after = jnp.where(lane < slot, ph[now, g + 2, r : r + 8, :], halo)
-                total = total + (roll(before, slot, 1) + roll(after, -slot, 1))
-                ph[then, g + 1, r : r + 8, :] = total * (weight_y * weight) - sh[g, t : t + 8, :]
+    def beside(m, h):
+        ml, mr, hl, hr = roll(m, 1, 1), roll(m, -1, 1), roll(h, 1, 1), roll(h, -1, 1)
+        return (
+            (jnp.where(first_lane, hl, ml), jnp.where(last_lane, hr, mr)),
+            (jnp.where(first_lane, ml, hl), jnp.where(last_lane, mr, hr)),
+        )
+
+    def sweep(number, now_m, then_m, now_t, then_t):
+        reach = SWEEPS - number
+        start = jnp.maximum(off - reach, 0) // 2
+        stop = (jnp.minimum(off + cells_x + reach, ext) + 1) // 2
+
+        def turn(q, carry):
+            for d in range(2):
+                x = 2 * q + d
+                scale = 1.0
+                if not one_sided:
+                    place = info[0] * cells_x + x - HB
+                    inside = (place >= 0) & (place < ax.count * cells_x)
+                    scale = jnp.where(inside, 1.0, 0.0)
+                for t in range(0, cells_z + 2 * ZP, 8):
+                    weight = scale
+                    if t < ZP:
+                        weight = weight * jnp.where(info[2] > 0, 1.0, 0.0)
+                    elif t >= ZP + cells_z:
+                        weight = weight * jnp.where(info[2] < az.count - 1, 1.0, 0.0)
+                    r = low + t
+                    sides = beside(now_m[x + 1, r : r + 8, :], now_t[x + 1, r : r + 8, :])
+                    for now, then, source, factor, (left, right) in (
+                        (now_m, then_m, sm, sixth * weight, sides[0]),
+                        (now_t, then_t, st, weight_y * weight, sides[1]),
+                    ):
+                        total = now[x, r : r + 8, :] + now[x + 2, r : r + 8, :]
+                        total = total + (
+                            now[x + 1, r - 1 : r + 7, :] + now[x + 1, r + 1 : r + 9, :]
+                        )
+                        total = total + (left + right)
+                        then[x + 1, r : r + 8, :] = total * factor - source[x, t : t + 8, :]
             return carry
 
-        return lax.fori_loop(0, npack, group, carry)
-
-    lax.fori_loop(0, SWEEPS - 1, sweep, 0)
-    done = (SWEEPS - 1) % 2
-    first_group = off // per
-
-    def gradient(q, carry):
-        g = first_group + q
-        for k in range(per):
-            x = q * per + k
-            at = g * per + k + 1
-            for t in range(0, cells_z, 8):
-                r = ZO + t
-                mid = pm[done, at, r : r + 8, :]
-                far = roll(ph[done, g + 1, r : r + 8, :], -(slot * k + HB), 1)
-                left = roll(jnp.where(last_lane, far, mid), 1, 1)
-                right = roll(jnp.where(first_lane, far, mid), -1, 1)
-                press[x, t : t + 8, :] = mid
-                gx = pm[done, at + 1, r : r + 8, :] - pm[done, at - 1, r : r + 8, :]
-                gz = pm[done, at, r + 1 : r + 9, :] - pm[done, at, r - 1 : r + 7, :]
-                vel[0, x, t : t + 8, :] = star[0, x, t : t + 8, :] - 0.5 * gx
-                vel[1, x, t : t + 8, :] = star[1, x, t : t + 8, :] - 0.5 * (right - left)
-                vel[2, x, t : t + 8, :] = star[2, x, t : t + 8, :] - 0.5 * gz
+        lax.fori_loop(start, stop, turn, 0)
+
+    def pair(number, carry):
+        sweep(2 * number + 1, pms[0], pms[1], pts[0], pts[1])
+        sweep(2 * number + 2, pms[1], pms[0], pts[1], pts[0])
         return carry
 
-    lax.fori_loop(0, cells_x // per, gradient, 0)
+    count = SWEEPS - 1
+    lax.fori_loop(0, count // 2, pair, 0)
+    if count % 2:
+        sweep(count, pms[0], pms[1], pts[0], pts[1])
+    pm, pt = pms[count % 2], pts[count % 2]
+
+    def gradient(x):
+        at = x + off + 1
+        for t in range(0, cells_z, 8):
+            r = ZO + t
+            mid = pm[at, r : r + 8, :]
+            far = pt[at, r : r + 8, :]
+            left = roll(jnp.where(last_lane, far, mid), 1, 1)
+            right = roll(jnp.where(first_lane, far, mid), -1, 1)
+            press[x, t : t + 8, :] = mid
+            gx = pm[at + 1, r : r + 8, :] - pm[at - 1, r : r + 8, :]
+            gz = pm[at, r + 1 : r + 9, :] - pm[at, r - 1 : r + 7, :]
+            vel[0, x, t : t + 8, :] = star[0, x, t : t + 8, :] - 0.5 * gx
+            vel[1, x, t : t + 8, :] = star[1, x, t : t + 8, :] - 0.5 * (right - left)
+            vel[2, x, t : t + 8, :] = star[2, x, t : t + 8, :] - 0.5 * gz
+
+    loop(cells_x, gradient, 4)
     if not last:
         column = lambda x: jnp.sum(vel[0, x], axis=0, keepdims=True)
         share = inflow_parts(info, column, inx[...], iny[...], turbines, cells_x, width)
@@ -775,9 +786,13 @@
             outs,
             [info, px, sx, star, inx, iny, *yr, *zr],
             scratch=[
-                vm(2, ext_b + 2, tall, width),
+                vm(ext_b + 2, tall, width),
+                vm(ext_b + 2, tall, width),
+                vm(ext_b + 2, tall, width),
+                vm(ext_b + 2, tall, width),
                 vm(ext_b, cells_z + 2 * ZP, width),
-                vm(2, pack_b + 2, tall, width),
+                vm(ext_b, cells_z + 2 * ZP, width),
+                vm(pack_b, cells_z + 2 * ZP, width),
                 vm(pack_b, cells_z + 2 * ZP, width),
             ],
             name="sweeps",

time: 358 us -> 123 us (0.34)
  Pallas kernels: 282 us -> 47.3 us
    pallas_call x14, Pallas kernels: 282 us -> 47.3 us  [call(): pl.pallas_call(kernel, out_shape=[jax.ShapeDtypeStruct(o, F32) for o in o...]
  transfers between devices with their start and end apart: 25 -> 25, of which waited for: 17 -> 17; matrix products, arithmetic and copies ran while one was open for 0% -> 0% of each run, Pallas kernels for 1% -> 3%
where the time goes in v3:
time: 123 us; the launch traced here: 122 us
  Pallas kernels  47.3 us (38%)
  starting transfers between devices  34.8 us (28%)
  waiting for transfers between devices  34.6 us (28%)
  local copies, waits for them, and re-layouts  3.76 us (3%)
  between operations  1.54 us (1%)
    pallas_call x14, Pallas kernels, call(): pl.pallas_call(kernel, out_shape=[jax.ShapeDtypeStruct(o, F32) for o in o...  47.3 us
    ppermute x20, waiting for transfers between devices, swap(): return [lax.ppermute(s, self.name, p) for s, p in zip(sends, perms)]  24.8 us
    ppermute x20, starting transfers between devices, swap(): return [lax.ppermute(s, self.name, p) for s, p in zip(sends, perms)]  22.5 us
    ppermute x2, waiting for transfers between devices, body(): cross = [lax.ppermute(parts, 'gz', az.cross)] if az.cross else []  5.41 us
    ppermute x2, starting transfers between devices, body(): cross = [lax.ppermute(parts, 'gz', az.cross)] if az.cross else []  4.93 us
    ppermute x2, waiting for transfers between devices, body(): cross = [lax.ppermute(parts, 'gy', ay.cross)] if ay.cross else []  4.46 us
    all_to_all x1, starting transfers between devices, body(): lax.all_to_all(packed.reshape(peers, block, width), ('gx', 'gy'), split_a...  4.32 us
    ppermute x2, starting transfers between devices, body(): cross = [lax.ppermute(parts, 'gy', ay.cross)] if ay.cross else []  2.97 us
  transfers between devices with their start and end apart: 25, of which 17 were waited for; matrix products, arithmetic and copies ran while one was open for 0% of the time, Pallas kernels for 3%

profile of v3, /device:TPU:12, one launch (start us, length us, event | category | flops | bytes accessed | tf_op | source)
XLA Modules:
  0.0 122.0 jit_solution(7658413185280004746)
XLA Ops:
  6.0 2.2 %pack_rows.1 = f32[576,128]{1,0:T(8,128)} custom-call(s32[4]{0:T(128)S(1)} %pad_add_fusion.info, f32[256,128]{1,0:T(8,128)S(1)} %copy-done.4, s32[256,1]{1,0:T(8,128)S(1)} %copy.12.owners, s32[1,256]{1,0:T(1,128)S(1)} %bitcast.14, s32[1,256]{1,0:T(1,128)S(1)} %bitcast.15), custom_call_target="tpu_custom_call" | custom-call | flops 429072 | bytes 429072 | tf_op jit(solution)/shard_map/pack_rows/pallas_call | solution.py:29
  8.2 4.3 %all-to-all-start = ((f32[8,72,128]{2,1,0:T(8,128)}), f32[8,72,128]{2,1,0:T(8,128)S(1)}, u32[]{:S(2)}, u32[]{:S(2)}) async-start(f32[8,72,128]{2,1,0:T(8,128)} %bitcast.8), calls=%async_computation | async-start | bytes 589824 | tf_op jit(solution)/shard_map/all_to_all | solution.py:708
  13.7 1.5 %collective-permute-start.1 = (f32[104,128]{1,0:T(8,128)S(1)}, f32[104,128]{1,0:T(8,128)S(1)}, u32[]{:S(2)}, u32[]{:S(2)}) collective-permute-start(f32[104,128]{1,0:T(8,128)S(1)} %get-tuple-element.47), channel_id=1, source_target_pairs={{0,4},{4,0},{8,12},{12,8},{1,5},{5,1},{9,13},{13,9},{2,6},{6,2},{1... | collective-permute-start | bytes 159752 | tf_op jit(solution)/shard_map/ppermute | solution.py:79
  15.3 1.9 %collective-permute-start.3 = (f32[8,128]{1,0:T(8,128)S(1)}, f32[8,128]{1,0:T(8,128)S(1)}, u32[]{:S(2)}, u32[]{:S(2)}) collective-permute-start(f32[8,128]{1,0:T(8,128)S(1)} %get-tuple-element.46.parts), channel_id=1, source_target_pairs={{0,8},{4,12},{8,0},{12,4},{1,9},{5,13},{9,1},{13,5},{2,10},{6,14},... | collective-permute-start | bytes 12296 | tf_op jit(solution)/shard_map/ppermute | solution.py:733
  17.3 1.7 %collective-permute-done.3.refs_3_ = f32[8,128]{1,0:T(8,128)S(1)} collective-permute-done((f32[8,128]{1,0:T(8,128)S(1)}, f32[8,128]{1,0:T(8,128)S(1)}, u32[]{:S(2)}, u32[]{:S(2)}) %collective-permute-start.3) | collective-permute-done | bytes 4128 | tf_op jit(solution)/shard_map/ppermute | solution.py:733
  21.7 2.7 %collective-permute-start.5 = (f32[104,128]{1,0:T(8,128)S(1)}, f32[104,128]{1,0:T(8,128)S(1)}, u32[]{:S(2)}, u32[]{:S(2)}) collective-permute-start(f32[104,128]{1,0:T(8,128)S(1)} %get-tuple-element.52), channel_id=1, source_target_pairs={{1,2},{3,0},{2,1},{0,3},{5,6},{7,4},{6,5},{4,7},{9,10},{11,8},{10,... | collective-permute-start | bytes 159752 | tf_op jit(solution)/shard_map/ppermute | solution.py:79
  25.6 3.3 %collective-permute-done.6.refs_5_ = f32[8,128]{1,0:T(8,128)S(1)} collective-permute-done((f32[8,128]{1,0:T(8,128)S(1)}, f32[8,128]{1,0:T(8,128)S(1)}, u32[]{:S(2)}, u32[]{:S(2)}) %collective-permute-start.6) | collective-permute-done | bytes 4128 | tf_op jit(solution)/shard_map/ppermute | solution.py:743
  28.9 6.3 %star.2 = (f32[3,16,48,128]{3,2,1,0:T(8,128)S(1)}, f32[16,48,128]{2,1,0:T(8,128)S(1)}, f32[16,48,128]{2,1,0:T(8,128)S(1)}, f32[2,48,128]{2,1,0:T(8,128)S(1)}, f32[17,48,128]{2,1,0:T(8,128)S(1)}) custom-call(s32[4]{0:T(128)S(1)} %pad_add_fusion.info, f32[3,16,48,128]{3,2,1,0:T(8,128)S(1)} %copy-done.1, f32[16,48,128]{2,1,0:T(8,128)S(1)} %copy-done.3, ...), custom_call_target="tpu_custom_call" | custom-call | flops 4747792 | bytes 4747792 | tf_op jit(solution)/shard_map/star/pallas_call | solution.py:29
  35.3 1.7 %collective-permute-done.7.refs_0_ = f32[17,48,128]{2,1,0:T(8,128)S(1)} collective-permute-done((f32[17,48,128]{2,1,0:T(8,128)S(1)}, f32[17,48,128]{2,1,0:T(8,128)S(1)}, u32[]{:S(2)}, u32[]{:S(2)}) %collective-permute-start.7) | collective-permute-done | bytes 417824 | tf_op jit(solution)/shard_map/ppermute | solution.py:79
  38.6 2.5 %collective-permute-start.9 = (f32[144,128]{1,0:T(8,128)S(1)}, f32[144,128]{1,0:T(8,128)S(1)}, u32[]{:S(2)}, u32[]{:S(2)}) collective-permute-start(f32[144,128]{1,0:T(8,128)S(1)} %get-tuple-element.61), channel_id=1, source_target_pairs={{4,8},{12,0},{8,4},{0,12},{5,9},{13,1},{9,5},{1,13},{6,10},{14,2},... | collective-permute-start | bytes 221192 | tf_op jit(solution)/shard_map/ppermute | solution.py:79
  41.1 1.8 %collective-permute-done.8.refs_0_ = f32[144,128]{1,0:T(8,128)S(1)} collective-permute-done((f32[144,128]{1,0:T(8,128)S(1)}, f32[144,128]{1,0:T(8,128)S(1)}, u32[]{:S(2)}, u32[]{:S(2)}) %collective-permute-start.8) | collective-permute-done | bytes 73760 | tf_op jit(solution)/shard_map/ppermute | solution.py:79
  42.9 2.1 %collective-permute-done.9.refs_1_ = f32[144,128]{1,0:T(8,128)S(1)} collective-permute-done((f32[144,128]{1,0:T(8,128)S(1)}, f32[144,128]{1,0:T(8,128)S(1)}, u32[]{:S(2)}, u32[]{:S(2)}) %collective-permute-start.9) | collective-permute-done | bytes 73760 | tf_op jit(solution)/shard_map/ppermute | solution.py:79
  45.6 1.4 %collective-permute-start.10 = (f32[54,8,128]{2,1,0:T(8,128)S(1)}, f32[54,8,128]{2,1,0:T(8,128)S(1)}, u32[]{:S(2)}, u32[]{:S(2)}) collective-permute-start(f32[54,8,128]{2,1,0:T(8,128)S(1)} %get-tuple-element.62), channel_id=1, source_target_pairs={{0,1},{1,0},{2,3},{3,2},{4,5},{5,4},{6,7},{7,6},{8,9},{9,8},{10,11... | collective-permute-start | bytes 663560 | tf_op jit(solution)/shard_map/ppermute | solution.py:79
  47.0 2.5 %collective-permute-start.11 = (f32[54,8,128]{2,1,0:T(8,128)S(1)}, f32[54,8,128]{2,1,0:T(8,128)S(1)}, u32[]{:S(2)}, u32[]{:S(2)}) collective-permute-start(f32[54,8,128]{2,1,0:T(8,128)S(1)} %get-tuple-element.63), channel_id=1, source_target_pairs={{1,2},{2,1},{5,6},{6,5},{9,10},{10,9},{13,14},{14,13},{17,18},{18,... | collective-permute-start | bytes 663560 | tf_op jit(solution)/shard_map/ppermute | solution.py:79
  49.5 2.5 %collective-permute-done.10.refs_2_ = f32[54,8,128]{2,1,0:T(8,128)S(1)} collective-permute-done((f32[54,8,128]{2,1,0:T(8,128)S(1)}, f32[54,8,128]{2,1,0:T(8,128)S(1)}, u32[]{:S(2)}, u32[]{:S(2)}) %collective-permute-start.10) | collective-permute-done | bytes 221216 | tf_op jit(solution)/shard_map/ppermute | solution.py:79
  52.0 2.9 %collective-permute-done.11.refs_3_ = f32[54,8,128]{2,1,0:T(8,128)S(1)} collective-permute-done((f32[54,8,128]{2,1,0:T(8,128)S(1)}, f32[54,8,128]{2,1,0:T(8,128)S(1)}, u32[]{:S(2)}, u32[]{:S(2)}) %collective-permute-start.11) | collective-permute-done | bytes 221216 | tf_op jit(solution)/shard_map/ppermute | solution.py:79
  54.9 12.0 %sweeps.2 = (f32[3,16,48,128]{3,2,1,0:T(8,128)S(1)}, f32[16,48,128]{2,1,0:T(8,128)S(1)}, f32[8,128]{1,0:T(8,128)S(1)}, f32[392,128]{1,0:T(8,128)S(1)}) custom-call(s32[4]{0:T(128)S(1)} %pad_add_fusion.info, f32[24,48,128]{2,1,0:T(8,128)S(1)} %get-tuple-element.57.px, f32[24,48,128]{2,1,0:T(8,128)S(1)} %get-tuple-element.58.sx, ...), custom_call_target="tpu_custom_call" | custom-call | flops 4727824 | bytes 4727824 | tf_op jit(solution)/shard_map/sweeps/pallas_call | solution.py:29
  66.9 1.4 %collective-permute-done.12.refs_0_ = f32[392,128]{1,0:T(8,128)S(1)} collective-permute-done((f32[392,128]{1,0:T(8,128)S(1)}, f32[392,128]{1,0:T(8,128)S(1)}, u32[]{:S(2)}, u32[]{:S(2)}) %collective-permute-start.12) | collective-permute-done | bytes 200736 | tf_op jit(solution)/shard_map/ppermute | solution.py:79
  70.8 1.3 %collective-permute-start.14 = (f32[104,128]{1,0:T(8,128)S(1)}, f32[104,128]{1,0:T(8,128)S(1)}, u32[]{:S(2)}, u32[]{:S(2)}) collective-permute-start(f32[104,128]{1,0:T(8,128)S(1)} %get-tuple-element.70), channel_id=1, source_target_pairs={{4,8},{12,0},{8,4},{0,12},{5,9},{13,1},{9,5},{1,13},{6,10},{14,2},... | collective-permute-start | bytes 159752 | tf_op jit(solution)/shard_map/ppermute | solution.py:79
  73.1 2.8 %collective-permute-done.15.refs_3_ = f32[8,128]{1,0:T(8,128)S(1)} collective-permute-done((f32[8,128]{1,0:T(8,128)S(1)}, f32[8,128]{1,0:T(8,128)S(1)}, u32[]{:S(2)}, u32[]{:S(2)}) %collective-permute-start.15) | collective-permute-done | bytes 4128 | tf_op jit(solution)/shard_map/ppermute | solution.py:733
  77.3 3.7 %collective-permute-start.18 = (f32[8,128]{1,0:T(8,128)S(1)}, f32[8,128]{1,0:T(8,128)S(1)}, u32[]{:S(2)}, u32[]{:S(2)}) collective-permute-start(f32[8,128]{1,0:T(8,128)S(1)} %get-tuple-element.71.parts), channel_id=1, source_target_pairs={{0,2},{1,3},{2,0},{3,1},{4,6},{5,7},{6,4},{7,5},{8,10},{9,11},{10,... | collective-permute-start | bytes 12296 | tf_op jit(solution)/shard_map/ppermute | solution.py:743
  81.0 2.2 %collective-permute-done.18.refs_5_ = f32[8,128]{1,0:T(8,128)S(1)} collective-permute-done((f32[8,128]{1,0:T(8,128)S(1)}, f32[8,128]{1,0:T(8,128)S(1)}, u32[]{:S(2)}, u32[]{:S(2)}) %collective-permute-start.18) | collective-permute-done | bytes 4128 | tf_op jit(solution)/shard_map/ppermute | solution.py:743
  83.1 6.3 %star.3 = (f32[3,16,48,128]{3,2,1,0:T(8,128)S(1)}, f32[16,48,128]{2,1,0:T(8,128)S(1)}, f32[16,48,128]{2,1,0:T(8,128)S(1)}, f32[2,48,128]{2,1,0:T(8,128)S(1)}, f32[17,48,128]{2,1,0:T(8,128)S(1)}) custom-call(s32[4]{0:T(128)S(1)} %pad_add_fusion.info, f32[3,16,48,128]{3,2,1,0:T(8,128)S(1)} %get-tuple-element.64.vel, ...), custom_call_target="tpu_custom_call" | custom-call | flops 4747792 | bytes 4747792 | tf_op jit(solution)/shard_map/star/pallas_call | solution.py:29
  89.5 1.7 %collective-permute-done.19.refs_0_ = f32[17,48,128]{2,1,0:T(8,128)S(1)} collective-permute-done((f32[17,48,128]{2,1,0:T(8,128)S(1)}, f32[17,48,128]{2,1,0:T(8,128)S(1)}, u32[]{:S(2)}, u32[]{:S(2)}) %collective-permute-start.19) | collective-permute-done | bytes 417824 | tf_op jit(solution)/shard_map/ppermute | solution.py:79
  93.3 1.5 %collective-permute-start.21 = (f32[144,128]{1,0:T(8,128)S(1)}, f32[144,128]{1,0:T(8,128)S(1)}, u32[]{:S(2)}, u32[]{:S(2)}) collective-permute-start(f32[144,128]{1,0:T(8,128)S(1)} %get-tuple-element.83), channel_id=1, source_target_pairs={{4,8},{12,0},{8,4},{0,12},{5,9},{13,1},{9,5},{1,13},{6,10},{14,2},... | collective-permute-start | bytes 221192 | tf_op jit(solution)/shard_map/ppermute | solution.py:79
  94.7 2.5 %collective-permute-done.20.refs_0_ = f32[144,128]{1,0:T(8,128)S(1)} collective-permute-done((f32[144,128]{1,0:T(8,128)S(1)}, f32[144,128]{1,0:T(8,128)S(1)}, u32[]{:S(2)}, u32[]{:S(2)}) %collective-permute-start.20) | collective-permute-done | bytes 73760 | tf_op jit(solution)/shard_map/ppermute | solution.py:79
  97.2 1.4 %collective-permute-done.21.refs_1_ = f32[144,128]{1,0:T(8,128)S(1)} collective-permute-done((f32[144,128]{1,0:T(8,128)S(1)}, f32[144,128]{1,0:T(8,128)S(1)}, u32[]{:S(2)}, u32[]{:S(2)}) %collective-permute-start.21) | collective-permute-done | bytes 73760 | tf_op jit(solution)/shard_map/ppermute | solution.py:79
  99.2 1.6 %collective-permute-start.22 = (f32[54,8,128]{2,1,0:T(8,128)S(1)}, f32[54,8,128]{2,1,0:T(8,128)S(1)}, u32[]{:S(2)}, u32[]{:S(2)}) collective-permute-start(f32[54,8,128]{2,1,0:T(8,128)S(1)} %get-tuple-element.84), channel_id=1, source_target_pairs={{0,1},{1,0},{2,3},{3,2},{4,5},{5,4},{6,7},{7,6},{8,9},{9,8},{10,11... | collective-permute-start | bytes 663560 | tf_op jit(solution)/shard_map/ppermute | solution.py:79
  100.8 3.3 %collective-permute-start.23 = (f32[54,8,128]{2,1,0:T(8,128)S(1)}, f32[54,8,128]{2,1,0:T(8,128)S(1)}, u32[]{:S(2)}, u32[]{:S(2)}) collective-permute-start(f32[54,8,128]{2,1,0:T(8,128)S(1)} %get-tuple-element.85), channel_id=1, source_target_pairs={{1,2},{2,1},{5,6},{6,5},{9,10},{10,9},{13,14},{14,13},{17,18},{18,... | collective-permute-start | bytes 663560 | tf_op jit(solution)/shard_map/ppermute | solution.py:79
  104.1 1.9 %collective-permute-done.22.refs_2_ = f32[54,8,128]{2,1,0:T(8,128)S(1)} collective-permute-done((f32[54,8,128]{2,1,0:T(8,128)S(1)}, f32[54,8,128]{2,1,0:T(8,128)S(1)}, u32[]{:S(2)}, u32[]{:S(2)}) %collective-permute-start.22) | collective-permute-done | bytes 221216 | tf_op jit(solution)/shard_map/ppermute | solution.py:79
  106.1 3.1 %collective-permute-done.23.refs_3_ = f32[54,8,128]{2,1,0:T(8,128)S(1)} collective-permute-done((f32[54,8,128]{2,1,0:T(8,128)S(1)}, f32[54,8,128]{2,1,0:T(8,128)S(1)}, u32[]{:S(2)}, u32[]{:S(2)}) %collective-permute-start.23) | collective-permute-done | bytes 221216 | tf_op jit(solution)/shard_map/ppermute | solution.py:79
  109.2 12.8 %sweeps.3 = (f32[3,16,48,128]{3,2,1,0:T(8,128)}, f32[16,48,128]{2,1,0:T(8,128)}) custom-call(s32[4]{0:T(128)S(1)} %pad_add_fusion.info, f32[24,48,128]{2,1,0:T(8,128)S(1)} %get-tuple-element.79.px, f32[24,48,128]{2,1,0:T(8,128)S(1)} %get-tuple-element.80.sx, f32[3,16,48,128]{3,2,1,0:T(8,128)S(1)} %get-tuple-element.81.star, s32[1,128]{1,0:T(1,128)S(1)} %pad.11.inx, ...), custom_call_target="tpu_custom_call" | custom-call | flops 4523024 | bytes 4523024 | tf_op jit(solution)/shard_map/sweeps/pallas_call | solution.py:29
  (55 shorter events, 19.7 us)
Async XLA Ops:
  0.6 5.2 %copy-start.7 = (s32[256,1]{0,1:T(1,128)S(1)}, s32[256,1]{0,1:T(1,128)}, u32[]{:S(2)}) copy-start(s32[256,1]{0,1:T(1,128)} %param.13) | copy-start | bytes 3076
  0.6 5.3 %copy-start.6 = (s32[256]{0:T(256)S(1)}, s32[256]{0:T(256)}, u32[]{:S(2)}) copy-start(s32[256]{0:T(256)} %param.15) | copy-start | bytes 3076
  0.7 5.3 %copy-start.5 = (s32[256]{0:T(256)S(1)}, s32[256]{0:T(256)}, u32[]{:S(2)}) copy-start(s32[256]{0:T(256)} %param.14) | copy-start | bytes 3076
  2.7 1.3 %copy-start = (f32[3,16,48,128]{3,2,1,0:T(8,128)S(1)}, f32[3,16,48,128]{3,2,1,0:T(8,128)}, u32[]{:S(2)}) copy-start(f32[3,16,48,128]{3,2,1,0:T(8,128)} %vel.7) | copy-start | bytes 3538948
  5.0 7.5 %copy-start.1 = (f32[3,16,48,128]{3,2,1,0:T(8,128)S(1)}, f32[3,16,48,128]{3,2,1,0:T(8,128)}, u32[]{:S(2)}) copy-start(f32[3,16,48,128]{3,2,1,0:T(8,128)} %vel.7) | copy-start | bytes 3538948
  5.0 7.5 %copy-start.3 = (f32[16,48,128]{2,1,0:T(8,128)S(1)}, f32[16,48,128]{2,1,0:T(8,128)}, u32[]{:S(2)}) copy-start(f32[16,48,128]{2,1,0:T(8,128)} %press.7) | copy-start | bytes 1179652
  5.7 6.7 %collective-permute-start = (f32[392,128]{1,0:T(8,128)S(1)}, f32[392,128]{1,0:T(8,128)S(1)}, u32[]{:S(2)}, u32[]{:S(2)}) collective-permute-start(f32[392,128]{1,0:T(8,128)S(1)} %get-tuple-element.45), channel_id=1, source_target_pairs={{0,16},{16,0},{1,17},{17,1},{2,18},{18,2},{3,19},{19,3},{4,20},{20... | collective-permute-start | bytes 602120 | tf_op jit(solution)/shard_map/ppermute | solution.py:79
  8.2 17.5 %all-to-all-start = ((f32[8,72,128]{2,1,0:T(8,128)}), f32[8,72,128]{2,1,0:T(8,128)S(1)}, u32[]{:S(2)}, u32[]{:S(2)}) async-start(f32[8,72,128]{2,1,0:T(8,128)} %bitcast.8), calls=%async_computation | async-start | bytes 589824 | tf_op jit(solution)/shard_map/all_to_all | solution.py:708
  13.7 11.9 %copy-start.8 = (f32[48]{0:T(128)S(1)}, f32[48]{0:T(128)}, u32[]{:S(2)}) copy-start(f32[48]{0:T(128)} %param.17) | copy-start | bytes 580
  13.7 6.3 %collective-permute-start.1 = (f32[104,128]{1,0:T(8,128)S(1)}, f32[104,128]{1,0:T(8,128)S(1)}, u32[]{:S(2)}, u32[]{:S(2)}) collective-permute-start(f32[104,128]{1,0:T(8,128)S(1)} %get-tuple-element.47), channel_id=1, source_target_pairs={{0,4},{4,0},{8,12},{12,8},{1,5},{5,1},{9,13},{13,9},{2,6},{6,2},{1... | collective-permute-start | bytes 159752 | tf_op jit(solution)/shard_map/ppermute | solution.py:79
  15.2 5.3 %collective-permute-start.2 = (f32[104,128]{1,0:T(8,128)S(1)}, f32[104,128]{1,0:T(8,128)S(1)}, u32[]{:S(2)}, u32[]{:S(2)}) collective-permute-start(f32[104,128]{1,0:T(8,128)S(1)} %get-tuple-element.48), channel_id=1, source_target_pairs={{4,8},{12,0},{8,4},{0,12},{5,9},{13,1},{9,5},{1,13},{6,10},{14,2},... | collective-permute-start | bytes 159752 | tf_op jit(solution)/shard_map/ppermute | solution.py:79
  15.3 3.6 %collective-permute-start.3 = (f32[8,128]{1,0:T(8,128)S(1)}, f32[8,128]{1,0:T(8,128)S(1)}, u32[]{:S(2)}, u32[]{:S(2)}) collective-permute-start(f32[8,128]{1,0:T(8,128)S(1)} %get-tuple-element.46.parts), channel_id=1, source_target_pairs={{0,8},{4,12},{8,0},{12,4},{1,9},{5,13},{9,1},{13,5},{2,10},{6,14},... | collective-permute-start | bytes 12296 | tf_op jit(solution)/shard_map/ppermute | solution.py:733
  21.2 7.7 %collective-permute-start.4 = (f32[104,128]{1,0:T(8,128)S(1)}, f32[104,128]{1,0:T(8,128)S(1)}, u32[]{:S(2)}, u32[]{:S(2)}) collective-permute-start(f32[104,128]{1,0:T(8,128)S(1)} %get-tuple-element.51), channel_id=1, source_target_pairs={{0,1},{1,0},{2,3},{3,2},{4,5},{5,4},{6,7},{7,6},{8,9},{9,8},{10,11... | collective-permute-start | bytes 159752 | tf_op jit(solution)/shard_map/ppermute | solution.py:79
  21.7 7.2 %collective-permute-start.5 = (f32[104,128]{1,0:T(8,128)S(1)}, f32[104,128]{1,0:T(8,128)S(1)}, u32[]{:S(2)}, u32[]{:S(2)}) collective-permute-start(f32[104,128]{1,0:T(8,128)S(1)} %get-tuple-element.52), channel_id=1, source_target_pairs={{1,2},{3,0},{2,1},{0,3},{5,6},{7,4},{6,5},{4,7},{9,10},{11,8},{10,... | collective-permute-start | bytes 159752 | tf_op jit(solution)/shard_map/ppermute | solution.py:79
  24.4 4.5 %collective-permute-start.6 = (f32[8,128]{1,0:T(8,128)S(1)}, f32[8,128]{1,0:T(8,128)S(1)}, u32[]{:S(2)}, u32[]{:S(2)}) collective-permute-start(f32[8,128]{1,0:T(8,128)S(1)} %get-tuple-element.49.parts), channel_id=1, source_target_pairs={{0,2},{1,3},{2,0},{3,1},{4,6},{5,7},{6,4},{7,5},{8,10},{9,11},{10,... | collective-permute-start | bytes 12296 | tf_op jit(solution)/shard_map/ppermute | solution.py:743
  35.2 1.8 %collective-permute-start.7 = (f32[17,48,128]{2,1,0:T(8,128)S(1)}, f32[17,48,128]{2,1,0:T(8,128)S(1)}, u32[]{:S(2)}, u32[]{:S(2)}) collective-permute-start(f32[17,48,128]{2,1,0:T(8,128)S(1)} %get-tuple-element.56), channel_id=1, source_target_pairs={{0,16},{16,0},{1,17},{17,1},{2,18},{18,2},{3,19},{19,3},{4,20},{20... | collective-permute-start | bytes 1253384 | tf_op jit(solution)/shard_map/ppermute | solution.py:79
  38.1 4.8 %collective-permute-start.8 = (f32[144,128]{1,0:T(8,128)S(1)}, f32[144,128]{1,0:T(8,128)S(1)}, u32[]{:S(2)}, u32[]{:S(2)}) collective-permute-start(f32[144,128]{1,0:T(8,128)S(1)} %get-tuple-element.60), channel_id=1, source_target_pairs={{0,4},{4,0},{8,12},{12,8},{1,5},{5,1},{9,13},{13,9},{2,6},{6,2},{1... | collective-permute-start | bytes 221192 | tf_op jit(solution)/shard_map/ppermute | solution.py:79
  38.6 6.3 %collective-permute-start.9 = (f32[144,128]{1,0:T(8,128)S(1)}, f32[144,128]{1,0:T(8,128)S(1)}, u32[]{:S(2)}, u32[]{:S(2)}) collective-permute-start(f32[144,128]{1,0:T(8,128)S(1)} %get-tuple-element.61), channel_id=1, source_target_pairs={{4,8},{12,0},{8,4},{0,12},{5,9},{13,1},{9,5},{1,13},{6,10},{14,2},... | collective-permute-start | bytes 221192 | tf_op jit(solution)/shard_map/ppermute | solution.py:79
  45.6 6.4 %collective-permute-start.10 = (f32[54,8,128]{2,1,0:T(8,128)S(1)}, f32[54,8,128]{2,1,0:T(8,128)S(1)}, u32[]{:S(2)}, u32[]{:S(2)}) collective-permute-start(f32[54,8,128]{2,1,0:T(8,128)S(1)} %get-tuple-element.62), channel_id=1, source_target_pairs={{0,1},{1,0},{2,3},{3,2},{4,5},{5,4},{6,7},{7,6},{8,9},{9,8},{10,11... | collective-permute-start | bytes 663560 | tf_op jit(solution)/shard_map/ppermute | solution.py:79
  47.0 7.9 %collective-permute-start.11 = (f32[54,8,128]{2,1,0:T(8,128)S(1)}, f32[54,8,128]{2,1,0:T(8,128)S(1)}, u32[]{:S(2)}, u32[]{:S(2)}) collective-permute-start(f32[54,8,128]{2,1,0:T(8,128)S(1)} %get-tuple-element.63), channel_id=1, source_target_pairs={{1,2},{2,1},{5,6},{6,5},{9,10},{10,9},{13,14},{14,13},{17,18},{18,... | collective-permute-start | bytes 663560 | tf_op jit(solution)/shard_map/ppermute | solution.py:79
  66.9 1.5 %collective-permute-start.12 = (f32[392,128]{1,0:T(8,128)S(1)}, f32[392,128]{1,0:T(8,128)S(1)}, u32[]{:S(2)}, u32[]{:S(2)}) collective-permute-start(f32[392,128]{1,0:T(8,128)S(1)} %get-tuple-element.67), channel_id=1, source_target_pairs={{0,16},{16,0},{1,17},{17,1},{2,18},{18,2},{3,19},{19,3},{4,20},{20... | collective-permute-start | bytes 602120 | tf_op jit(solution)/shard_map/ppermute | solution.py:79
  69.6 6.3 %collective-permute-start.13 = (f32[104,128]{1,0:T(8,128)S(1)}, f32[104,128]{1,0:T(8,128)S(1)}, u32[]{:S(2)}, u32[]{:S(2)}) collective-permute-start(f32[104,128]{1,0:T(8,128)S(1)} %get-tuple-element.69), channel_id=1, source_target_pairs={{0,4},{4,0},{8,12},{12,8},{1,5},{5,1},{9,13},{13,9},{2,6},{6,2},{1... | collective-permute-start | bytes 159752 | tf_op jit(solution)/shard_map/ppermute | solution.py:79
  70.8 5.1 %collective-permute-start.14 = (f32[104,128]{1,0:T(8,128)S(1)}, f32[104,128]{1,0:T(8,128)S(1)}, u32[]{:S(2)}, u32[]{:S(2)}) collective-permute-start(f32[104,128]{1,0:T(8,128)S(1)} %get-tuple-element.70), channel_id=1, source_target_pairs={{4,8},{12,0},{8,4},{0,12},{5,9},{13,1},{9,5},{1,13},{6,10},{14,2},... | collective-permute-start | bytes 159752 | tf_op jit(solution)/shard_map/ppermute | solution.py:79
  72.1 3.8 %collective-permute-start.15 = (f32[8,128]{1,0:T(8,128)S(1)}, f32[8,128]{1,0:T(8,128)S(1)}, u32[]{:S(2)}, u32[]{:S(2)}) collective-permute-start(f32[8,128]{1,0:T(8,128)S(1)} %get-tuple-element.68.parts), channel_id=1, source_target_pairs={{0,8},{4,12},{8,0},{12,4},{1,9},{5,13},{9,1},{13,5},{2,10},{6,14},... | collective-permute-start | bytes 12296 | tf_op jit(solution)/shard_map/ppermute | solution.py:733
  76.5 6.6 %collective-permute-start.16 = (f32[104,128]{1,0:T(8,128)S(1)}, f32[104,128]{1,0:T(8,128)S(1)}, u32[]{:S(2)}, u32[]{:S(2)}) collective-permute-start(f32[104,128]{1,0:T(8,128)S(1)} %get-tuple-element.73), channel_id=1, source_target_pairs={{0,1},{1,0},{2,3},{3,2},{4,5},{5,4},{6,7},{7,6},{8,9},{9,8},{10,11... | collective-permute-start | bytes 159752 | tf_op jit(solution)/shard_map/ppermute | solution.py:79
  76.6 6.5 %collective-permute-start.17 = (f32[104,128]{1,0:T(8,128)S(1)}, f32[104,128]{1,0:T(8,128)S(1)}, u32[]{:S(2)}, u32[]{:S(2)}) collective-permute-start(f32[104,128]{1,0:T(8,128)S(1)} %get-tuple-element.74), channel_id=1, source_target_pairs={{1,2},{3,0},{2,1},{0,3},{5,6},{7,4},{6,5},{4,7},{9,10},{11,8},{10,... | collective-permute-start | bytes 159752 | tf_op jit(solution)/shard_map/ppermute | solution.py:79
  77.3 5.8 %collective-permute-start.18 = (f32[8,128]{1,0:T(8,128)S(1)}, f32[8,128]{1,0:T(8,128)S(1)}, u32[]{:S(2)}, u32[]{:S(2)}) collective-permute-start(f32[8,128]{1,0:T(8,128)S(1)} %get-tuple-element.71.parts), channel_id=1, source_target_pairs={{0,2},{1,3},{2,0},{3,1},{4,6},{5,7},{6,4},{7,5},{8,10},{9,11},{10,... | collective-permute-start | bytes 12296 | tf_op jit(solution)/shard_map/ppermute | solution.py:743
  89.4 1.8 %collective-permute-start.19 = (f32[17,48,128]{2,1,0:T(8,128)S(1)}, f32[17,48,128]{2,1,0:T(8,128)S(1)}, u32[]{:S(2)}, u32[]{:S(2)}) collective-permute-start(f32[17,48,128]{2,1,0:T(8,128)S(1)} %get-tuple-element.78), channel_id=1, source_target_pairs={{0,16},{16,0},{1,17},{17,1},{2,18},{18,2},{3,19},{19,3},{4,20},{20... | collective-permute-start | bytes 1253384 | tf_op jit(solution)/shard_map/ppermute | solution.py:79
  92.4 4.9 %collective-permute-start.20 = (f32[144,128]{1,0:T(8,128)S(1)}, f32[144,128]{1,0:T(8,128)S(1)}, u32[]{:S(2)}, u32[]{:S(2)}) collective-permute-start(f32[144,128]{1,0:T(8,128)S(1)} %get-tuple-element.82), channel_id=1, source_target_pairs={{0,4},{4,0},{8,12},{12,8},{1,5},{5,1},{9,13},{13,9},{2,6},{6,2},{1... | collective-permute-start | bytes 221192 | tf_op jit(solution)/shard_map/ppermute | solution.py:79
  93.3 5.4 %collective-permute-start.21 = (f32[144,128]{1,0:T(8,128)S(1)}, f32[144,128]{1,0:T(8,128)S(1)}, u32[]{:S(2)}, u32[]{:S(2)}) collective-permute-start(f32[144,128]{1,0:T(8,128)S(1)} %get-tuple-element.83), channel_id=1, source_target_pairs={{4,8},{12,0},{8,4},{0,12},{5,9},{13,1},{9,5},{1,13},{6,10},{14,2},... | collective-permute-start | bytes 221192 | tf_op jit(solution)/shard_map/ppermute | solution.py:79
  99.2 6.8 %collective-permute-start.22 = (f32[54,8,128]{2,1,0:T(8,128)S(1)}, f32[54,8,128]{2,1,0:T(8,128)S(1)}, u32[]{:S(2)}, u32[]{:S(2)}) collective-permute-start(f32[54,8,128]{2,1,0:T(8,128)S(1)} %get-tuple-element.84), channel_id=1, source_target_pairs={{0,1},{1,0},{2,3},{3,2},{4,5},{5,4},{6,7},{7,6},{8,9},{9,8},{10,11... | collective-permute-start | bytes 663560 | tf_op jit(solution)/shard_map/ppermute | solution.py:79
  100.8 8.4 %collective-permute-start.23 = (f32[54,8,128]{2,1,0:T(8,128)S(1)}, f32[54,8,128]{2,1,0:T(8,128)S(1)}, u32[]{:S(2)}, u32[]{:S(2)}) collective-permute-start(f32[54,8,128]{2,1,0:T(8,128)S(1)} %get-tuple-element.85), channel_id=1, source_target_pairs={{1,2},{2,1},{5,6},{6,5},{9,10},{10,9},{13,14},{14,13},{17,18},{18,... | collective-permute-start | bytes 663560 | tf_op jit(solution)/shard_map/ppermute | solution.py:79
  (2 other events, 2.0 us)

commit v4 on v3

--- a/solution.py
+++ b/solution.py
@@ -7,6 +7,7 @@
 from jax.experimental import pallas as pl
 from jax.experimental.pallas import tpu as pltpu
 from jax.sharding import PartitionSpec as P
+
 
 BAND = 32
 STEPS = 2
@@ -21,7 +22,7 @@
 BF16 = jnp.bfloat16
 
 
-def call(kernel, outs, args, smem=(0,), scratch=(), name=None):
+def call(kernel, outs, args, smem=(0,), scratch=()):
     specs = [
         pl.BlockSpec(memory_space=pltpu.SMEM if i in smem else pltpu.VMEM) for i in range(len(args))
     ]
@@ -32,7 +33,6 @@
         in_specs=specs,
         out_specs=[pl.BlockSpec(memory_space=pltpu.VMEM)] * len(outs),
         scratch_shapes=list(scratch),
-        name=name,
         cost_estimate=pl.CostEstimate(flops=size, bytes_accessed=size, transcendentals=0),
         compiler_params=pltpu.CompilerParams(vmem_limit_bytes=48 << 20),
     )(*args)
@@ -117,7 +117,7 @@
 
 
 def column_of(tile, count):
-    wide = jnp.broadcast_to(tile[0:1, :], (count, 128))
+    wide = jnp.broadcast_to(tile[0:1, :], (count, tile.shape[1]))
     keep = rows_of(wide.shape) == lanes_of(wide.shape)
     return jnp.sum(jnp.where(keep, wide, 0.0), axis=1, keepdims=True)
 
@@ -152,8 +152,8 @@
     fill_xsend(info, outs[1 : 1 + nsend], planes, parts, cells_x, cells_z)
 
 
-def pack_kernel(peers, capacity, info, kern, owners, lines, turbine, out):
-    rows, width = kern.shape
+def pack_kernel(peers, capacity, info, kern, owners, lines, turbine, after, out):
+    rows, _ = kern.shape
     slots = peers * capacity
     wide = -(-peers // 128) * 128
     owner = owners[...]
@@ -246,7 +246,7 @@
 def halo_y_kernel(ax, ay, info, vel, press, parts, *refs):
     nx = len(ax.perms)
     xr, outs = refs[:nx], refs[nx:]
-    _, cells_x, cells_z, width = vel.shape
+    _, cells_x, cells_z, _ = vel.shape
     ext = cells_x + 2 * HA
     total = total_of(parts[...], xr, ax.fold, 4 * HA * cells_z)
     halo = x_halo(info, ax.count, xr, cells_x, cells_z)
@@ -267,7 +267,7 @@
         outs[2 + which][2 * cells_z :, :] = total
 
 
-def halo_z_kernel(ax, ay, az, info, vel, press, parts, *refs):
+def halo_z_kernel(ax, ay, info, vel, press, parts, *refs):
     nx, ny = len(ax.perms), len(ay.perms)
     ncross = 1 if ay.cross else 0
     xr, yr, cross = refs[:nx], refs[nx : nx + ny], refs[nx + ny : nx + ny + ncross]
@@ -477,7 +477,7 @@
     xr, refs = refs[:nx], refs[nx:]
     px, sx = refs[:2]
     sends = refs[2:]
-    cells_x, cells_z, width = p1.shape
+    cells_x, cells_z, _ = p1.shape
     one_sided = ax.count == 2
     ext = px.shape[0]
     off = jnp.where(info[0] == 0, 0, HB) if one_sided else HB
@@ -487,7 +487,6 @@
         away = jnp.where(info[0] == 0, cells_x, 0)
         px[pl.ds(away, HB)] = xr[0][:HB]
         sx[pl.ds(away, HB)] = xr[0][HB : 2 * HB]
-        near = [(True, info[0] == 0)]
     else:
         for k in range(HB):
             lower, upper = from_sides(info[0], ax.count, [r[k] for r in xr], 0.0)
@@ -519,7 +518,7 @@
 def deep_z_kernel(ay, az, npack, info, px, sx, *refs):
     ny = len(ay.perms)
     yr, sends = refs[:ny], refs[ny:]
-    ext, cells_z, width = px.shape
+    ext, cells_z, _ = px.shape
     for which in range(len(az.perms)):
         out = sends[which]
         start = pl.multiple_of(pick_side(info[2], cells_z - HB, 0, which), 8)
@@ -602,12 +601,12 @@
 
     def sweep(number, now_m, then_m, now_t, then_t):
         reach = SWEEPS - number
-        start = jnp.maximum(off - reach, 0) // 2
-        stop = (jnp.minimum(off + cells_x + reach, ext) + 1) // 2
+        start = jnp.maximum(off - reach, 0) // 8
+        stop = (jnp.minimum(off + cells_x + reach, ext) + 7) // 8
 
         def turn(q, carry):
-            for d in range(2):
-                x = 2 * q + d
+            for d in range(8):
+                x = 8 * q + d
                 scale = 1.0
                 if not one_sided:
                     place = info[0] * cells_x + x - HB
@@ -695,26 +694,14 @@
     ).astype(jnp.int32)
     inx = inflow_x[None, :]
     iny = inflow_y[None, :]
-    push = jnp.pad(thrust[None, :], ((0, 0), (0, 128 - turbines)))
-    wide = lambda row: jnp.pad(row, ((0, 0), (0, 128 - turbines)))
-    inx, iny = wide(inx), wide(iny)
+    push = thrust[None, :]
     block = capacity + 8
-    (packed,) = call(
-        functools.partial(pack_kernel, peers, capacity),
-        [(peers * block, width)],
-        [info, kernel, owners, lines[None, :], point_turbine[None, :]],
-        name="pack_rows",
-    )
-    rows = lax.all_to_all(
-        packed.reshape(peers, block, width), ("gx", "gy"), split_axis=0, concat_axis=0, tiled=True
-    ).reshape(peers * block, width)
     xsize = (4 * HA * cells_z + 8, width)
     vel, press = velocity, pressure
     parts, *xsend = call(
         functools.partial(begin_kernel, nx, turbines),
         [(8, width)] + [xsize] * nx,
         [info, vel, press, inx, iny],
-        name="begin",
     )
     zrows = z_table(cells_x)[1] + ny * 2 * HA
     zrows = -(-zrows // 8) * 8 + 8
@@ -727,17 +714,28 @@
             functools.partial(halo_y_kernel, ax, ay),
             [(8, width), (cells_z, width)] + [(2 * cells_z + 8, width)] * ny,
             [info, vel, press, parts, *xr],
-            name="halo_y",
         )
         yr = ay.swap(ysend)
         cross = [lax.ppermute(parts, "gy", ay.cross)] if ay.cross else []
+        if repeat == 0:
+            (packed,) = call(
+                functools.partial(pack_kernel, peers, capacity),
+                [(peers * block, width)],
+                [info, kernel, owners, lines[None, :], point_turbine[None, :], parts],
+            )
+            rows = lax.all_to_all(
+                packed.reshape(peers, block, width),
+                ("gx", "gy"),
+                split_axis=0,
+                concat_axis=0,
+                tiled=True,
+            ).reshape(peers * block, width)
         if not ay.fold:
             parts = lax.psum(parts, "gy")
         parts, *zsend = call(
-            functools.partial(halo_z_kernel, ax, ay, az),
+            functools.partial(halo_z_kernel, ax, ay),
             [(8, width)] + [(zrows, width)] * nz,
             [info, vel, press, parts, *xr, *yr, *cross],
-            name="halo_z",
         )
         zr = az.swap(zsend)
         cross = [lax.ppermute(parts, "gz", az.cross)] if az.cross else []
@@ -761,21 +759,18 @@
                 vm(cells_x, cells_z + 2 * ZP, width),
                 vm(cells_x * cells_z, width),
             ],
-            name="star",
         )
         xr = ax.swap(xsend)
         px, sx, *ysend = call(
             functools.partial(deep_y_kernel, ax, ay),
             [(ext_b, cells_z, width)] * 2 + [(pack_b * cells_z, width)] * ny,
             [info, p1, s6, edge, *xr],
-            name="deep_y",
         )
         yr = ay.swap(ysend)
         zsend = call(
             functools.partial(deep_z_kernel, ay, az, pack_b),
             [(2 * ext_b + ny * pack_b, HB, width)] * nz,
             [info, px, sx, *yr],
-            name="deep_z",
         )
         zr = az.swap(zsend, wide=True)
         outs = [(3, cells_x, cells_z, width), (cells_x, cells_z, width)]
@@ -795,7 +790,6 @@
                 vm(pack_b, cells_z + 2 * ZP, width),
                 vm(pack_b, cells_z + 2 * ZP, width),
             ],
-            name="sweeps",
         )
         vel, press = results[:2]
         if not last:
@@ -816,6 +810,7 @@
         P(),
         P(),
     )
+
     return jax.shard_map(
         body,
         mesh=mesh,

time: 123 us -> 120 us (0.976)
  Pallas kernels: 47.3 us -> 41.6 us
  waiting for transfers between devices: 34.6 us -> 37.1 us
    pallas_call x14, Pallas kernels: 47.3 us -> 41.6 us  [call(): pl.pallas_call(kernel, out_shape=[jax.ShapeDtypeStruct(o, F32) for o in o...]
    ppermute x20, waiting for transfers between devices: 24.8 us -> 27.2 us  [swap(): return [lax.ppermute(s, self.name, p) for s, p in zip(sends, perms)]]
    pad x3 -> x0, local copies, waits for them, and re-layouts: 1.33 us -> none  [the longest x2 1.32 us: body(): wide = lambda row: jnp.pad(row, ((0, 0), (0, 128 - turbines)))]
    unnamed x19 -> x27, local copies, waits for them, and re-layouts: 2.43 us -> 3.75 us
  transfers between devices with their start and end apart: 25 -> 25, of which waited for: 17 -> 18; matrix products, arithmetic and copies ran while one was open for 0% -> 0% of each run, Pallas kernels for 3% -> 1%
where the time goes in v4:
time: 120 us; the launch traced here: 119 us
  Pallas kernels  41.6 us (35%)
  waiting for transfers between devices  37.1 us (31%)
  starting transfers between devices  34.9 us (29%)
  local copies, waits for them, and re-layouts  3.75 us (3%)
  between operations  1.52 us (1%)
    pallas_call x14, Pallas kernels, call(): pl.pallas_call(kernel, out_shape=[jax.ShapeDtypeStruct(o, F32) for o in o...  41.6 us
    ppermute x20, waiting for transfers between devices, swap(): return [lax.ppermute(s, self.name, p) for s, p in zip(sends, perms)]  27.2 us
    ppermute x20, starting transfers between devices, swap(): return [lax.ppermute(s, self.name, p) for s, p in zip(sends, perms)]  22.6 us
    ppermute x2, waiting for transfers between devices, body(): cross = [lax.ppermute(parts, 'gz', az.cross)] if az.cross else []  5.42 us
    ppermute x2, starting transfers between devices, body(): cross = [lax.ppermute(parts, 'gz', az.cross)] if az.cross else []  4.93 us
    ppermute x2, waiting for transfers between devices, body(): cross = [lax.ppermute(parts, 'gy', ay.cross)] if ay.cross else []  4.46 us
    all_to_all x1, starting transfers between devices, body(): lax.all_to_all(packed.reshape(peers, block, width), ('gx', 'gy'), split_a...  4.36 us
    unnamed x27, local copies, waits for them, and re-layouts  3.75 us
  transfers between devices with their start and end apart: 25, of which 18 were waited for; matrix products, arithmetic and copies ran while one was open for 0% of the time, Pallas kernels for 1%

profile of v4, /device:TPU:12, one launch (start us, length us, event | category | flops | bytes accessed | tf_op | source)
XLA Modules:
  0.0 118.9 jit_solution(875366443334470263)
XLA Ops:
  8.5 2.2 %shard_map.116 = f32[576,128]{1,0:T(8,128)} custom-call(s32[4]{0:T(128)S(1)} %pad_add_fusion.info, f32[256,128]{1,0:T(8,128)S(1)} %copy-done.4, s32[256,1]{1,0:T(8,128)S(1)} %copy.12.owners, s32[1,256]{1,0:T(1,128)S(1)} %bitcast.22, s32[1,256]{1,0:T(1,128)S(1)} %bitcast.23, f32[8,128]{1,0:T(8,128)S(1)} %get-tuple-element.46.parts.after), custom_call_target="tpu_custom_call" | custom-call | flops 433168 | bytes 433168 | tf_op jit(solution)/shard_map/pallas_call | solution.py:30
  10.6 4.4 %all-to-all-start = ((f32[8,72,128]{2,1,0:T(8,128)}), f32[8,72,128]{2,1,0:T(8,128)S(1)}, u32[]{:S(2)}, u32[]{:S(2)}) async-start(f32[8,72,128]{2,1,0:T(8,128)} %bitcast.8), calls=%async_computation | async-start | bytes 589824 | tf_op jit(solution)/shard_map/all_to_all | solution.py:726
  15.0 1.5 %collective-permute-start.1 = (f32[104,128]{1,0:T(8,128)S(1)}, f32[104,128]{1,0:T(8,128)S(1)}, u32[]{:S(2)}, u32[]{:S(2)}) collective-permute-start(f32[104,128]{1,0:T(8,128)S(1)} %get-tuple-element.47), channel_id=1, source_target_pairs={{0,4},{4,0},{8,12},{12,8},{1,5},{5,1},{9,13},{13,9},{2,6},{6,2},{1... | collective-permute-start | bytes 159752 | tf_op jit(solution)/shard_map/ppermute | solution.py:79
  16.5 2.0 %collective-permute-start.3 = (f32[8,128]{1,0:T(8,128)S(1)}, f32[8,128]{1,0:T(8,128)S(1)}, u32[]{:S(2)}, u32[]{:S(2)}) collective-permute-start(f32[8,128]{1,0:T(8,128)S(1)} %get-tuple-element.46.parts.after), channel_id=1, source_target_pairs={{0,8},{4,12},{8,0},{12,4},{1,9},{5,13},{9,1},{13,5},{2,10},{6,14},... | collective-permute-start | bytes 12296 | tf_op jit(solution)/shard_map/ppermute | solution.py:719
  18.5 1.8 %collective-permute-done.3.refs_3_ = f32[8,128]{1,0:T(8,128)S(1)} collective-permute-done((f32[8,128]{1,0:T(8,128)S(1)}, f32[8,128]{1,0:T(8,128)S(1)}, u32[]{:S(2)}, u32[]{:S(2)}) %collective-permute-start.3) | collective-permute-done | bytes 4128 | tf_op jit(solution)/shard_map/ppermute | solution.py:719
  20.3 2.2 %collective-permute-done.1.refs_1_ = f32[104,128]{1,0:T(8,128)S(1)} collective-permute-done((f32[104,128]{1,0:T(8,128)S(1)}, f32[104,128]{1,0:T(8,128)S(1)}, u32[]{:S(2)}, u32[]{:S(2)}) %collective-permute-start.1) | collective-permute-done | bytes 53280 | tf_op jit(solution)/shard_map/ppermute | solution.py:79
  24.2 2.7 %collective-permute-start.5 = (f32[104,128]{1,0:T(8,128)S(1)}, f32[104,128]{1,0:T(8,128)S(1)}, u32[]{:S(2)}, u32[]{:S(2)}) collective-permute-start(f32[104,128]{1,0:T(8,128)S(1)} %get-tuple-element.52), channel_id=1, source_target_pairs={{1,2},{3,0},{2,1},{0,3},{5,6},{7,4},{6,5},{4,7},{9,10},{11,8},{10,... | collective-permute-start | bytes 159752 | tf_op jit(solution)/shard_map/ppermute | solution.py:79
  28.1 3.3 %collective-permute-done.6.refs_5_ = f32[8,128]{1,0:T(8,128)S(1)} collective-permute-done((f32[8,128]{1,0:T(8,128)S(1)}, f32[8,128]{1,0:T(8,128)S(1)}, u32[]{:S(2)}, u32[]{:S(2)}) %collective-permute-start.6) | collective-permute-done | bytes 4128 | tf_op jit(solution)/shard_map/ppermute | solution.py:741
  31.4 6.3 %shard_map.117 = (f32[3,16,48,128]{3,2,1,0:T(8,128)S(1)}, f32[16,48,128]{2,1,0:T(8,128)S(1)}, f32[16,48,128]{2,1,0:T(8,128)S(1)}, f32[2,48,128]{2,1,0:T(8,128)S(1)}, f32[17,48,128]{2,1,0:T(8,128)S(1)}) custom-call(s32[4]{0:T(128)S(1)} %pad_add_fusion.info, f32[3,16,48,128]{3,2,1,0:T(8,128)S(1)} %copy-done.1, f32[16,48,128]{2,1,0:T(8,128)S(1)} %copy-done.3, ...), custom_call_target="tpu_custom_call" | custom-call | flops 4747472 | bytes 4747472 | tf_op jit(solution)/shard_map/pallas_call | solution.py:30
  37.8 1.7 %collective-permute-done.7.refs_0_ = f32[17,48,128]{2,1,0:T(8,128)S(1)} collective-permute-done((f32[17,48,128]{2,1,0:T(8,128)S(1)}, f32[17,48,128]{2,1,0:T(8,128)S(1)}, u32[]{:S(2)}, u32[]{:S(2)}) %collective-permute-start.7) | collective-permute-done | bytes 417824 | tf_op jit(solution)/shard_map/ppermute | solution.py:79
  41.1 2.5 %collective-permute-start.9 = (f32[144,128]{1,0:T(8,128)S(1)}, f32[144,128]{1,0:T(8,128)S(1)}, u32[]{:S(2)}, u32[]{:S(2)}) collective-permute-start(f32[144,128]{1,0:T(8,128)S(1)} %get-tuple-element.61), channel_id=1, source_target_pairs={{4,8},{12,0},{8,4},{0,12},{5,9},{13,1},{9,5},{1,13},{6,10},{14,2},... | collective-permute-start | bytes 221192 | tf_op jit(solution)/shard_map/ppermute | solution.py:79
  43.7 1.9 %collective-permute-done.8.refs_0_ = f32[144,128]{1,0:T(8,128)S(1)} collective-permute-done((f32[144,128]{1,0:T(8,128)S(1)}, f32[144,128]{1,0:T(8,128)S(1)}, u32[]{:S(2)}, u32[]{:S(2)}) %collective-permute-start.8) | collective-permute-done | bytes 73760 | tf_op jit(solution)/shard_map/ppermute | solution.py:79
  45.5 2.0 %collective-permute-done.9.refs_1_ = f32[144,128]{1,0:T(8,128)S(1)} collective-permute-done((f32[144,128]{1,0:T(8,128)S(1)}, f32[144,128]{1,0:T(8,128)S(1)}, u32[]{:S(2)}, u32[]{:S(2)}) %collective-permute-start.9) | collective-permute-done | bytes 73760 | tf_op jit(solution)/shard_map/ppermute | solution.py:79
  49.5 2.5 %collective-permute-start.11 = (f32[54,8,128]{2,1,0:T(8,128)S(1)}, f32[54,8,128]{2,1,0:T(8,128)S(1)}, u32[]{:S(2)}, u32[]{:S(2)}) collective-permute-start(f32[54,8,128]{2,1,0:T(8,128)S(1)} %get-tuple-element.63), channel_id=1, source_target_pairs={{1,2},{2,1},{5,6},{6,5},{9,10},{10,9},{13,14},{14,13},{17,18},{18,... | collective-permute-start | bytes 663560 | tf_op jit(solution)/shard_map/ppermute | solution.py:79
  52.1 2.5 %collective-permute-done.10.refs_2_ = f32[54,8,128]{2,1,0:T(8,128)S(1)} collective-permute-done((f32[54,8,128]{2,1,0:T(8,128)S(1)}, f32[54,8,128]{2,1,0:T(8,128)S(1)}, u32[]{:S(2)}, u32[]{:S(2)}) %collective-permute-start.10) | collective-permute-done | bytes 221216 | tf_op jit(solution)/shard_map/ppermute | solution.py:79
  54.5 2.9 %collective-permute-done.11.refs_3_ = f32[54,8,128]{2,1,0:T(8,128)S(1)} collective-permute-done((f32[54,8,128]{2,1,0:T(8,128)S(1)}, f32[54,8,128]{2,1,0:T(8,128)S(1)}, u32[]{:S(2)}, u32[]{:S(2)}) %collective-permute-start.11) | collective-permute-done | bytes 221216 | tf_op jit(solution)/shard_map/ppermute | solution.py:79
  57.5 9.1 %shard_map.120 = (f32[3,16,48,128]{3,2,1,0:T(8,128)S(1)}, f32[16,48,128]{2,1,0:T(8,128)S(1)}, f32[8,128]{1,0:T(8,128)S(1)}, f32[392,128]{1,0:T(8,128)S(1)}) custom-call(s32[4]{0:T(128)S(1)} %pad_add_fusion.info, f32[24,48,128]{2,1,0:T(8,128)S(1)} %get-tuple-element.57.px, f32[24,48,128]{2,1,0:T(8,128)S(1)} %get-tuple-element.58.sx, ...), custom_call_target="tpu_custom_call" | custom-call | flops 4727184 | bytes 4727184 | tf_op jit(solution)/shard_map/pallas_call | solution.py:30
  66.7 1.4 %collective-permute-done.12.refs_0_ = f32[392,128]{1,0:T(8,128)S(1)} collective-permute-done((f32[392,128]{1,0:T(8,128)S(1)}, f32[392,128]{1,0:T(8,128)S(1)}, u32[]{:S(2)}, u32[]{:S(2)}) %collective-permute-start.12) | collective-permute-done | bytes 200736 | tf_op jit(solution)/shard_map/ppermute | solution.py:79
  70.4 1.5 %collective-permute-start.14 = (f32[104,128]{1,0:T(8,128)S(1)}, f32[104,128]{1,0:T(8,128)S(1)}, u32[]{:S(2)}, u32[]{:S(2)}) collective-permute-start(f32[104,128]{1,0:T(8,128)S(1)} %get-tuple-element.70), channel_id=1, source_target_pairs={{4,8},{12,0},{8,4},{0,12},{5,9},{13,1},{9,5},{1,13},{6,10},{14,2},... | collective-permute-start | bytes 159752 | tf_op jit(solution)/shard_map/ppermute | solution.py:79
  72.9 2.6 %collective-permute-done.15.refs_3_ = f32[8,128]{1,0:T(8,128)S(1)} collective-permute-done((f32[8,128]{1,0:T(8,128)S(1)}, f32[8,128]{1,0:T(8,128)S(1)}, u32[]{:S(2)}, u32[]{:S(2)}) %collective-permute-start.15) | collective-permute-done | bytes 4128 | tf_op jit(solution)/shard_map/ppermute | solution.py:719
  76.9 3.7 %collective-permute-start.18 = (f32[8,128]{1,0:T(8,128)S(1)}, f32[8,128]{1,0:T(8,128)S(1)}, u32[]{:S(2)}, u32[]{:S(2)}) collective-permute-start(f32[8,128]{1,0:T(8,128)S(1)} %get-tuple-element.71.parts), channel_id=1, source_target_pairs={{0,2},{1,3},{2,0},{3,1},{4,6},{5,7},{6,4},{7,5},{8,10},{9,11},{10,... | collective-permute-start | bytes 12296 | tf_op jit(solution)/shard_map/ppermute | solution.py:741
  80.6 2.2 %collective-permute-done.18.refs_5_ = f32[8,128]{1,0:T(8,128)S(1)} collective-permute-done((f32[8,128]{1,0:T(8,128)S(1)}, f32[8,128]{1,0:T(8,128)S(1)}, u32[]{:S(2)}, u32[]{:S(2)}) %collective-permute-start.18) | collective-permute-done | bytes 4128 | tf_op jit(solution)/shard_map/ppermute | solution.py:741
  82.7 6.3 %shard_map.123 = (f32[3,16,48,128]{3,2,1,0:T(8,128)S(1)}, f32[16,48,128]{2,1,0:T(8,128)S(1)}, f32[16,48,128]{2,1,0:T(8,128)S(1)}, f32[2,48,128]{2,1,0:T(8,128)S(1)}, f32[17,48,128]{2,1,0:T(8,128)S(1)}) custom-call(s32[4]{0:T(128)S(1)} %pad_add_fusion.info, f32[3,16,48,128]{3,2,1,0:T(8,128)S(1)} %get-tuple-element.64.vel, ...), custom_call_target="tpu_custom_call" | custom-call | flops 4747472 | bytes 4747472 | tf_op jit(solution)/shard_map/pallas_call | solution.py:30
  89.1 1.7 %collective-permute-done.19.refs_0_ = f32[17,48,128]{2,1,0:T(8,128)S(1)} collective-permute-done((f32[17,48,128]{2,1,0:T(8,128)S(1)}, f32[17,48,128]{2,1,0:T(8,128)S(1)}, u32[]{:S(2)}, u32[]{:S(2)}) %collective-permute-start.19) | collective-permute-done | bytes 417824 | tf_op jit(solution)/shard_map/ppermute | solution.py:79
  93.0 1.5 %collective-permute-start.21 = (f32[144,128]{1,0:T(8,128)S(1)}, f32[144,128]{1,0:T(8,128)S(1)}, u32[]{:S(2)}, u32[]{:S(2)}) collective-permute-start(f32[144,128]{1,0:T(8,128)S(1)} %get-tuple-element.83), channel_id=1, source_target_pairs={{4,8},{12,0},{8,4},{0,12},{5,9},{13,1},{9,5},{1,13},{6,10},{14,2},... | collective-permute-start | bytes 221192 | tf_op jit(solution)/shard_map/ppermute | solution.py:79
  94.5 2.4 %collective-permute-done.20.refs_0_ = f32[144,128]{1,0:T(8,128)S(1)} collective-permute-done((f32[144,128]{1,0:T(8,128)S(1)}, f32[144,128]{1,0:T(8,128)S(1)}, u32[]{:S(2)}, u32[]{:S(2)}) %collective-permute-start.20) | collective-permute-done | bytes 73760 | tf_op jit(solution)/shard_map/ppermute | solution.py:79
  96.8 1.5 %collective-permute-done.21.refs_1_ = f32[144,128]{1,0:T(8,128)S(1)} collective-permute-done((f32[144,128]{1,0:T(8,128)S(1)}, f32[144,128]{1,0:T(8,128)S(1)}, u32[]{:S(2)}, u32[]{:S(2)}) %collective-permute-start.21) | collective-permute-done | bytes 73760 | tf_op jit(solution)/shard_map/ppermute | solution.py:79
  99.0 1.6 %collective-permute-start.22 = (f32[54,8,128]{2,1,0:T(8,128)S(1)}, f32[54,8,128]{2,1,0:T(8,128)S(1)}, u32[]{:S(2)}, u32[]{:S(2)}) collective-permute-start(f32[54,8,128]{2,1,0:T(8,128)S(1)} %get-tuple-element.84), channel_id=1, source_target_pairs={{0,1},{1,0},{2,3},{3,2},{4,5},{5,4},{6,7},{7,6},{8,9},{9,8},{10,11... | collective-permute-start | bytes 663560 | tf_op jit(solution)/shard_map/ppermute | solution.py:79
  100.5 3.3 %collective-permute-start.23 = (f32[54,8,128]{2,1,0:T(8,128)S(1)}, f32[54,8,128]{2,1,0:T(8,128)S(1)}, u32[]{:S(2)}, u32[]{:S(2)}) collective-permute-start(f32[54,8,128]{2,1,0:T(8,128)S(1)} %get-tuple-element.85), channel_id=1, source_target_pairs={{1,2},{2,1},{5,6},{6,5},{9,10},{10,9},{13,14},{14,13},{17,18},{18,... | collective-permute-start | bytes 663560 | tf_op jit(solution)/shard_map/ppermute | solution.py:79
  103.9 1.9 %collective-permute-done.22.refs_2_ = f32[54,8,128]{2,1,0:T(8,128)S(1)} collective-permute-done((f32[54,8,128]{2,1,0:T(8,128)S(1)}, f32[54,8,128]{2,1,0:T(8,128)S(1)}, u32[]{:S(2)}, u32[]{:S(2)}) %collective-permute-start.22) | collective-permute-done | bytes 221216 | tf_op jit(solution)/shard_map/ppermute | solution.py:79
  105.8 3.1 %collective-permute-done.23.refs_3_ = f32[54,8,128]{2,1,0:T(8,128)S(1)} collective-permute-done((f32[54,8,128]{2,1,0:T(8,128)S(1)}, f32[54,8,128]{2,1,0:T(8,128)S(1)}, u32[]{:S(2)}, u32[]{:S(2)}) %collective-permute-start.23) | collective-permute-done | bytes 221216 | tf_op jit(solution)/shard_map/ppermute | solution.py:79
  108.9 10.0 %shard_map.126 = (f32[3,16,48,128]{3,2,1,0:T(8,128)}, f32[16,48,128]{2,1,0:T(8,128)}) custom-call(s32[4]{0:T(128)S(1)} %pad_add_fusion.info, f32[24,48,128]{2,1,0:T(8,128)S(1)} %get-tuple-element.79.px, f32[24,48,128]{2,1,0:T(8,128)S(1)} %get-tuple-element.80.sx, f32[3,16,48,128]{3,2,1,0:T(8,128)S(1)} %get-tuple-element.81.star, s32[1,48]{1,0:T(1,128)S(1)} %bitcast.16, ...), custom_call_target="tpu_custom_call" | custom-call | flops 4522384 | bytes 4522384 | tf_op jit(solution)/shard_map/pallas_call | solution.py:30
  (60 shorter events, 21.2 us)
Async XLA Ops:
  0.6 5.2 %copy-start.12 = (s32[256,1]{0,1:T(1,128)S(1)}, s32[256,1]{0,1:T(1,128)}, u32[]{:S(2)}) copy-start(s32[256,1]{0,1:T(1,128)} %param.13) | copy-start | bytes 3076
  5.7 2.7 %copy-start.4 = (f32[256,128]{1,0:T(8,128)S(1)}, f32[256,128]{1,0:T(8,128)}, u32[]{:S(2)}) copy-start(f32[256,128]{1,0:T(8,128)} %kern.1) | copy-start | bytes 393220
  5.7 2.8 %copy-start.10 = (s32[256]{0:T(256)S(1)}, s32[256]{0:T(256)}, u32[]{:S(2)}) copy-start(s32[256]{0:T(256)} %param.14) | copy-start | bytes 3076
  5.7 2.8 %copy-start.11 = (s32[256]{0:T(256)S(1)}, s32[256]{0:T(256)}, u32[]{:S(2)}) copy-start(s32[256]{0:T(256)} %param.15) | copy-start | bytes 3076
  5.7 1.5 %collective-permute-start = (f32[392,128]{1,0:T(8,128)S(1)}, f32[392,128]{1,0:T(8,128)S(1)}, u32[]{:S(2)}, u32[]{:S(2)}) collective-permute-start(f32[392,128]{1,0:T(8,128)S(1)} %get-tuple-element.45), channel_id=1, source_target_pairs={{0,16},{16,0},{1,17},{17,1},{2,18},{18,2},{3,19},{19,3},{4,20},{20... | collective-permute-start | bytes 602120 | tf_op jit(solution)/shard_map/ppermute | solution.py:79
  10.6 20.8 %copy-start.9 = (f32[48]{0:T(128)S(1)}, f32[48]{0:T(128)}, u32[]{:S(2)}) copy-start(f32[48]{0:T(128)} %param.17) | copy-start | bytes 580
  10.6 20.8 %all-to-all-start = ((f32[8,72,128]{2,1,0:T(8,128)}), f32[8,72,128]{2,1,0:T(8,128)S(1)}, u32[]{:S(2)}, u32[]{:S(2)}) async-start(f32[8,72,128]{2,1,0:T(8,128)} %bitcast.8), calls=%async_computation | async-start | bytes 589824 | tf_op jit(solution)/shard_map/all_to_all | solution.py:726
  15.0 7.5 %collective-permute-start.1 = (f32[104,128]{1,0:T(8,128)S(1)}, f32[104,128]{1,0:T(8,128)S(1)}, u32[]{:S(2)}, u32[]{:S(2)}) collective-permute-start(f32[104,128]{1,0:T(8,128)S(1)} %get-tuple-element.47), channel_id=1, source_target_pairs={{0,4},{4,0},{8,12},{12,8},{1,5},{5,1},{9,13},{13,9},{2,6},{6,2},{1... | collective-permute-start | bytes 159752 | tf_op jit(solution)/shard_map/ppermute | solution.py:79
  16.5 6.6 %collective-permute-start.2 = (f32[104,128]{1,0:T(8,128)S(1)}, f32[104,128]{1,0:T(8,128)S(1)}, u32[]{:S(2)}, u32[]{:S(2)}) collective-permute-start(f32[104,128]{1,0:T(8,128)S(1)} %get-tuple-element.48), channel_id=1, source_target_pairs={{4,8},{12,0},{8,4},{0,12},{5,9},{13,1},{9,5},{1,13},{6,10},{14,2},... | collective-permute-start | bytes 159752 | tf_op jit(solution)/shard_map/ppermute | solution.py:79
  16.5 3.8 %collective-permute-start.3 = (f32[8,128]{1,0:T(8,128)S(1)}, f32[8,128]{1,0:T(8,128)S(1)}, u32[]{:S(2)}, u32[]{:S(2)}) collective-permute-start(f32[8,128]{1,0:T(8,128)S(1)} %get-tuple-element.46.parts.after), channel_id=1, source_target_pairs={{0,8},{4,12},{8,0},{12,4},{1,9},{5,13},{9,1},{13,5},{2,10},{6,14},... | collective-permute-start | bytes 12296 | tf_op jit(solution)/shard_map/ppermute | solution.py:719
  23.7 7.7 %collective-permute-start.4 = (f32[104,128]{1,0:T(8,128)S(1)}, f32[104,128]{1,0:T(8,128)S(1)}, u32[]{:S(2)}, u32[]{:S(2)}) collective-permute-start(f32[104,128]{1,0:T(8,128)S(1)} %get-tuple-element.51), channel_id=1, source_target_pairs={{0,1},{1,0},{2,3},{3,2},{4,5},{5,4},{6,7},{7,6},{8,9},{9,8},{10,11... | collective-permute-start | bytes 159752 | tf_op jit(solution)/shard_map/ppermute | solution.py:79
  24.2 7.2 %collective-permute-start.5 = (f32[104,128]{1,0:T(8,128)S(1)}, f32[104,128]{1,0:T(8,128)S(1)}, u32[]{:S(2)}, u32[]{:S(2)}) collective-permute-start(f32[104,128]{1,0:T(8,128)S(1)} %get-tuple-element.52), channel_id=1, source_target_pairs={{1,2},{3,0},{2,1},{0,3},{5,6},{7,4},{6,5},{4,7},{9,10},{11,8},{10,... | collective-permute-start | bytes 159752 | tf_op jit(solution)/shard_map/ppermute | solution.py:79
  26.9 4.5 %collective-permute-start.6 = (f32[8,128]{1,0:T(8,128)S(1)}, f32[8,128]{1,0:T(8,128)S(1)}, u32[]{:S(2)}, u32[]{:S(2)}) collective-permute-start(f32[8,128]{1,0:T(8,128)S(1)} %get-tuple-element.49.parts), channel_id=1, source_target_pairs={{0,2},{1,3},{2,0},{3,1},{4,6},{5,7},{6,4},{7,5},{8,10},{9,11},{10,... | collective-permute-start | bytes 12296 | tf_op jit(solution)/shard_map/ppermute | solution.py:741
  37.8 1.8 %collective-permute-start.7 = (f32[17,48,128]{2,1,0:T(8,128)S(1)}, f32[17,48,128]{2,1,0:T(8,128)S(1)}, u32[]{:S(2)}, u32[]{:S(2)}) collective-permute-start(f32[17,48,128]{2,1,0:T(8,128)S(1)} %get-tuple-element.56), channel_id=1, source_target_pairs={{0,16},{16,0},{1,17},{17,1},{2,18},{18,2},{3,19},{19,3},{4,20},{20... | collective-permute-start | bytes 1253384 | tf_op jit(solution)/shard_map/ppermute | solution.py:79
  39.6 17.9 %copy-start.6 = (s32[48]{0:T(128)S(1)}, s32[48]{0:T(128)}, u32[]{:S(2)}) copy-start(s32[48]{0:T(128)} %param.18) | copy-start | bytes 580
  39.6 17.9 %copy-start.8 = (s32[48]{0:T(128)S(1)}, s32[48]{0:T(128)}, u32[]{:S(2)}) copy-start(s32[48]{0:T(128)} %param.19) | copy-start | bytes 580
  40.7 4.9 %collective-permute-start.8 = (f32[144,128]{1,0:T(8,128)S(1)}, f32[144,128]{1,0:T(8,128)S(1)}, u32[]{:S(2)}, u32[]{:S(2)}) collective-permute-start(f32[144,128]{1,0:T(8,128)S(1)} %get-tuple-element.60), channel_id=1, source_target_pairs={{0,4},{4,0},{8,12},{12,8},{1,5},{5,1},{9,13},{13,9},{2,6},{6,2},{1... | collective-permute-start | bytes 221192 | tf_op jit(solution)/shard_map/ppermute | solution.py:79
  41.1 6.4 %collective-permute-start.9 = (f32[144,128]{1,0:T(8,128)S(1)}, f32[144,128]{1,0:T(8,128)S(1)}, u32[]{:S(2)}, u32[]{:S(2)}) collective-permute-start(f32[144,128]{1,0:T(8,128)S(1)} %get-tuple-element.61), channel_id=1, source_target_pairs={{4,8},{12,0},{8,4},{0,12},{5,9},{13,1},{9,5},{1,13},{6,10},{14,2},... | collective-permute-start | bytes 221192 | tf_op jit(solution)/shard_map/ppermute | solution.py:79
  48.1 6.4 %collective-permute-start.10 = (f32[54,8,128]{2,1,0:T(8,128)S(1)}, f32[54,8,128]{2,1,0:T(8,128)S(1)}, u32[]{:S(2)}, u32[]{:S(2)}) collective-permute-start(f32[54,8,128]{2,1,0:T(8,128)S(1)} %get-tuple-element.62), channel_id=1, source_target_pairs={{0,1},{1,0},{2,3},{3,2},{4,5},{5,4},{6,7},{7,6},{8,9},{9,8},{10,11... | collective-permute-start | bytes 663560 | tf_op jit(solution)/shard_map/ppermute | solution.py:79
  49.5 7.9 %collective-permute-start.11 = (f32[54,8,128]{2,1,0:T(8,128)S(1)}, f32[54,8,128]{2,1,0:T(8,128)S(1)}, u32[]{:S(2)}, u32[]{:S(2)}) collective-permute-start(f32[54,8,128]{2,1,0:T(8,128)S(1)} %get-tuple-element.63), channel_id=1, source_target_pairs={{1,2},{2,1},{5,6},{6,5},{9,10},{10,9},{13,14},{14,13},{17,18},{18,... | collective-permute-start | bytes 663560 | tf_op jit(solution)/shard_map/ppermute | solution.py:79
  66.6 1.5 %collective-permute-start.12 = (f32[392,128]{1,0:T(8,128)S(1)}, f32[392,128]{1,0:T(8,128)S(1)}, u32[]{:S(2)}, u32[]{:S(2)}) collective-permute-start(f32[392,128]{1,0:T(8,128)S(1)} %get-tuple-element.67), channel_id=1, source_target_pairs={{0,16},{16,0},{1,17},{17,1},{2,18},{18,2},{3,19},{19,3},{4,20},{20... | collective-permute-start | bytes 602120 | tf_op jit(solution)/shard_map/ppermute | solution.py:79
  69.3 6.2 %collective-permute-start.13 = (f32[104,128]{1,0:T(8,128)S(1)}, f32[104,128]{1,0:T(8,128)S(1)}, u32[]{:S(2)}, u32[]{:S(2)}) collective-permute-start(f32[104,128]{1,0:T(8,128)S(1)} %get-tuple-element.69), channel_id=1, source_target_pairs={{0,4},{4,0},{8,12},{12,8},{1,5},{5,1},{9,13},{13,9},{2,6},{6,2},{1... | collective-permute-start | bytes 159752 | tf_op jit(solution)/shard_map/ppermute | solution.py:79
  70.4 5.1 %collective-permute-start.14 = (f32[104,128]{1,0:T(8,128)S(1)}, f32[104,128]{1,0:T(8,128)S(1)}, u32[]{:S(2)}, u32[]{:S(2)}) collective-permute-start(f32[104,128]{1,0:T(8,128)S(1)} %get-tuple-element.70), channel_id=1, source_target_pairs={{4,8},{12,0},{8,4},{0,12},{5,9},{13,1},{9,5},{1,13},{6,10},{14,2},... | collective-permute-start | bytes 159752 | tf_op jit(solution)/shard_map/ppermute | solution.py:79
  71.9 3.6 %collective-permute-start.15 = (f32[8,128]{1,0:T(8,128)S(1)}, f32[8,128]{1,0:T(8,128)S(1)}, u32[]{:S(2)}, u32[]{:S(2)}) collective-permute-start(f32[8,128]{1,0:T(8,128)S(1)} %get-tuple-element.68.parts), channel_id=1, source_target_pairs={{0,8},{4,12},{8,0},{12,4},{1,9},{5,13},{9,1},{13,5},{2,10},{6,14},... | collective-permute-start | bytes 12296 | tf_op jit(solution)/shard_map/ppermute | solution.py:719
  76.1 6.6 %collective-permute-start.16 = (f32[104,128]{1,0:T(8,128)S(1)}, f32[104,128]{1,0:T(8,128)S(1)}, u32[]{:S(2)}, u32[]{:S(2)}) collective-permute-start(f32[104,128]{1,0:T(8,128)S(1)} %get-tuple-element.73), channel_id=1, source_target_pairs={{0,1},{1,0},{2,3},{3,2},{4,5},{5,4},{6,7},{7,6},{8,9},{9,8},{10,11... | collective-permute-start | bytes 159752 | tf_op jit(solution)/shard_map/ppermute | solution.py:79
  76.2 6.5 %collective-permute-start.17 = (f32[104,128]{1,0:T(8,128)S(1)}, f32[104,128]{1,0:T(8,128)S(1)}, u32[]{:S(2)}, u32[]{:S(2)}) collective-permute-start(f32[104,128]{1,0:T(8,128)S(1)} %get-tuple-element.74), channel_id=1, source_target_pairs={{1,2},{3,0},{2,1},{0,3},{5,6},{7,4},{6,5},{4,7},{9,10},{11,8},{10,... | collective-permute-start | bytes 159752 | tf_op jit(solution)/shard_map/ppermute | solution.py:79
  76.9 5.8 %collective-permute-start.18 = (f32[8,128]{1,0:T(8,128)S(1)}, f32[8,128]{1,0:T(8,128)S(1)}, u32[]{:S(2)}, u32[]{:S(2)}) collective-permute-start(f32[8,128]{1,0:T(8,128)S(1)} %get-tuple-element.71.parts), channel_id=1, source_target_pairs={{0,2},{1,3},{2,0},{3,1},{4,6},{5,7},{6,4},{7,5},{8,10},{9,11},{10,... | collective-permute-start | bytes 12296 | tf_op jit(solution)/shard_map/ppermute | solution.py:741
  89.1 1.8 %collective-permute-start.19 = (f32[17,48,128]{2,1,0:T(8,128)S(1)}, f32[17,48,128]{2,1,0:T(8,128)S(1)}, u32[]{:S(2)}, u32[]{:S(2)}) collective-permute-start(f32[17,48,128]{2,1,0:T(8,128)S(1)} %get-tuple-element.78), channel_id=1, source_target_pairs={{0,16},{16,0},{1,17},{17,1},{2,18},{18,2},{3,19},{19,3},{4,20},{20... | collective-permute-start | bytes 1253384 | tf_op jit(solution)/shard_map/ppermute | solution.py:79
  92.0 4.9 %collective-permute-start.20 = (f32[144,128]{1,0:T(8,128)S(1)}, f32[144,128]{1,0:T(8,128)S(1)}, u32[]{:S(2)}, u32[]{:S(2)}) collective-permute-start(f32[144,128]{1,0:T(8,128)S(1)} %get-tuple-element.82), channel_id=1, source_target_pairs={{0,4},{4,0},{8,12},{12,8},{1,5},{5,1},{9,13},{13,9},{2,6},{6,2},{1... | collective-permute-start | bytes 221192 | tf_op jit(solution)/shard_map/ppermute | solution.py:79
  93.0 5.4 %collective-permute-start.21 = (f32[144,128]{1,0:T(8,128)S(1)}, f32[144,128]{1,0:T(8,128)S(1)}, u32[]{:S(2)}, u32[]{:S(2)}) collective-permute-start(f32[144,128]{1,0:T(8,128)S(1)} %get-tuple-element.83), channel_id=1, source_target_pairs={{4,8},{12,0},{8,4},{0,12},{5,9},{13,1},{9,5},{1,13},{6,10},{14,2},... | collective-permute-start | bytes 221192 | tf_op jit(solution)/shard_map/ppermute | solution.py:79
  99.0 6.8 %collective-permute-start.22 = (f32[54,8,128]{2,1,0:T(8,128)S(1)}, f32[54,8,128]{2,1,0:T(8,128)S(1)}, u32[]{:S(2)}, u32[]{:S(2)}) collective-permute-start(f32[54,8,128]{2,1,0:T(8,128)S(1)} %get-tuple-element.84), channel_id=1, source_target_pairs={{0,1},{1,0},{2,3},{3,2},{4,5},{5,4},{6,7},{7,6},{8,9},{9,8},{10,11... | collective-permute-start | bytes 663560 | tf_op jit(solution)/shard_map/ppermute | solution.py:79
  100.5 8.4 %collective-permute-start.23 = (f32[54,8,128]{2,1,0:T(8,128)S(1)}, f32[54,8,128]{2,1,0:T(8,128)S(1)}, u32[]{:S(2)}, u32[]{:S(2)}) collective-permute-start(f32[54,8,128]{2,1,0:T(8,128)S(1)} %get-tuple-element.85), channel_id=1, source_target_pairs={{1,2},{2,1},{5,6},{6,5},{9,10},{10,9},{13,14},{14,13},{17,18},{18,... | collective-permute-start | bytes 663560 | tf_op jit(solution)/shard_map/ppermute | solution.py:79
  (6 other events, 8.2 us)

commit v5 on v4

--- a/solution.py
+++ b/solution.py
@@ -34,7 +34,7 @@
         out_specs=[pl.BlockSpec(memory_space=pltpu.VMEM)] * len(outs),
         scratch_shapes=list(scratch),
         cost_estimate=pl.CostEstimate(flops=size, bytes_accessed=size, transcendentals=0),
-        compiler_params=pltpu.CompilerParams(vmem_limit_bytes=48 << 20),
+        compiler_params=pltpu.CompilerParams(vmem_limit_bytes=24 << 20),
     )(*args)
 
 
@@ -530,9 +530,129 @@
                 out[2 * ext + j * npack + i] = yr[j][pl.ds(at, HB), :]
 
 
+def beside(m, h):
+    width = m.shape[1]
+    first_lane, last_lane = lanes_of(m.shape) == 0, lanes_of(m.shape) == width - 1
+    ml, mr, hl, hr = roll(m, 1, 1), roll(m, -1, 1), roll(h, 1, 1), roll(h, -1, 1)
+    return (
+        (jnp.where(first_lane, hl, ml), jnp.where(last_lane, hr, mr)),
+        (jnp.where(first_lane, ml, hl), jnp.where(last_lane, mr, hr)),
+    )
+
+
+def run_sweeps(ax, ay, az, info, pms, pts, sm, st, cells_x, cells_z, tiles, after):
+    one_sided = ax.count == 2
+    ext, _, width = sm.shape
+    off = jnp.where(info[0] == 0, 0, HB) if one_sided else HB
+    low = ZO - ZP
+    lane = lanes_of((8, width))
+    keep_y = ((lane < HB) & (info[1] < ay.count - 1)) | ((lane >= width - HB) & (info[1] > 0))
+    sixth = 1.0 / 6.0
+    weight_y = jnp.where(keep_y, sixth, 0.0)
+    turns = 8
+
+    def sweep(number, now_m, then_m, now_t, then_t):
+        reach = SWEEPS - number
+        start = jnp.maximum(off - reach, 0) // turns
+        stop = (jnp.minimum(off + cells_x + reach, ext) + turns - 1) // turns
+
+        def turn(q, carry):
+            for d in range(turns):
+                x = turns * q + d
+                scale = 1.0
+                if not one_sided:
+                    place = info[0] * cells_x + x - HB
+                    inside = (place >= 0) & (place < ax.count * cells_x)
+                    scale = jnp.where(inside, 1.0, 0.0)
+                for t in tiles:
+                    weight = scale
+                    if t < ZP:
+                        weight = weight * jnp.where(info[2] > 0, 1.0, 0.0)
+                    elif t >= ZP + cells_z:
+                        weight = weight * jnp.where(info[2] < az.count - 1, 1.0, 0.0)
+                    r = low + t
+                    sides = beside(now_m[x + 1, r : r + 8, :], now_t[x + 1, r : r + 8, :])
+                    for now, then, source, factor, (left, right) in (
+                        (now_m, then_m, sm, sixth * weight, sides[0]),
+                        (now_t, then_t, st, weight_y * weight, sides[1]),
+                    ):
+                        total = now[x, r : r + 8, :] + now[x + 2, r : r + 8, :]
+                        total = total + (
+                            now[x + 1, r - 1 : r + 7, :] + now[x + 1, r + 1 : r + 9, :]
+                        )
+                        total = total + (left + right)
+                        then[x + 1, r : r + 8, :] = total * factor - source[x, t : t + 8, :]
+                after(number, x, then_m, then_t)
+            return carry
+
+        lax.fori_loop(start, stop, turn, 0)
+
+    def pair(number, carry):
+        sweep(2 * number + 1, pms[0], pms[1], pts[0], pts[1])
+        sweep(2 * number + 2, pms[1], pms[0], pts[1], pts[0])
+        return carry
+
+    count = SWEEPS - 1
+    lax.fori_loop(0, count // 2, pair, 0)
+    if count % 2:
+        sweep(count, pms[0], pms[1], pts[0], pts[1])
+    return count % 2
+
+
+def inner_tiles(cells_z):
+    return ZP + 8, cells_z - 8
+
+
+def inner_kernel(ax, ay, az, npack, cells_x, info, px, sx, *refs):
+    ny = len(ay.perms)
+    yr, refs = refs[:ny], refs[ny:]
+    edge_m, edge_t, last_m, last_t, first_t, source_t = refs[:6]
+    pms, pts = refs[6:8], refs[8:10]
+    sm, st = refs[10:]
+    ext, cells_z, width = px.shape
+    slot = 2 * HB
+    per = width // slot
+    end = ZO + cells_z
+    blank = jnp.zeros((cells_z + 2 * ZO, width), F32)
+    for planes in pms + pts:
+        planes[0] = blank
+        planes[ext + 1] = blank
+    halves = []
+    for i in range(npack):
+        lower, upper = from_sides(
+            info[1], ay.count, [r[i * cells_z : (i + 1) * cells_z, :] for r in yr], 0.0
+        )
+        halves.append(split_edges(lower, upper, HB))
+    for k in range(per):
+        for x in range(k, ext, per):
+            one, two = halves[x // per]
+            one = roll(one, -(slot * k + HB), 1)
+            two = roll(two, -(slot * k + HB), 1)
+            pts[0][x + 1, ZO:end, :] = one
+            first_t[x] = one
+            st[x, ZP : ZP + cells_z, :] = two
+            source_t[x] = two
+    for x in range(ext):
+        pms[0][x + 1, ZO:end, :] = px[x]
+        sm[x, ZP : ZP + cells_z, :] = sx[x]
+
+    def after(number, x, then_m, then_t):
+        for side, t in enumerate(inner_tiles(cells_z)):
+            r = ZO - ZP + t
+            edge_m[number - 1, side, x] = then_m[x + 1, r : r + 8, :]
+            edge_t[number - 1, side, x] = then_t[x + 1, r : r + 8, :]
+
+    tiles = range(ZP, ZP + cells_z, 8)
+    done = run_sweeps(ax, ay, az, info, pms, pts, sm, st, cells_x, cells_z, tiles, after)
+    for x in range(ext):
+        last_m[x] = pms[done][x + 1, ZO:end, :]
+        last_t[x] = pts[done][x + 1, ZO:end, :]
+
+
 def sweep_kernel(ax, ay, az, npack, last, turbines, info, px, sx, star, inx, iny, *refs):
     ny, nz = len(ay.perms), len(az.perms)
-    yr, refs = refs[:ny], refs[ny:]
+    edge_m, edge_t, last_m, last_t, first_t, source_t = refs[:6]
+    refs = refs[6:]
     zr, refs = refs[:nz], refs[nz:]
     vel, press = refs[:2]
     refs = refs[2:]
@@ -560,90 +680,51 @@
     def z_tile(k):
         return from_sides(info[2], az.count, [r[k] for r in zr], 0.0)
 
+    outer = (slice(0, 16), slice(cells_z - 16, cells_z))
     for x in range(ext):
         lower, upper = z_tile(x)
         pm[x + 1, low:ZO, :] = lower
         pm[x + 1, end : end + ZP, :] = upper
-        pm[x + 1, ZO:end, :] = px[x]
         lower, upper = z_tile(ext + x)
         sm[x, :ZP, :] = lower
         sm[x, ZP + cells_z :, :] = upper
-        sm[x, ZP : ZP + cells_z, :] = sx[x]
+        for rows in outer:
+            pm[x + 1, ZO + rows.start : ZO + rows.stop, :] = px[x, rows, :]
+            pt[x + 1, ZO + rows.start : ZO + rows.stop, :] = first_t[x, rows, :]
+            sm[x, ZP + rows.start : ZP + rows.stop, :] = sx[x, rows, :]
+            st[x, ZP + rows.start : ZP + rows.stop, :] = source_t[x, rows, :]
     for i in range(npack):
         zs = [z_tile(2 * ext + j * npack + i) for j in range(ny)]
-        for start, stop, pieces in (
-            (ZO, end, [r[i * cells_z : (i + 1) * cells_z, :] for r in yr]),
-            (low, ZO, [z[0] for z in zs]),
-            (end, end + ZP, [z[1] for z in zs]),
-        ):
-            lower, upper = from_sides(info[1], ay.count, pieces, 0.0)
+        for k in range(2):
+            lower, upper = from_sides(info[1], ay.count, [z[k] for z in zs], 0.0)
             one, two = split_edges(lower, upper, HB)
-            ph[i, start - low : stop - low, :] = one
-            sh[i, start - low : stop - low, :] = two
-
+            ph[i, k * ZP : (k + 1) * ZP, :] = one
+            sh[i, k * ZP : (k + 1) * ZP, :] = two
     for k in range(per):
         for x in range(k, ext, per):
-            pt[x + 1, low : end + ZP, :] = roll(ph[x // per], -(slot * k + HB), 1)
-            st[x] = roll(sh[x // per], -(slot * k + HB), 1)
-
-    lane = lanes_of((8, width))
-    keep_y = ((lane < HB) & (info[1] < ay.count - 1)) | ((lane >= width - HB) & (info[1] > 0))
-    sixth = 1.0 / 6.0
-    weight_y = jnp.where(keep_y, sixth, 0.0)
-    first_lane, last_lane = lane == 0, lane == width - 1
-
-    def beside(m, h):
-        ml, mr, hl, hr = roll(m, 1, 1), roll(m, -1, 1), roll(h, 1, 1), roll(h, -1, 1)
-        return (
-            (jnp.where(first_lane, hl, ml), jnp.where(last_lane, hr, mr)),
-            (jnp.where(first_lane, ml, hl), jnp.where(last_lane, mr, hr)),
-        )
-
-    def sweep(number, now_m, then_m, now_t, then_t):
-        reach = SWEEPS - number
-        start = jnp.maximum(off - reach, 0) // 8
-        stop = (jnp.minimum(off + cells_x + reach, ext) + 7) // 8
-
-        def turn(q, carry):
-            for d in range(8):
-                x = 8 * q + d
-                scale = 1.0
-                if not one_sided:
-                    place = info[0] * cells_x + x - HB
-                    inside = (place >= 0) & (place < ax.count * cells_x)
-                    scale = jnp.where(inside, 1.0, 0.0)
-                for t in range(0, cells_z + 2 * ZP, 8):
-                    weight = scale
-                    if t < ZP:
-                        weight = weight * jnp.where(info[2] > 0, 1.0, 0.0)
-                    elif t >= ZP + cells_z:
-                        weight = weight * jnp.where(info[2] < az.count - 1, 1.0, 0.0)
-                    r = low + t
-                    sides = beside(now_m[x + 1, r : r + 8, :], now_t[x + 1, r : r + 8, :])
-                    for now, then, source, factor, (left, right) in (
-                        (now_m, then_m, sm, sixth * weight, sides[0]),
-                        (now_t, then_t, st, weight_y * weight, sides[1]),
-                    ):
-                        total = now[x, r : r + 8, :] + now[x + 2, r : r + 8, :]
-                        total = total + (
-                            now[x + 1, r - 1 : r + 7, :] + now[x + 1, r + 1 : r + 9, :]
-                        )
-                        total = total + (left + right)
-                        then[x + 1, r : r + 8, :] = total * factor - source[x, t : t + 8, :]
-            return carry
-
-        lax.fori_loop(start, stop, turn, 0)
-
-    def pair(number, carry):
-        sweep(2 * number + 1, pms[0], pms[1], pts[0], pts[1])
-        sweep(2 * number + 2, pms[1], pms[0], pts[1], pts[0])
-        return carry
-
-    count = SWEEPS - 1
-    lax.fori_loop(0, count // 2, pair, 0)
-    if count % 2:
-        sweep(count, pms[0], pms[1], pts[0], pts[1])
-    pm, pt = pms[count % 2], pts[count % 2]
+            one = roll(ph[x // per], -(slot * k + HB), 1)
+            two = roll(sh[x // per], -(slot * k + HB), 1)
+            pt[x + 1, low:ZO, :] = one[:ZP]
+            pt[x + 1, end : end + ZP, :] = one[ZP:]
+            st[x, :ZP, :] = two[:ZP]
+            st[x, ZP + cells_z :, :] = two[ZP:]
+
+    def after(number, x, then_m, then_t):
+        for side, t in enumerate(inner_tiles(cells_z)):
+            then_m[x + 1, low + t : low + t + 8, :] = edge_m[number - 1, side, x]
+            then_t[x + 1, low + t : low + t + 8, :] = edge_t[number - 1, side, x]
+
+    tiles = (0, ZP, cells_z, ZP + cells_z)
+    done = run_sweeps(ax, ay, az, info, pms, pts, sm, st, cells_x, cells_z, tiles, after)
+    pm, pt = pms[done], pts[done]
+    first_lane = lanes_of((8, width)) == 0
+    last_lane = lanes_of((8, width)) == width - 1
+
+    def settle(x):
+        pm[x + 1, ZO + 8 : end - 8, :] = last_m[x, 8 : cells_z - 8, :]
+        pt[x + 1, ZO + 8 : end - 8, :] = last_t[x, 8 : cells_z - 8, :]
+
+    loop(ext, settle, 4)
 
     def gradient(x):
         at = x + off + 1
@@ -773,13 +854,21 @@
             [info, px, sx, *yr],
         )
         zr = az.swap(zsend, wide=True)
+        levels = (SWEEPS - 1, 2, ext_b, 8, width)
+        inner = call(
+            functools.partial(inner_kernel, ax, ay, az, pack_b, cells_x),
+            [levels, levels] + [(ext_b, cells_z, width)] * 4,
+            [info, px, sx, *yr],
+            scratch=[vm(ext_b + 2, tall, width)] * 4
+            + [vm(ext_b, cells_z + 2 * ZP, width)] * 2,
+        )
         outs = [(3, cells_x, cells_z, width), (cells_x, cells_z, width)]
         if not last:
             outs = outs + [(8, width)] + [xsize] * nx
         results = call(
             functools.partial(sweep_kernel, ax, ay, az, pack_b, last, turbines),
             outs,
-            [info, px, sx, star, inx, iny, *yr, *zr],
+            [info, px, sx, star, inx, iny, *inner, *zr],
             scratch=[
                 vm(ext_b + 2, tall, width),
                 vm(ext_b + 2, tall, width),
@@ -787,8 +876,8 @@
                 vm(ext_b + 2, tall, width),
                 vm(ext_b, cells_z + 2 * ZP, width),
                 vm(ext_b, cells_z + 2 * ZP, width),
-                vm(pack_b, cells_z + 2 * ZP, width),
-                vm(pack_b, cells_z + 2 * ZP, width),
+                vm(pack_b, 2 * ZP, width),
+                vm(pack_b, 2 * ZP, width),
             ],
         )
         vel, press = results[:2]

time: 120 us -> 117 us (0.975)
  waiting for transfers between devices: 37.1 us -> 26.2 us
  Pallas kernels: 41.6 us -> 49.6 us
    ppermute x20, waiting for transfers between devices: 27.2 us -> 16.8 us  [swap(): return [lax.ppermute(s, self.name, p) for s, p in zip(sends, perms)]]
    pallas_call x14 -> x16, Pallas kernels: 41.6 us -> 49.6 us  [call(): pl.pallas_call(kernel, out_shape=[jax.ShapeDtypeStruct(o, F32) for o in o...]
  transfers between devices with their start and end apart: 25 -> 25, of which waited for: 18 -> 14; matrix products, arithmetic and copies ran while one was open for 0% -> 0% of each run, Pallas kernels for 1% -> 12%
where the time goes in v5:
time: 117 us
  Pallas kernels  49.6 us (42%)
  starting transfers between devices  35.3 us (30%)
  waiting for transfers between devices  26.2 us (22%)
  local copies, waits for them, and re-layouts  3.75 us (3%)
  between operations  1.58 us (1%)
    pallas_call x16, Pallas kernels, call(): pl.pallas_call(kernel, out_shape=[jax.ShapeDtypeStruct(o, F32) for o in o...  49.6 us
    ppermute x20, starting transfers between devices, swap(): return [lax.ppermute(s, self.name, p) for s, p in zip(sends, perms)]  23.4 us
    ppermute x20, waiting for transfers between devices, swap(): return [lax.ppermute(s, self.name, p) for s, p in zip(sends, perms)]  16.8 us
    ppermute x2, waiting for transfers between devices, body(): cross = [lax.ppermute(parts, 'gz', az.cross)] if az.cross else []  5.42 us
    all_to_all x1, starting transfers between devices, body(): lax.all_to_all(packed.reshape(peers, block, width), ('gx', 'gy'), split_a...  4.36 us
    ppermute x2, starting transfers between devices, body(): cross = [lax.ppermute(parts, 'gz', az.cross)] if az.cross else []  4.13 us
    ppermute x2, waiting for transfers between devices, body(): cross = [lax.ppermute(parts, 'gy', ay.cross)] if ay.cross else []  4.01 us
    unnamed x27, local copies, waits for them, and re-layouts  3.75 us
  transfers between devices with their start and end apart: 25, of which 14 were waited for; matrix products, arithmetic and copies ran while one was open for 0% of the time, Pallas kernels for 12%

profile of v5, /device:TPU:12, one launch (start us, length us, event | category | flops | bytes accessed | tf_op | source)
XLA Modules:
  0.0 116.6 jit_solution(1273014692990927438)
XLA Ops:
  8.5 2.2 %shard_map.116 = f32[576,128]{1,0:T(8,128)} custom-call(s32[4]{0:T(128)S(1)} %pad_add_fusion.info, f32[256,128]{1,0:T(8,128)S(1)} %copy-done.4, s32[256,1]{1,0:T(8,128)S(1)} %copy.12.owners, s32[1,256]{1,0:T(1,128)S(1)} %bitcast.22, s32[1,256]{1,0:T(1,128)S(1)} %bitcast.23, f32[8,128]{1,0:T(8,128)S(1)} %get-tuple-element.58.parts.after), custom_call_target="tpu_custom_call" | custom-call | flops 433168 | bytes 433168 | tf_op jit(solution)/shard_map/pallas_call | solution.py:30
  10.6 4.4 %all-to-all-start = ((f32[8,72,128]{2,1,0:T(8,128)}), f32[8,72,128]{2,1,0:T(8,128)S(1)}, u32[]{:S(2)}, u32[]{:S(2)}) async-start(f32[8,72,128]{2,1,0:T(8,128)} %bitcast.8), calls=%async_computation | async-start | bytes 589824 | tf_op jit(solution)/shard_map/all_to_all | solution.py:807
  15.0 1.5 %collective-permute-start.1 = (f32[104,128]{1,0:T(8,128)S(1)}, f32[104,128]{1,0:T(8,128)S(1)}, u32[]{:S(2)}, u32[]{:S(2)}) collective-permute-start(f32[104,128]{1,0:T(8,128)S(1)} %get-tuple-element.59), channel_id=1, source_target_pairs={{0,4},{4,0},{8,12},{12,8},{1,5},{5,1},{9,13},{13,9},{2,6},{6,2},{1... | collective-permute-start | bytes 159752 | tf_op jit(solution)/shard_map/ppermute | solution.py:79
  16.5 2.0 %collective-permute-start.3 = (f32[8,128]{1,0:T(8,128)S(1)}, f32[8,128]{1,0:T(8,128)S(1)}, u32[]{:S(2)}, u32[]{:S(2)}) collective-permute-start(f32[8,128]{1,0:T(8,128)S(1)} %get-tuple-element.58.parts.after), channel_id=1, source_target_pairs={{0,8},{4,12},{8,0},{12,4},{1,9},{5,13},{9,1},{13,5},{2,10},{6,14},... | collective-permute-start | bytes 12296 | tf_op jit(solution)/shard_map/ppermute | solution.py:800
  18.5 1.8 %collective-permute-done.3.refs_3_ = f32[8,128]{1,0:T(8,128)S(1)} collective-permute-done((f32[8,128]{1,0:T(8,128)S(1)}, f32[8,128]{1,0:T(8,128)S(1)}, u32[]{:S(2)}, u32[]{:S(2)}) %collective-permute-start.3) | collective-permute-done | bytes 4128 | tf_op jit(solution)/shard_map/ppermute | solution.py:800
  20.3 2.2 %collective-permute-done.1.refs_1_ = f32[104,128]{1,0:T(8,128)S(1)} collective-permute-done((f32[104,128]{1,0:T(8,128)S(1)}, f32[104,128]{1,0:T(8,128)S(1)}, u32[]{:S(2)}, u32[]{:S(2)}) %collective-permute-start.1) | collective-permute-done | bytes 53280 | tf_op jit(solution)/shard_map/ppermute | solution.py:79
  24.2 2.7 %collective-permute-start.5 = (f32[104,128]{1,0:T(8,128)S(1)}, f32[104,128]{1,0:T(8,128)S(1)}, u32[]{:S(2)}, u32[]{:S(2)}) collective-permute-start(f32[104,128]{1,0:T(8,128)S(1)} %get-tuple-element.64), channel_id=1, source_target_pairs={{1,2},{3,0},{2,1},{0,3},{5,6},{7,4},{6,5},{4,7},{9,10},{11,8},{10,... | collective-permute-start | bytes 159752 | tf_op jit(solution)/shard_map/ppermute | solution.py:79
  28.1 3.3 %collective-permute-done.6.refs_5_ = f32[8,128]{1,0:T(8,128)S(1)} collective-permute-done((f32[8,128]{1,0:T(8,128)S(1)}, f32[8,128]{1,0:T(8,128)S(1)}, u32[]{:S(2)}, u32[]{:S(2)}) %collective-permute-start.6) | collective-permute-done | bytes 4128 | tf_op jit(solution)/shard_map/ppermute | solution.py:822
  31.4 6.3 %shard_map.117 = (f32[3,16,48,128]{3,2,1,0:T(8,128)S(1)}, f32[16,48,128]{2,1,0:T(8,128)S(1)}, f32[16,48,128]{2,1,0:T(8,128)S(1)}, f32[2,48,128]{2,1,0:T(8,128)S(1)}, f32[17,48,128]{2,1,0:T(8,128)S(1)}) custom-call(s32[4]{0:T(128)S(1)} %pad_add_fusion.info, f32[3,16,48,128]{3,2,1,0:T(8,128)S(1)} %copy-done.1, f32[16,48,128]{2,1,0:T(8,128)S(1)} %copy-done.3, ...), custom_call_target="tpu_custom_call" | custom-call | flops 4747472 | bytes 4747472 | tf_op jit(solution)/shard_map/pallas_call | solution.py:30
  37.8 1.7 %collective-permute-done.7.refs_0_ = f32[17,48,128]{2,1,0:T(8,128)S(1)} collective-permute-done((f32[17,48,128]{2,1,0:T(8,128)S(1)}, f32[17,48,128]{2,1,0:T(8,128)S(1)}, u32[]{:S(2)}, u32[]{:S(2)}) %collective-permute-start.7) | collective-permute-done | bytes 417824 | tf_op jit(solution)/shard_map/ppermute | solution.py:79
  41.1 2.5 %collective-permute-start.9 = (f32[144,128]{1,0:T(8,128)S(1)}, f32[144,128]{1,0:T(8,128)S(1)}, u32[]{:S(2)}, u32[]{:S(2)}) collective-permute-start(f32[144,128]{1,0:T(8,128)S(1)} %get-tuple-element.73), channel_id=1, source_target_pairs={{4,8},{12,0},{8,4},{0,12},{5,9},{13,1},{9,5},{1,13},{6,10},{14,2},... | collective-permute-start | bytes 221192 | tf_op jit(solution)/shard_map/ppermute | solution.py:79
  43.7 1.9 %collective-permute-done.8.refs_0_ = f32[144,128]{1,0:T(8,128)S(1)} collective-permute-done((f32[144,128]{1,0:T(8,128)S(1)}, f32[144,128]{1,0:T(8,128)S(1)}, u32[]{:S(2)}, u32[]{:S(2)}) %collective-permute-start.8) | collective-permute-done | bytes 73760 | tf_op jit(solution)/shard_map/ppermute | solution.py:79
  45.5 2.0 %collective-permute-done.9.refs_1_ = f32[144,128]{1,0:T(8,128)S(1)} collective-permute-done((f32[144,128]{1,0:T(8,128)S(1)}, f32[144,128]{1,0:T(8,128)S(1)}, u32[]{:S(2)}, u32[]{:S(2)}) %collective-permute-start.9) | collective-permute-done | bytes 73760 | tf_op jit(solution)/shard_map/ppermute | solution.py:79
  49.5 2.5 %collective-permute-start.11 = (f32[54,8,128]{2,1,0:T(8,128)S(1)}, f32[54,8,128]{2,1,0:T(8,128)S(1)}, u32[]{:S(2)}, u32[]{:S(2)}) collective-permute-start(f32[54,8,128]{2,1,0:T(8,128)S(1)} %get-tuple-element.81), channel_id=1, source_target_pairs={{1,2},{2,1},{5,6},{6,5},{9,10},{10,9},{13,14},{14,13},{17,18},{18,... | collective-permute-start | bytes 663560 | tf_op jit(solution)/shard_map/ppermute | solution.py:79
  52.1 6.9 %shard_map.119 = (f32[7,2,24,8,128]{4,3,2,1,0:T(8,128)S(1)}, f32[7,2,24,8,128]{4,3,2,1,0:T(8,128)S(1)}, f32[24,48,128]{2,1,0:T(8,128)S(1)}, f32[24,48,128]{2,1,0...) custom-call(s32[4]{0:T(128)S(1)} %pad_add_fusion.info, f32[24,48,128]{2,1,0:T(8,128)S(1)} %get-tuple-element.69.px, ...), custom_call_target="tpu_custom_call" | custom-call | flops 6438928 | bytes 6438928 | tf_op jit(solution)/shard_map/pallas_call | solution.py:30
  59.0 6.2 %shard_map.121 = (f32[3,16,48,128]{3,2,1,0:T(8,128)S(1)}, f32[16,48,128]{2,1,0:T(8,128)S(1)}, f32[8,128]{1,0:T(8,128)S(1)}, f32[392,128]{1,0:T(8,128)S(1)}) custom-call(s32[4]{0:T(128)S(1)} %pad_add_fusion.info, f32[24,48,128]{2,1,0:T(8,128)S(1)} %get-tuple-element.69.px, f32[24,48,128]{2,1,0:T(8,128)S(1)} %get-tuple-element.70.sx, ...), custom_call_target="tpu_custom_call" | custom-call | flops 9691536 | bytes 9691536 | tf_op jit(solution)/shard_map/pallas_call | solution.py:30
  65.3 1.4 %collective-permute-done.12.refs_0_ = f32[392,128]{1,0:T(8,128)S(1)} collective-permute-done((f32[392,128]{1,0:T(8,128)S(1)}, f32[392,128]{1,0:T(8,128)S(1)}, u32[]{:S(2)}, u32[]{:S(2)}) %collective-permute-start.12) | collective-permute-done | bytes 200736 | tf_op jit(solution)/shard_map/ppermute | solution.py:79
  68.6 1.5 %collective-permute-start.14 = (f32[104,128]{1,0:T(8,128)S(1)}, f32[104,128]{1,0:T(8,128)S(1)}, u32[]{:S(2)}, u32[]{:S(2)}) collective-permute-start(f32[104,128]{1,0:T(8,128)S(1)} %get-tuple-element.88), channel_id=1, source_target_pairs={{4,8},{12,0},{8,4},{0,12},{5,9},{13,1},{9,5},{1,13},{6,10},{14,2},... | collective-permute-start | bytes 159752 | tf_op jit(solution)/shard_map/ppermute | solution.py:79
  71.5 2.2 %collective-permute-done.15.refs_3_ = f32[8,128]{1,0:T(8,128)S(1)} collective-permute-done((f32[8,128]{1,0:T(8,128)S(1)}, f32[8,128]{1,0:T(8,128)S(1)}, u32[]{:S(2)}, u32[]{:S(2)}) %collective-permute-start.15) | collective-permute-done | bytes 4128 | tf_op jit(solution)/shard_map/ppermute | solution.py:800
  74.4 1.5 %collective-permute-start.17 = (f32[104,128]{1,0:T(8,128)S(1)}, f32[104,128]{1,0:T(8,128)S(1)}, u32[]{:S(2)}, u32[]{:S(2)}) collective-permute-start(f32[104,128]{1,0:T(8,128)S(1)} %get-tuple-element.92), channel_id=1, source_target_pairs={{1,2},{3,0},{2,1},{0,3},{5,6},{7,4},{6,5},{4,7},{9,10},{11,8},{10,... | collective-permute-start | bytes 159752 | tf_op jit(solution)/shard_map/ppermute | solution.py:79
  75.9 2.9 %collective-permute-start.18 = (f32[8,128]{1,0:T(8,128)S(1)}, f32[8,128]{1,0:T(8,128)S(1)}, u32[]{:S(2)}, u32[]{:S(2)}) collective-permute-start(f32[8,128]{1,0:T(8,128)S(1)} %get-tuple-element.89.parts), channel_id=1, source_target_pairs={{0,2},{1,3},{2,0},{3,1},{4,6},{5,7},{6,4},{7,5},{8,10},{9,11},{10,... | collective-permute-start | bytes 12296 | tf_op jit(solution)/shard_map/ppermute | solution.py:822
  78.8 2.2 %collective-permute-done.18.refs_5_ = f32[8,128]{1,0:T(8,128)S(1)} collective-permute-done((f32[8,128]{1,0:T(8,128)S(1)}, f32[8,128]{1,0:T(8,128)S(1)}, u32[]{:S(2)}, u32[]{:S(2)}) %collective-permute-start.18) | collective-permute-done | bytes 4128 | tf_op jit(solution)/shard_map/ppermute | solution.py:822
  80.9 6.3 %shard_map.124 = (f32[3,16,48,128]{3,2,1,0:T(8,128)S(1)}, f32[16,48,128]{2,1,0:T(8,128)S(1)}, f32[16,48,128]{2,1,0:T(8,128)S(1)}, f32[2,48,128]{2,1,0:T(8,128)S(1)}, f32[17,48,128]{2,1,0:T(8,128)S(1)}) custom-call(s32[4]{0:T(128)S(1)} %pad_add_fusion.info, f32[3,16,48,128]{3,2,1,0:T(8,128)S(1)} %get-tuple-element.82.vel, ...), custom_call_target="tpu_custom_call" | custom-call | flops 4747472 | bytes 4747472 | tf_op jit(solution)/shard_map/pallas_call | solution.py:30
  87.4 1.7 %collective-permute-done.19.refs_0_ = f32[17,48,128]{2,1,0:T(8,128)S(1)} collective-permute-done((f32[17,48,128]{2,1,0:T(8,128)S(1)}, f32[17,48,128]{2,1,0:T(8,128)S(1)}, u32[]{:S(2)}, u32[]{:S(2)}) %collective-permute-start.19) | collective-permute-done | bytes 417824 | tf_op jit(solution)/shard_map/ppermute | solution.py:79
  90.2 1.5 %collective-permute-start.20 = (f32[144,128]{1,0:T(8,128)S(1)}, f32[144,128]{1,0:T(8,128)S(1)}, u32[]{:S(2)}, u32[]{:S(2)}) collective-permute-start(f32[144,128]{1,0:T(8,128)S(1)} %get-tuple-element.100), channel_id=1, source_target_pairs={{0,4},{4,0},{8,12},{12,8},{1,5},{5,1},{9,13},{13,9},{2,6},{6,2},{1... | collective-permute-start | bytes 221192 | tf_op jit(solution)/shard_map/ppermute | solution.py:79
  91.7 1.5 %collective-permute-start.21 = (f32[144,128]{1,0:T(8,128)S(1)}, f32[144,128]{1,0:T(8,128)S(1)}, u32[]{:S(2)}, u32[]{:S(2)}) collective-permute-start(f32[144,128]{1,0:T(8,128)S(1)} %get-tuple-element.101), channel_id=1, source_target_pairs={{4,8},{12,0},{8,4},{0,12},{5,9},{13,1},{9,5},{1,13},{6,10},{14,2},... | collective-permute-start | bytes 221192 | tf_op jit(solution)/shard_map/ppermute | solution.py:79
  93.1 1.9 %collective-permute-done.20.refs_0_ = f32[144,128]{1,0:T(8,128)S(1)} collective-permute-done((f32[144,128]{1,0:T(8,128)S(1)}, f32[144,128]{1,0:T(8,128)S(1)}, u32[]{:S(2)}, u32[]{:S(2)}) %collective-permute-start.20) | collective-permute-done | bytes 73760 | tf_op jit(solution)/shard_map/ppermute | solution.py:79
  95.0 2.0 %collective-permute-done.21.refs_1_ = f32[144,128]{1,0:T(8,128)S(1)} collective-permute-done((f32[144,128]{1,0:T(8,128)S(1)}, f32[144,128]{1,0:T(8,128)S(1)}, u32[]{:S(2)}, u32[]{:S(2)}) %collective-permute-start.21) | collective-permute-done | bytes 73760 | tf_op jit(solution)/shard_map/ppermute | solution.py:79
  97.6 2.4 %collective-permute-start.22 = (f32[54,8,128]{2,1,0:T(8,128)S(1)}, f32[54,8,128]{2,1,0:T(8,128)S(1)}, u32[]{:S(2)}, u32[]{:S(2)}) collective-permute-start(f32[54,8,128]{2,1,0:T(8,128)S(1)} %get-tuple-element.108), channel_id=1, source_target_pairs={{0,1},{1,0},{2,3},{3,2},{4,5},{5,4},{6,7},{7,6},{8,9},{9,8},{10,11... | collective-permute-start | bytes 663560 | tf_op jit(solution)/shard_map/ppermute | solution.py:79
  100.0 2.5 %collective-permute-start.23 = (f32[54,8,128]{2,1,0:T(8,128)S(1)}, f32[54,8,128]{2,1,0:T(8,128)S(1)}, u32[]{:S(2)}, u32[]{:S(2)}) collective-permute-start(f32[54,8,128]{2,1,0:T(8,128)S(1)} %get-tuple-element.109), channel_id=1, source_target_pairs={{1,2},{2,1},{5,6},{6,5},{9,10},{10,9},{13,14},{14,13},{17,18},{18,... | collective-permute-start | bytes 663560 | tf_op jit(solution)/shard_map/ppermute | solution.py:79
  102.5 6.9 %shard_map.126 = (f32[7,2,24,8,128]{4,3,2,1,0:T(8,128)S(1)}, f32[7,2,24,8,128]{4,3,2,1,0:T(8,128)S(1)}, f32[24,48,128]{2,1,0:T(8,128)S(1)}, f32[24,48,128]{2,1,0...) custom-call(s32[4]{0:T(128)S(1)} %pad_add_fusion.info, f32[24,48,128]{2,1,0:T(8,128)S(1)} %get-tuple-element.97.px, ...), custom_call_target="tpu_custom_call" | custom-call | flops 6438928 | bytes 6438928 | tf_op jit(solution)/shard_map/pallas_call | solution.py:30
  109.4 7.1 %shard_map.128 = (f32[3,16,48,128]{3,2,1,0:T(8,128)}, f32[16,48,128]{2,1,0:T(8,128)}) custom-call(s32[4]{0:T(128)S(1)} %pad_add_fusion.info, f32[24,48,128]{2,1,0:T(8,128)S(1)} %get-tuple-element.97.px, f32[24,48,128]{2,1,0:T(8,128)S(1)} %get-tuple-element.98.sx, f32[3,16,48,128]{3,2,1,0:T(8,128)S(1)} %get-tuple-element.99.star, s32[1,48]{1,0:T(1,128)S(1)} %bitcast.16, ...), custom_call_target="tpu_custom_call" | custom-call | flops 9486736 | bytes 9486736 | tf_op jit(solution)/shard_map/pallas_call | solution.py:30
  (62 shorter events, 19.5 us)
Async XLA Ops:
  0.6 5.2 %copy-start.12 = (s32[256,1]{0,1:T(1,128)S(1)}, s32[256,1]{0,1:T(1,128)}, u32[]{:S(2)}) copy-start(s32[256,1]{0,1:T(1,128)} %param.13) | copy-start | bytes 3076
  5.7 2.7 %copy-start.4 = (f32[256,128]{1,0:T(8,128)S(1)}, f32[256,128]{1,0:T(8,128)}, u32[]{:S(2)}) copy-start(f32[256,128]{1,0:T(8,128)} %kern.1) | copy-start | bytes 393220
  5.7 2.8 %copy-start.10 = (s32[256]{0:T(256)S(1)}, s32[256]{0:T(256)}, u32[]{:S(2)}) copy-start(s32[256]{0:T(256)} %param.14) | copy-start | bytes 3076
  5.7 2.8 %copy-start.11 = (s32[256]{0:T(256)S(1)}, s32[256]{0:T(256)}, u32[]{:S(2)}) copy-start(s32[256]{0:T(256)} %param.15) | copy-start | bytes 3076
  5.7 1.5 %collective-permute-start = (f32[392,128]{1,0:T(8,128)S(1)}, f32[392,128]{1,0:T(8,128)S(1)}, u32[]{:S(2)}, u32[]{:S(2)}) collective-permute-start(f32[392,128]{1,0:T(8,128)S(1)} %get-tuple-element.57), channel_id=1, source_target_pairs={{0,16},{16,0},{1,17},{17,1},{2,18},{18,2},{3,19},{19,3},{4,20},{20... | collective-permute-start | bytes 602120 | tf_op jit(solution)/shard_map/ppermute | solution.py:79
  10.6 20.8 %copy-start.9 = (f32[48]{0:T(128)S(1)}, f32[48]{0:T(128)}, u32[]{:S(2)}) copy-start(f32[48]{0:T(128)} %param.17) | copy-start | bytes 580
  10.6 20.8 %all-to-all-start = ((f32[8,72,128]{2,1,0:T(8,128)}), f32[8,72,128]{2,1,0:T(8,128)S(1)}, u32[]{:S(2)}, u32[]{:S(2)}) async-start(f32[8,72,128]{2,1,0:T(8,128)} %bitcast.8), calls=%async_computation | async-start | bytes 589824 | tf_op jit(solution)/shard_map/all_to_all | solution.py:807
  15.0 7.5 %collective-permute-start.1 = (f32[104,128]{1,0:T(8,128)S(1)}, f32[104,128]{1,0:T(8,128)S(1)}, u32[]{:S(2)}, u32[]{:S(2)}) collective-permute-start(f32[104,128]{1,0:T(8,128)S(1)} %get-tuple-element.59), channel_id=1, source_target_pairs={{0,4},{4,0},{8,12},{12,8},{1,5},{5,1},{9,13},{13,9},{2,6},{6,2},{1... | collective-permute-start | bytes 159752 | tf_op jit(solution)/shard_map/ppermute | solution.py:79
  16.5 6.6 %collective-permute-start.2 = (f32[104,128]{1,0:T(8,128)S(1)}, f32[104,128]{1,0:T(8,128)S(1)}, u32[]{:S(2)}, u32[]{:S(2)}) collective-permute-start(f32[104,128]{1,0:T(8,128)S(1)} %get-tuple-element.60), channel_id=1, source_target_pairs={{4,8},{12,0},{8,4},{0,12},{5,9},{13,1},{9,5},{1,13},{6,10},{14,2},... | collective-permute-start | bytes 159752 | tf_op jit(solution)/shard_map/ppermute | solution.py:79
  16.5 3.8 %collective-permute-start.3 = (f32[8,128]{1,0:T(8,128)S(1)}, f32[8,128]{1,0:T(8,128)S(1)}, u32[]{:S(2)}, u32[]{:S(2)}) collective-permute-start(f32[8,128]{1,0:T(8,128)S(1)} %get-tuple-element.58.parts.after), channel_id=1, source_target_pairs={{0,8},{4,12},{8,0},{12,4},{1,9},{5,13},{9,1},{13,5},{2,10},{6,14},... | collective-permute-start | bytes 12296 | tf_op jit(solution)/shard_map/ppermute | solution.py:800
  23.7 7.7 %collective-permute-start.4 = (f32[104,128]{1,0:T(8,128)S(1)}, f32[104,128]{1,0:T(8,128)S(1)}, u32[]{:S(2)}, u32[]{:S(2)}) collective-permute-start(f32[104,128]{1,0:T(8,128)S(1)} %get-tuple-element.63), channel_id=1, source_target_pairs={{0,1},{1,0},{2,3},{3,2},{4,5},{5,4},{6,7},{7,6},{8,9},{9,8},{10,11... | collective-permute-start | bytes 159752 | tf_op jit(solution)/shard_map/ppermute | solution.py:79
  24.2 7.2 %collective-permute-start.5 = (f32[104,128]{1,0:T(8,128)S(1)}, f32[104,128]{1,0:T(8,128)S(1)}, u32[]{:S(2)}, u32[]{:S(2)}) collective-permute-start(f32[104,128]{1,0:T(8,128)S(1)} %get-tuple-element.64), channel_id=1, source_target_pairs={{1,2},{3,0},{2,1},{0,3},{5,6},{7,4},{6,5},{4,7},{9,10},{11,8},{10,... | collective-permute-start | bytes 159752 | tf_op jit(solution)/shard_map/ppermute | solution.py:79
  26.9 4.5 %collective-permute-start.6 = (f32[8,128]{1,0:T(8,128)S(1)}, f32[8,128]{1,0:T(8,128)S(1)}, u32[]{:S(2)}, u32[]{:S(2)}) collective-permute-start(f32[8,128]{1,0:T(8,128)S(1)} %get-tuple-element.61.parts), channel_id=1, source_target_pairs={{0,2},{1,3},{2,0},{3,1},{4,6},{5,7},{6,4},{7,5},{8,10},{9,11},{10,... | collective-permute-start | bytes 12296 | tf_op jit(solution)/shard_map/ppermute | solution.py:822
  37.8 1.8 %collective-permute-start.7 = (f32[17,48,128]{2,1,0:T(8,128)S(1)}, f32[17,48,128]{2,1,0:T(8,128)S(1)}, u32[]{:S(2)}, u32[]{:S(2)}) collective-permute-start(f32[17,48,128]{2,1,0:T(8,128)S(1)} %get-tuple-element.68), channel_id=1, source_target_pairs={{0,16},{16,0},{1,17},{17,1},{2,18},{18,2},{3,19},{19,3},{4,20},{20... | collective-permute-start | bytes 1253384 | tf_op jit(solution)/shard_map/ppermute | solution.py:79
  40.7 4.9 %collective-permute-start.8 = (f32[144,128]{1,0:T(8,128)S(1)}, f32[144,128]{1,0:T(8,128)S(1)}, u32[]{:S(2)}, u32[]{:S(2)}) collective-permute-start(f32[144,128]{1,0:T(8,128)S(1)} %get-tuple-element.72), channel_id=1, source_target_pairs={{0,4},{4,0},{8,12},{12,8},{1,5},{5,1},{9,13},{13,9},{2,6},{6,2},{1... | collective-permute-start | bytes 221192 | tf_op jit(solution)/shard_map/ppermute | solution.py:79
  41.1 6.4 %collective-permute-start.9 = (f32[144,128]{1,0:T(8,128)S(1)}, f32[144,128]{1,0:T(8,128)S(1)}, u32[]{:S(2)}, u32[]{:S(2)}) collective-permute-start(f32[144,128]{1,0:T(8,128)S(1)} %get-tuple-element.73), channel_id=1, source_target_pairs={{4,8},{12,0},{8,4},{0,12},{5,9},{13,1},{9,5},{1,13},{6,10},{14,2},... | collective-permute-start | bytes 221192 | tf_op jit(solution)/shard_map/ppermute | solution.py:79
  47.5 11.5 %copy-start.6 = (s32[48]{0:T(128)S(1)}, s32[48]{0:T(128)}, u32[]{:S(2)}) copy-start(s32[48]{0:T(128)} %param.18) | copy-start | bytes 580
  47.5 11.5 %copy-start.8 = (s32[48]{0:T(128)S(1)}, s32[48]{0:T(128)}, u32[]{:S(2)}) copy-start(s32[48]{0:T(128)} %param.19) | copy-start | bytes 580
  48.1 10.8 %collective-permute-start.10 = (f32[54,8,128]{2,1,0:T(8,128)S(1)}, f32[54,8,128]{2,1,0:T(8,128)S(1)}, u32[]{:S(2)}, u32[]{:S(2)}) collective-permute-start(f32[54,8,128]{2,1,0:T(8,128)S(1)} %get-tuple-element.80), channel_id=1, source_target_pairs={{0,1},{1,0},{2,3},{3,2},{4,5},{5,4},{6,7},{7,6},{8,9},{9,8},{10,11... | collective-permute-start | bytes 663560 | tf_op jit(solution)/shard_map/ppermute | solution.py:79
  49.5 9.4 %collective-permute-start.11 = (f32[54,8,128]{2,1,0:T(8,128)S(1)}, f32[54,8,128]{2,1,0:T(8,128)S(1)}, u32[]{:S(2)}, u32[]{:S(2)}) collective-permute-start(f32[54,8,128]{2,1,0:T(8,128)S(1)} %get-tuple-element.81), channel_id=1, source_target_pairs={{1,2},{2,1},{5,6},{6,5},{9,10},{10,9},{13,14},{14,13},{17,18},{18,... | collective-permute-start | bytes 663560 | tf_op jit(solution)/shard_map/ppermute | solution.py:79
  65.3 1.5 %collective-permute-start.12 = (f32[392,128]{1,0:T(8,128)S(1)}, f32[392,128]{1,0:T(8,128)S(1)}, u32[]{:S(2)}, u32[]{:S(2)}) collective-permute-start(f32[392,128]{1,0:T(8,128)S(1)} %get-tuple-element.85), channel_id=1, source_target_pairs={{0,16},{16,0},{1,17},{17,1},{2,18},{18,2},{3,19},{19,3},{4,20},{20... | collective-permute-start | bytes 602120 | tf_op jit(solution)/shard_map/ppermute | solution.py:79
  68.0 5.7 %collective-permute-start.13 = (f32[104,128]{1,0:T(8,128)S(1)}, f32[104,128]{1,0:T(8,128)S(1)}, u32[]{:S(2)}, u32[]{:S(2)}) collective-permute-start(f32[104,128]{1,0:T(8,128)S(1)} %get-tuple-element.87), channel_id=1, source_target_pairs={{0,4},{4,0},{8,12},{12,8},{1,5},{5,1},{9,13},{13,9},{2,6},{6,2},{1... | collective-permute-start | bytes 159752 | tf_op jit(solution)/shard_map/ppermute | solution.py:79
  68.6 5.1 %collective-permute-start.14 = (f32[104,128]{1,0:T(8,128)S(1)}, f32[104,128]{1,0:T(8,128)S(1)}, u32[]{:S(2)}, u32[]{:S(2)}) collective-permute-start(f32[104,128]{1,0:T(8,128)S(1)} %get-tuple-element.88), channel_id=1, source_target_pairs={{4,8},{12,0},{8,4},{0,12},{5,9},{13,1},{9,5},{1,13},{6,10},{14,2},... | collective-permute-start | bytes 159752 | tf_op jit(solution)/shard_map/ppermute | solution.py:79
  70.1 3.6 %collective-permute-start.15 = (f32[8,128]{1,0:T(8,128)S(1)}, f32[8,128]{1,0:T(8,128)S(1)}, u32[]{:S(2)}, u32[]{:S(2)}) collective-permute-start(f32[8,128]{1,0:T(8,128)S(1)} %get-tuple-element.86.parts), channel_id=1, source_target_pairs={{0,8},{4,12},{8,0},{12,4},{1,9},{5,13},{9,1},{13,5},{2,10},{6,14},... | collective-permute-start | bytes 12296 | tf_op jit(solution)/shard_map/ppermute | solution.py:800
  74.3 6.6 %collective-permute-start.16 = (f32[104,128]{1,0:T(8,128)S(1)}, f32[104,128]{1,0:T(8,128)S(1)}, u32[]{:S(2)}, u32[]{:S(2)}) collective-permute-start(f32[104,128]{1,0:T(8,128)S(1)} %get-tuple-element.91), channel_id=1, source_target_pairs={{0,1},{1,0},{2,3},{3,2},{4,5},{5,4},{6,7},{7,6},{8,9},{9,8},{10,11... | collective-permute-start | bytes 159752 | tf_op jit(solution)/shard_map/ppermute | solution.py:79
  74.4 6.5 %collective-permute-start.17 = (f32[104,128]{1,0:T(8,128)S(1)}, f32[104,128]{1,0:T(8,128)S(1)}, u32[]{:S(2)}, u32[]{:S(2)}) collective-permute-start(f32[104,128]{1,0:T(8,128)S(1)} %get-tuple-element.92), channel_id=1, source_target_pairs={{1,2},{3,0},{2,1},{0,3},{5,6},{7,4},{6,5},{4,7},{9,10},{11,8},{10,... | collective-permute-start | bytes 159752 | tf_op jit(solution)/shard_map/ppermute | solution.py:79
  75.9 5.0 %collective-permute-start.18 = (f32[8,128]{1,0:T(8,128)S(1)}, f32[8,128]{1,0:T(8,128)S(1)}, u32[]{:S(2)}, u32[]{:S(2)}) collective-permute-start(f32[8,128]{1,0:T(8,128)S(1)} %get-tuple-element.89.parts), channel_id=1, source_target_pairs={{0,2},{1,3},{2,0},{3,1},{4,6},{5,7},{6,4},{7,5},{8,10},{9,11},{10,... | collective-permute-start | bytes 12296 | tf_op jit(solution)/shard_map/ppermute | solution.py:822
  87.3 1.8 %collective-permute-start.19 = (f32[17,48,128]{2,1,0:T(8,128)S(1)}, f32[17,48,128]{2,1,0:T(8,128)S(1)}, u32[]{:S(2)}, u32[]{:S(2)}) collective-permute-start(f32[17,48,128]{2,1,0:T(8,128)S(1)} %get-tuple-element.96), channel_id=1, source_target_pairs={{0,16},{16,0},{1,17},{17,1},{2,18},{18,2},{3,19},{19,3},{4,20},{20... | collective-permute-start | bytes 1253384 | tf_op jit(solution)/shard_map/ppermute | solution.py:79
  90.2 4.9 %collective-permute-start.20 = (f32[144,128]{1,0:T(8,128)S(1)}, f32[144,128]{1,0:T(8,128)S(1)}, u32[]{:S(2)}, u32[]{:S(2)}) collective-permute-start(f32[144,128]{1,0:T(8,128)S(1)} %get-tuple-element.100), channel_id=1, source_target_pairs={{0,4},{4,0},{8,12},{12,8},{1,5},{5,1},{9,13},{13,9},{2,6},{6,2},{1... | collective-permute-start | bytes 221192 | tf_op jit(solution)/shard_map/ppermute | solution.py:79
  91.7 5.4 %collective-permute-start.21 = (f32[144,128]{1,0:T(8,128)S(1)}, f32[144,128]{1,0:T(8,128)S(1)}, u32[]{:S(2)}, u32[]{:S(2)}) collective-permute-start(f32[144,128]{1,0:T(8,128)S(1)} %get-tuple-element.101), channel_id=1, source_target_pairs={{4,8},{12,0},{8,4},{0,12},{5,9},{13,1},{9,5},{1,13},{6,10},{14,2},... | collective-permute-start | bytes 221192 | tf_op jit(solution)/shard_map/ppermute | solution.py:79
  97.6 11.8 %collective-permute-start.22 = (f32[54,8,128]{2,1,0:T(8,128)S(1)}, f32[54,8,128]{2,1,0:T(8,128)S(1)}, u32[]{:S(2)}, u32[]{:S(2)}) collective-permute-start(f32[54,8,128]{2,1,0:T(8,128)S(1)} %get-tuple-element.108), channel_id=1, source_target_pairs={{0,1},{1,0},{2,3},{3,2},{4,5},{5,4},{6,7},{7,6},{8,9},{9,8},{10,11... | collective-permute-start | bytes 663560 | tf_op jit(solution)/shard_map/ppermute | solution.py:79
  100.0 9.4 %collective-permute-start.23 = (f32[54,8,128]{2,1,0:T(8,128)S(1)}, f32[54,8,128]{2,1,0:T(8,128)S(1)}, u32[]{:S(2)}, u32[]{:S(2)}) collective-permute-start(f32[54,8,128]{2,1,0:T(8,128)S(1)} %get-tuple-element.109), channel_id=1, source_target_pairs={{1,2},{2,1},{5,6},{6,5},{9,10},{10,9},{13,14},{14,13},{17,18},{18,... | collective-permute-start | bytes 663560 | tf_op jit(solution)/shard_map/ppermute | solution.py:79
  (6 other events, 8.2 us)

commit v6 on v5

--- a/solution.py
+++ b/solution.py
@@ -22,19 +22,21 @@
 BF16 = jnp.bfloat16
 
 
-def call(kernel, outs, args, smem=(0,), scratch=()):
+def call(kernel, outs, args, smem=(0,), scratch=(), types=None):
     specs = [
         pl.BlockSpec(memory_space=pltpu.SMEM if i in smem else pltpu.VMEM) for i in range(len(args))
     ]
     size = sum(a.size * 4 for a in args) + sum(math.prod(o) * 4 for o in outs)
     return pl.pallas_call(
         kernel,
-        out_shape=[jax.ShapeDtypeStruct(o, F32) for o in outs],
+        out_shape=[
+            jax.ShapeDtypeStruct(o, t) for o, t in zip(outs, types or [F32] * len(outs))
+        ],
         in_specs=specs,
         out_specs=[pl.BlockSpec(memory_space=pltpu.VMEM)] * len(outs),
         scratch_shapes=list(scratch),
         cost_estimate=pl.CostEstimate(flops=size, bytes_accessed=size, transcendentals=0),
-        compiler_params=pltpu.CompilerParams(vmem_limit_bytes=24 << 20),
+        compiler_params=pltpu.CompilerParams(vmem_limit_bytes=16 << 20),
     )(*args)
 
 
@@ -299,42 +301,115 @@
         out[pad:, :] = total
 
 
-def force_field(rows, thrust, total, depth_total, peers, capacity, lines_total):
-    turbines = thrust.shape[0]
-    width = rows.shape[-1]
-    slots = peers * capacity
+def prepare_kernel(peers, capacity, info, rows, values, landing, pick):
     block = capacity + 8
-    uref = total / (BAND * depth_total)
-    magnitude = 0.5 * thrust * uref * jnp.abs(uref)
-    magnitude = jnp.broadcast_to(magnitude, (turbines, width))
-    mag_parts = split3(magnitude)
-    force = jnp.zeros((lines_total, width), F32)
+    lines_total, slots = landing.shape
+    for peer in range(peers):
+        values[peer * capacity : (peer + 1) * capacity, :] = rows[
+            peer * block : peer * block + capacity, :
+        ]
+    square = (128, 128)
     for first in range(0, slots, 128):
         line = jnp.zeros((8, 128), F32)
-        values = []
-        for at in range(first, min(first + 128, slots), capacity):
+        for at in range(first, first + 128, capacity):
             peer = at // capacity
             line = line + roll(
                 rows[peer * block + capacity : (peer + 1) * block, :], at - first, 1
             )
-            values.append(rows[peer * block : peer * block + capacity, :])
-        values = jnp.concatenate(values, axis=0) if len(values) > 1 else values[0]
-        used = values.shape[0]
         line = line.astype(jnp.int32)
-        turbine = line[1:2, :used]
-        line = line[0:1, :used]
-        chosen = (rows_of((turbines, used)) == turbine).astype(BF16)
-        scale = sum(dot0(chosen, part) for part in mag_parts)
-        values = split3(values * scale)
-        landing = (rows_of((lines_total, used)) == line - 1).astype(BF16)
-        for part in values[:2]:
-            force = force + jnp.dot(landing, part, preferred_element_type=F32)
-    return force
-
-
-def star_kernel(ax, ay, az, peers, capacity, turbines, info, vel, press, parts, rows, thrust, own_v, *refs):
+        chosen = jnp.where(rows_of(square) == line[1:2, :], 1.0, 0.0)
+        pick[first : first + 128, :] = chosen.T.astype(BF16)
+        place = rows_of((lines_total, 128)) == line[0:1, :] - 1
+        landing[:, first : first + 128] = jnp.where(place, 1.0, 0.0).astype(BF16)
+
+
+def force_field(values, landing, pick, thrust, total, depth_total):
+    uref = total / (BAND * depth_total)
+    magnitude = jnp.broadcast_to(0.5 * thrust * uref * jnp.abs(uref), (128, values.shape[-1]))
+    pick = pick[...]
+    scale = sum(
+        jnp.dot(pick, part, preferred_element_type=F32) for part in split3(magnitude)
+    )
+    landing = landing[...]
+    parts = split3(values[...] * scale)[:2]
+    return sum(jnp.dot(landing, part, preferred_element_type=F32) for part in parts)
+
+
+def stencil(fm, hm):
+    width = fm.shape[-1]
+    lane = lanes_of((8, width))
+    slot = 2 * HA
+    rate = TIME_STEP * VISCOSITY
+
+    def turn(xe):
+        return (width - HA) - slot * xe + jnp.where(slot * xe + HA > width, width, 0)
+
+    def sides(mid, packed, xe):
+        far = roll_by(packed, turn(xe))
+        left = roll(jnp.where(lane == width - 1, far, mid), 1, 1)
+        right = roll(jnp.where(lane == 0, far, mid), -1, 1)
+        return left, right
+
+    def around(f, xe, r):
+        mid = fm[f, xe, r : r + 8, :]
+        total = fm[f, xe - 1, r : r + 8, :] + fm[f, xe + 1, r : r + 8, :]
+        total = total + (fm[f, xe, r - 1 : r + 7, :] + fm[f, xe, r + 1 : r + 9, :])
+        left, right = sides(mid, hm[f, r : r + 8, :], xe)
+        return total + (left + right), mid
+
+    def diffused(f, xe, r):
+        total, mid = around(f, xe, r)
+        return mid + rate * (total - 6.0 * mid)
+
+    return sides, around, diffused
+
+
+def calm_kernel(ax, ay, info, vel, press, *refs):
+    nx, ny = len(ax.perms), len(ay.perms)
+    xr, refs = refs[:nx], refs[nx:]
+    yr, refs = refs[:ny], refs[ny:]
+    su, sv, sw, sp, fm, hm = refs
+    _, cells_x, cells_z, _ = vel.shape
+    ext = cells_x + 2 * HA
+    halo = x_halo(info, ax.count, xr, cells_x, cells_z)
+    end = ZO + cells_z
+    for f in range(4):
+        for xe in range(ext):
+            if f == 0 or 0 < xe < ext - 1:
+                fm[f, xe, ZO:end, :] = ext_plane(vel, press, halo, f, xe, cells_x)
+    for i in range(2):
+        pieces = [r[i * cells_z : (i + 1) * cells_z, :] for r in yr]
+        lower, upper = from_sides(info[1], ay.count, pieces, 0.0)
+        one, two = split_edges(lower, upper, HA)
+        hm[2 * i, ZO:end, :] = one
+        hm[2 * i + 1, ZO:end, :] = two
+    _, around, diffused = stencil(fm, hm)
+    middle = range(8, cells_z - 8, 8)
+
+    def u_plane(k):
+        for t in middle:
+            su[k, t : t + 8, :] = diffused(0, k + 1, ZO + t)
+
+    def rest(x):
+        for t in middle:
+            sv[x, t : t + 8, :] = diffused(1, x + HA, ZO + t)
+        for t in middle:
+            sw[x, t : t + 8, :] = diffused(2, x + HA, ZO + t)
+        for t in middle:
+            sp[x, t : t + 8, :] = around(3, x + HA, ZO + t)[0] * (1.0 / 6.0)
+
+    loop(cells_x + 2, u_plane, 3)
+    loop(cells_x, rest, 2)
+
+
+def star_kernel(
+    ax, ay, az, ready, info, vel, press, parts, values, landing, pick, thrust, own_v, *refs
+):
     nx, ny, nz = len(ax.perms), len(ay.perms), len(az.perms)
     ncross = 1 if az.cross else 0
+    if ready:
+        su0, sv0, sw0, sp0 = refs[:4]
+        refs = refs[4:]
     xr, refs = refs[:nx], refs[nx:]
     yr, refs = refs[:ny], refs[ny:]
     zr, refs = refs[:nz], refs[nz:]
@@ -348,20 +423,24 @@
     for c in cross:
         total = total + c[...]
     force_ref[...] = force_field(
-        rows,
-        column_of(thrust[...], turbines),
-        column_of(total, turbines),
+        values,
+        landing,
+        pick,
+        column_of(thrust[...], 128),
+        column_of(total, 128),
         cells_z * az.count,
-        peers,
-        capacity,
-        cells_x * cells_z,
     )
     halo = x_halo(info, ax.count, xr, cells_x, cells_z)
     end = ZO + cells_z
     for f in range(4):
         for xe in range(ext):
             if f == 0 or 0 < xe < ext - 1:
-                fm[f, xe, ZO:end, :] = ext_plane(vel, press, halo, f, xe, cells_x)
+                value = ext_plane(vel, press, halo, f, xe, cells_x)
+                if ready:
+                    fm[f, xe, ZO : ZO + 16, :] = value[:16]
+                    fm[f, xe, end - 16 : end, :] = value[cells_z - 16 :]
+                else:
+                    fm[f, xe, ZO:end, :] = value
     table, corner = z_table(cells_x)
     for f, xe, depth, at in table:
         lower, upper = from_sides(info[2], az.count, [r[at : at + depth, :] for r in zr], 0.0)
@@ -391,24 +470,13 @@
     lane = lanes_of((8, width))
     slot = 2 * HA
 
-    def turn(xe):
-        return (width - HA) - slot * xe + jnp.where(slot * xe + HA > width, width, 0)
-
-    def around(f, xe, r):
-        mid = fm[f, xe, r : r + 8, :]
-        far = roll_by(hm[f, r : r + 8, :], turn(xe))
-        total = fm[f, xe - 1, r : r + 8, :] + fm[f, xe + 1, r : r + 8, :]
-        total = total + (fm[f, xe, r - 1 : r + 7, :] + fm[f, xe, r + 1 : r + 9, :])
-        left = roll(jnp.where(lane == width - 1, far, mid), 1, 1)
-        right = roll(jnp.where(lane == 0, far, mid), -1, 1)
-        return total + (left + right), mid
-
-    def diffused(f, xe, r):
-        total, mid = around(f, xe, r)
-        return mid + rate * (total - 6.0 * mid)
+    sides, around, diffused = stencil(fm, hm)
+    outer = (0, cells_z - 8) if ready else range(0, cells_z, 8)
 
     def u_plane(k):
-        for t in range(0, cells_z, 8):
+        if ready:
+            su[k, 8 : cells_z - 8, :] = su0[k, 8 : cells_z - 8, :]
+        for t in outer:
             su[k, t : t + 8, :] = diffused(0, k + 1, ZO + t)
 
     loop(cells_x + 2, u_plane, 3)
@@ -434,7 +502,10 @@
             su[x + 1, t : t + 8, :] = u
             star[0, x, t : t + 8, :] = u
         for t in range(-8, cells_z + 8, 8):
-            w = diffused(2, xe, ZO + t)
+            if ready and 0 < t < cells_z - 8:
+                w = sw0[x, t : t + 8, :]
+            else:
+                w = diffused(2, xe, ZO + t)
             if t < 0:
                 w = jnp.where(info[2] > 0, w, 0.0)
             elif t >= cells_z:
@@ -443,11 +514,9 @@
                 star[2, x, t : t + 8, :] = w
             sw[x, t + 8 : t + 16, :] = w
         for t in range(0, cells_z, 8):
-            v = diffused(1, xe, ZO + t)
+            v = diffused(1, xe, ZO + t) if t in outer else sv0[x, t : t + 8, :]
             star[1, x, t : t + 8, :] = v
-            far = roll_by(svh[t : t + 8, :], turn(xe))
-            left = roll(jnp.where(lane == width - 1, far, v), 1, 1)
-            right = roll(jnp.where(lane == 0, far, v), -1, 1)
+            left, right = sides(v, svh[t : t + 8, :], xe)
             s6[x, t : t + 8, :] = right - left
 
     loop(cells_x, forced, 2)
@@ -458,8 +527,11 @@
             source = source + (su[x + 2, t : t + 8, :] - su[x, t : t + 8, :])
             source = source * (0.5 / 6.0)
             s6[x, t : t + 8, :] = source
-            total, _ = around(3, x + HA, ZO + t)
-            p1[x, t : t + 8, :] = total * (1.0 / 6.0) - source
+            if t in outer:
+                mean = around(3, x + HA, ZO + t)[0] * (1.0 / 6.0)
+            else:
+                mean = sp0[x, t : t + 8, :]
+            p1[x, t : t + 8, :] = mean - source
 
     loop(cells_x, first, 4)
     scale = 0.5 * TIME_STEP / 6.0
@@ -820,10 +892,29 @@
         )
         zr = az.swap(zsend)
         cross = [lax.ppermute(parts, "gz", az.cross)] if az.cross else []
+        if repeat == 0:
+            prepared = call(
+                functools.partial(prepare_kernel, peers, capacity),
+                [
+                    (peers * capacity, width),
+                    (cells_x * cells_z, peers * capacity),
+                    (peers * capacity, 128),
+                ],
+                [info, rows],
+                types=(F32, BF16, BF16),
+            )
+        calm = []
+        if repeat > 0:
+            calm = call(
+                functools.partial(calm_kernel, ax, ay),
+                [(cells_x + 2, cells_z, width)] + [(cells_x, cells_z, width)] * 3,
+                [info, vel, press, *xr, *yr],
+                scratch=[vm(4, ext_a, tall, width), vm(4, tall, width)],
+            )
         if not az.fold:
             parts = lax.psum(parts, "gz")
         star, p1, s6, edge, *xsend = call(
-            functools.partial(star_kernel, ax, ay, az, peers, capacity, turbines),
+            functools.partial(star_kernel, ax, ay, az, bool(calm)),
             [
                 (3, cells_x, cells_z, width),
                 (cells_x, cells_z, width),
@@ -831,7 +922,7 @@
                 (2, cells_z, width),
             ]
             + [(2 * HB + 1, cells_z, width)] * nx,
-            [info, vel, press, parts, rows, push, own_v, *xr, *yr, *zr, *cross],
+            [info, vel, press, parts, *prepared, push, own_v, *calm, *xr, *yr, *zr, *cross],
             scratch=[
                 vm(4, ext_a, tall, width),
                 vm(4, tall, width),

time: 117 us -> 115 us (0.983)
  waiting for transfers between devices: 26.2 us -> 23 us
  Pallas kernels: 49.6 us -> 52.3 us
  starting transfers between devices: 35.3 us -> 34.1 us
    ppermute x2, waiting for transfers between devices: 5.42 us -> 2.22 us  [body(): cross = [lax.ppermute(parts, 'gz', az.cross)] if az.cross else []]
    pallas_call x16 -> x18, Pallas kernels: 49.6 us -> 52.3 us  [call(): pl.pallas_call(kernel, out_shape=[jax.ShapeDtypeStruct(o, t) for o, t in...]
  transfers between devices with their start and end apart: 25 -> 25, of which waited for: 14 -> 13; matrix products, arithmetic and copies ran while one was open for 0% -> 0% of each run, Pallas kernels for 12% -> 16%
where the time goes in v6:
time: 115 us
  Pallas kernels  52.3 us (45%)
  starting transfers between devices  34.1 us (30%)
  waiting for transfers between devices  23 us (20%)
  local copies, waits for them, and re-layouts  3.75 us (3%)
  between operations  1.61 us (1%)
    pallas_call x18, Pallas kernels, call(): pl.pallas_call(kernel, out_shape=[jax.ShapeDtypeStruct(o, t) for o, t in...  52.3 us
    ppermute x20, starting transfers between devices, swap(): return [lax.ppermute(s, self.name, p) for s, p in zip(sends, perms)]  22.4 us
    ppermute x20, waiting for transfers between devices, swap(): return [lax.ppermute(s, self.name, p) for s, p in zip(sends, perms)]  16.8 us
    all_to_all x1, starting transfers between devices, body(): lax.all_to_all(packed.reshape(peers, block, width), ('gx', 'gy'), split_a...  4.22 us
    ppermute x2, starting transfers between devices, body(): cross = [lax.ppermute(parts, 'gz', az.cross)] if az.cross else []  4.13 us
    ppermute x2, waiting for transfers between devices, body(): cross = [lax.ppermute(parts, 'gy', ay.cross)] if ay.cross else []  4.01 us
    unnamed x27, local copies, waits for them, and re-layouts  3.75 us
    ppermute x2, starting transfers between devices, body(): cross = [lax.ppermute(parts, 'gy', ay.cross)] if ay.cross else []  3.38 us
  transfers between devices with their start and end apart: 25, of which 13 were waited for; matrix products, arithmetic and copies ran while one was open for 0% of the time, Pallas kernels for 16%

profile of v6, /device:TPU:12, one launch (start us, length us, event | category | flops | bytes accessed | tf_op | source)
XLA Modules:
  0.0 114.8 jit_solution(6344095111903025609)
XLA Ops:
  8.5 2.2 %shard_map.116 = f32[576,128]{1,0:T(8,128)} custom-call(s32[4]{0:T(128)S(1)} %pad_add_fusion.info, f32[256,128]{1,0:T(8,128)S(1)} %copy-done.4, s32[256,1]{1,0:T(8,128)S(1)} %copy.12.owners, s32[1,256]{1,0:T(1,128)S(1)} %bitcast.21, s32[1,256]{1,0:T(1,128)S(1)} %bitcast.22, f32[8,128]{1,0:T(8,128)S(1)} %get-tuple-element.65.parts.after), custom_call_target="tpu_custom_call" | custom-call | flops 433168 | bytes 433168 | tf_op jit(solution)/shard_map/pallas_call | solution.py:30
  10.6 4.2 %all-to-all-start = ((f32[8,72,128]{2,1,0:T(8,128)}), f32[8,72,128]{2,1,0:T(8,128)S(1)}, u32[]{:S(2)}, u32[]{:S(2)}) async-start(f32[8,72,128]{2,1,0:T(8,128)} %bitcast.8), calls=%async_computation | async-start | bytes 589824 | tf_op jit(solution)/shard_map/all_to_all | solution.py:879
  14.9 1.5 %collective-permute-start.1 = (f32[104,128]{1,0:T(8,128)S(1)}, f32[104,128]{1,0:T(8,128)S(1)}, u32[]{:S(2)}, u32[]{:S(2)}) collective-permute-start(f32[104,128]{1,0:T(8,128)S(1)} %get-tuple-element.66), channel_id=1, source_target_pairs={{0,4},{4,0},{8,12},{12,8},{1,5},{5,1},{9,13},{13,9},{2,6},{6,2},{1... | collective-permute-start | bytes 159752 | tf_op jit(solution)/shard_map/ppermute | solution.py:81
  16.4 2.0 %collective-permute-start.3 = (f32[8,128]{1,0:T(8,128)S(1)}, f32[8,128]{1,0:T(8,128)S(1)}, u32[]{:S(2)}, u32[]{:S(2)}) collective-permute-start(f32[8,128]{1,0:T(8,128)S(1)} %get-tuple-element.65.parts.after), channel_id=1, source_target_pairs={{0,8},{4,12},{8,0},{12,4},{1,9},{5,13},{9,1},{13,5},{2,10},{6,14},... | collective-permute-start | bytes 12296 | tf_op jit(solution)/shard_map/ppermute | solution.py:872
  18.4 1.8 %collective-permute-done.3.refs_3_ = f32[8,128]{1,0:T(8,128)S(1)} collective-permute-done((f32[8,128]{1,0:T(8,128)S(1)}, f32[8,128]{1,0:T(8,128)S(1)}, u32[]{:S(2)}, u32[]{:S(2)}) %collective-permute-start.3) | collective-permute-done | bytes 4128 | tf_op jit(solution)/shard_map/ppermute | solution.py:872
  20.2 2.2 %collective-permute-done.1.refs_1_ = f32[104,128]{1,0:T(8,128)S(1)} collective-permute-done((f32[104,128]{1,0:T(8,128)S(1)}, f32[104,128]{1,0:T(8,128)S(1)}, u32[]{:S(2)}, u32[]{:S(2)}) %collective-permute-start.1) | collective-permute-done | bytes 53280 | tf_op jit(solution)/shard_map/ppermute | solution.py:81
  24.1 2.7 %collective-permute-start.5 = (f32[104,128]{1,0:T(8,128)S(1)}, f32[104,128]{1,0:T(8,128)S(1)}, u32[]{:S(2)}, u32[]{:S(2)}) collective-permute-start(f32[104,128]{1,0:T(8,128)S(1)} %get-tuple-element.74), channel_id=1, source_target_pairs={{1,2},{3,0},{2,1},{0,3},{5,6},{7,4},{6,5},{4,7},{9,10},{11,8},{10,... | collective-permute-start | bytes 159752 | tf_op jit(solution)/shard_map/ppermute | solution.py:81
  29.1 2.2 %collective-permute-done.6.refs_5_ = f32[8,128]{1,0:T(8,128)S(1)} collective-permute-done((f32[8,128]{1,0:T(8,128)S(1)}, f32[8,128]{1,0:T(8,128)S(1)}, u32[]{:S(2)}, u32[]{:S(2)}) %collective-permute-start.6) | collective-permute-done | bytes 4128 | tf_op jit(solution)/shard_map/ppermute | solution.py:894
  31.3 5.9 %shard_map.118 = (f32[3,16,48,128]{3,2,1,0:T(8,128)S(1)}, f32[16,48,128]{2,1,0:T(8,128)S(1)}, f32[16,48,128]{2,1,0:T(8,128)S(1)}, f32[2,48,128]{2,1,0:T(8,128)S(1)}, f32[17,48,128]{2,1,0:T(8,128)S(1)}) custom-call(s32[4]{0:T(128)S(1)} %pad_add_fusion.info, f32[3,16,48,128]{3,2,1,0:T(8,128)S(1)} %copy-done.1, f32[16,48,128]{2,1,0:T(8,128)S(1)} %copy-done.3, ...), custom_call_target="tpu_custom_call" | custom-call | flops 6549712 | bytes 6549712 | tf_op jit(solution)/shard_map/pallas_call | solution.py:30
  37.3 1.7 %collective-permute-done.7.refs_0_ = f32[17,48,128]{2,1,0:T(8,128)S(1)} collective-permute-done((f32[17,48,128]{2,1,0:T(8,128)S(1)}, f32[17,48,128]{2,1,0:T(8,128)S(1)}, u32[]{:S(2)}, u32[]{:S(2)}) %collective-permute-start.7) | collective-permute-done | bytes 417824 | tf_op jit(solution)/shard_map/ppermute | solution.py:81
  40.6 2.5 %collective-permute-start.9 = (f32[144,128]{1,0:T(8,128)S(1)}, f32[144,128]{1,0:T(8,128)S(1)}, u32[]{:S(2)}, u32[]{:S(2)}) collective-permute-start(f32[144,128]{1,0:T(8,128)S(1)} %get-tuple-element.83), channel_id=1, source_target_pairs={{4,8},{12,0},{8,4},{0,12},{5,9},{13,1},{9,5},{1,13},{6,10},{14,2},... | collective-permute-start | bytes 221192 | tf_op jit(solution)/shard_map/ppermute | solution.py:81
  43.1 1.9 %collective-permute-done.8.refs_0_ = f32[144,128]{1,0:T(8,128)S(1)} collective-permute-done((f32[144,128]{1,0:T(8,128)S(1)}, f32[144,128]{1,0:T(8,128)S(1)}, u32[]{:S(2)}, u32[]{:S(2)}) %collective-permute-start.8) | collective-permute-done | bytes 73760 | tf_op jit(solution)/shard_map/ppermute | solution.py:81
  45.0 2.0 %collective-permute-done.9.refs_1_ = f32[144,128]{1,0:T(8,128)S(1)} collective-permute-done((f32[144,128]{1,0:T(8,128)S(1)}, f32[144,128]{1,0:T(8,128)S(1)}, u32[]{:S(2)}, u32[]{:S(2)}) %collective-permute-start.9) | collective-permute-done | bytes 73760 | tf_op jit(solution)/shard_map/ppermute | solution.py:81
  49.0 2.5 %collective-permute-start.11 = (f32[54,8,128]{2,1,0:T(8,128)S(1)}, f32[54,8,128]{2,1,0:T(8,128)S(1)}, u32[]{:S(2)}, u32[]{:S(2)}) collective-permute-start(f32[54,8,128]{2,1,0:T(8,128)S(1)} %get-tuple-element.91), channel_id=1, source_target_pairs={{1,2},{2,1},{5,6},{6,5},{9,10},{10,9},{13,14},{14,13},{17,18},{18,... | collective-permute-start | bytes 663560 | tf_op jit(solution)/shard_map/ppermute | solution.py:81
  51.5 6.9 %shard_map.120 = (f32[7,2,24,8,128]{4,3,2,1,0:T(8,128)S(1)}, f32[7,2,24,8,128]{4,3,2,1,0:T(8,128)S(1)}, f32[24,48,128]{2,1,0:T(8,128)S(1)}, f32[24,48,128]{2,1,0...) custom-call(s32[4]{0:T(128)S(1)} %pad_add_fusion.info, f32[24,48,128]{2,1,0:T(8,128)S(1)} %get-tuple-element.79.px, ...), custom_call_target="tpu_custom_call" | custom-call | flops 6438928 | bytes 6438928 | tf_op jit(solution)/shard_map/pallas_call | solution.py:30
  58.4 6.2 %shard_map.122 = (f32[3,16,48,128]{3,2,1,0:T(8,128)S(1)}, f32[16,48,128]{2,1,0:T(8,128)S(1)}, f32[8,128]{1,0:T(8,128)S(1)}, f32[392,128]{1,0:T(8,128)S(1)}) custom-call(s32[4]{0:T(128)S(1)} %pad_add_fusion.info, f32[24,48,128]{2,1,0:T(8,128)S(1)} %get-tuple-element.79.px, f32[24,48,128]{2,1,0:T(8,128)S(1)} %get-tuple-element.80.sx, ...), custom_call_target="tpu_custom_call" | custom-call | flops 9691536 | bytes 9691536 | tf_op jit(solution)/shard_map/pallas_call | solution.py:30
  64.8 1.4 %collective-permute-done.12.refs_0_.refs_4_ = f32[392,128]{1,0:T(8,128)S(1)} collective-permute-done((f32[392,128]{1,0:T(8,128)S(1)}, f32[392,128]{1,0:T(8,128)S(1)}, u32[]{:S(2)}, u32[]{:S(2)}) %collective-permute-start.12) | collective-permute-done | bytes 200736 | tf_op jit(solution)/shard_map/ppermute | solution.py:81
  68.1 1.5 %collective-permute-start.14 = (f32[104,128]{1,0:T(8,128)S(1)}, f32[104,128]{1,0:T(8,128)S(1)}, u32[]{:S(2)}, u32[]{:S(2)}) collective-permute-start(f32[104,128]{1,0:T(8,128)S(1)} %get-tuple-element.98), channel_id=1, source_target_pairs={{4,8},{12,0},{8,4},{0,12},{5,9},{13,1},{9,5},{1,13},{6,10},{14,2},... | collective-permute-start | bytes 159752 | tf_op jit(solution)/shard_map/ppermute | solution.py:81
  69.5 1.4 %collective-permute-start.15 = (f32[8,128]{1,0:T(8,128)S(1)}, f32[8,128]{1,0:T(8,128)S(1)}, u32[]{:S(2)}, u32[]{:S(2)}) collective-permute-start(f32[8,128]{1,0:T(8,128)S(1)} %get-tuple-element.96.parts), channel_id=1, source_target_pairs={{0,8},{4,12},{8,0},{12,4},{1,9},{5,13},{9,1},{13,5},{2,10},{6,14},... | collective-permute-start | bytes 12296 | tf_op jit(solution)/shard_map/ppermute | solution.py:872
  70.9 2.2 %collective-permute-done.15.refs_3_ = f32[8,128]{1,0:T(8,128)S(1)} collective-permute-done((f32[8,128]{1,0:T(8,128)S(1)}, f32[8,128]{1,0:T(8,128)S(1)}, u32[]{:S(2)}, u32[]{:S(2)}) %collective-permute-start.15) | collective-permute-done | bytes 4128 | tf_op jit(solution)/shard_map/ppermute | solution.py:872
  73.8 1.5 %collective-permute-start.17 = (f32[104,128]{1,0:T(8,128)S(1)}, f32[104,128]{1,0:T(8,128)S(1)}, u32[]{:S(2)}, u32[]{:S(2)}) collective-permute-start(f32[104,128]{1,0:T(8,128)S(1)} %get-tuple-element.106), channel_id=1, source_target_pairs={{1,2},{3,0},{2,1},{0,3},{5,6},{7,4},{6,5},{4,7},{9,10},{11,8},{10,... | collective-permute-start | bytes 159752 | tf_op jit(solution)/shard_map/ppermute | solution.py:81
  75.3 2.9 %collective-permute-start.18 = (f32[8,128]{1,0:T(8,128)S(1)}, f32[8,128]{1,0:T(8,128)S(1)}, u32[]{:S(2)}, u32[]{:S(2)}) collective-permute-start(f32[8,128]{1,0:T(8,128)S(1)} %get-tuple-element.99.parts), channel_id=1, source_target_pairs={{0,2},{1,3},{2,0},{3,1},{4,6},{5,7},{6,4},{7,5},{8,10},{9,11},{10,... | collective-permute-start | bytes 12296 | tf_op jit(solution)/shard_map/ppermute | solution.py:894
  78.2 3.2 %shard_map.125 = (f32[18,48,128]{2,1,0:T(8,128)S(1)}, f32[16,48,128]{2,1,0:T(8,128)S(1)}, f32[16,48,128]{2,1,0:T(8,128)S(1)}, f32[16,48,128]{2,1,0:T(8,128)S(1)}) custom-call(s32[4]{0:T(128)S(1)} %pad_add_fusion.info, f32[3,16,48,128]{3,2,1,0:T(8,128)S(1)} %get-tuple-element.92.vel, f32[16,48,128]{2,1,0:T(8,128)S(1)} %get-tuple-element.93.press, ...), custom_call_target="tpu_custom_call" | custom-call | flops 3502096 | bytes 3502096 | tf_op jit(solution)/shard_map/pallas_call | solution.py:30
  81.4 5.2 %shard_map.126 = (f32[3,16,48,128]{3,2,1,0:T(8,128)S(1)}, f32[16,48,128]{2,1,0:T(8,128)S(1)}, f32[16,48,128]{2,1,0:T(8,128)S(1)}, f32[2,48,128]{2,1,0:T(8,128)S(1)}, f32[17,48,128]{2,1,0:T(8,128)S(1)}) custom-call(s32[4]{0:T(128)S(1)} %pad_add_fusion.info, f32[3,16,48,128]{3,2,1,0:T(8,128)S(1)} %get-tuple-element.92.vel, ...), custom_call_target="tpu_custom_call" | custom-call | flops 8171728 | bytes 8171728 | tf_op jit(solution)/shard_map/pallas_call | solution.py:30
  86.7 1.7 %collective-permute-done.19.refs_0_ = f32[17,48,128]{2,1,0:T(8,128)S(1)} collective-permute-done((f32[17,48,128]{2,1,0:T(8,128)S(1)}, f32[17,48,128]{2,1,0:T(8,128)S(1)}, u32[]{:S(2)}, u32[]{:S(2)}) %collective-permute-start.19) | collective-permute-done | bytes 417824 | tf_op jit(solution)/shard_map/ppermute | solution.py:81
  89.6 1.5 %collective-permute-start.20 = (f32[144,128]{1,0:T(8,128)S(1)}, f32[144,128]{1,0:T(8,128)S(1)}, u32[]{:S(2)}, u32[]{:S(2)}) collective-permute-start(f32[144,128]{1,0:T(8,128)S(1)} %get-tuple-element.114), channel_id=1, source_target_pairs={{0,4},{4,0},{8,12},{12,8},{1,5},{5,1},{9,13},{13,9},{2,6},{6,2},{1... | collective-permute-start | bytes 221192 | tf_op jit(solution)/shard_map/ppermute | solution.py:81
  91.0 1.5 %collective-permute-start.21 = (f32[144,128]{1,0:T(8,128)S(1)}, f32[144,128]{1,0:T(8,128)S(1)}, u32[]{:S(2)}, u32[]{:S(2)}) collective-permute-start(f32[144,128]{1,0:T(8,128)S(1)} %get-tuple-element.115), channel_id=1, source_target_pairs={{4,8},{12,0},{8,4},{0,12},{5,9},{13,1},{9,5},{1,13},{6,10},{14,2},... | collective-permute-start | bytes 221192 | tf_op jit(solution)/shard_map/ppermute | solution.py:81
  92.5 1.9 %collective-permute-done.20.refs_0_ = f32[144,128]{1,0:T(8,128)S(1)} collective-permute-done((f32[144,128]{1,0:T(8,128)S(1)}, f32[144,128]{1,0:T(8,128)S(1)}, u32[]{:S(2)}, u32[]{:S(2)}) %collective-permute-start.20) | collective-permute-done | bytes 73760 | tf_op jit(solution)/shard_map/ppermute | solution.py:81
  94.4 2.0 %collective-permute-done.21.refs_1_ = f32[144,128]{1,0:T(8,128)S(1)} collective-permute-done((f32[144,128]{1,0:T(8,128)S(1)}, f32[144,128]{1,0:T(8,128)S(1)}, u32[]{:S(2)}, u32[]{:S(2)}) %collective-permute-start.21) | collective-permute-done | bytes 73760 | tf_op jit(solution)/shard_map/ppermute | solution.py:81
  98.3 2.5 %collective-permute-start.23 = (f32[54,8,128]{2,1,0:T(8,128)S(1)}, f32[54,8,128]{2,1,0:T(8,128)S(1)}, u32[]{:S(2)}, u32[]{:S(2)}) collective-permute-start(f32[54,8,128]{2,1,0:T(8,128)S(1)} %get-tuple-element.123), channel_id=1, source_target_pairs={{1,2},{2,1},{5,6},{6,5},{9,10},{10,9},{13,14},{14,13},{17,18},{18,... | collective-permute-start | bytes 663560 | tf_op jit(solution)/shard_map/ppermute | solution.py:81
  100.8 6.9 %shard_map.128 = (f32[7,2,24,8,128]{4,3,2,1,0:T(8,128)S(1)}, f32[7,2,24,8,128]{4,3,2,1,0:T(8,128)S(1)}, f32[24,48,128]{2,1,0:T(8,128)S(1)}, f32[24,48,128]{2,1,0...) custom-call(s32[4]{0:T(128)S(1)} %pad_add_fusion.info, f32[24,48,128]{2,1,0:T(8,128)S(1)} %get-tuple-element.111.px, ...), custom_call_target="tpu_custom_call" | custom-call | flops 6438928 | bytes 6438928 | tf_op jit(solution)/shard_map/pallas_call | solution.py:30
  107.7 7.1 %shard_map.130 = (f32[3,16,48,128]{3,2,1,0:T(8,128)}, f32[16,48,128]{2,1,0:T(8,128)}) custom-call(s32[4]{0:T(128)S(1)} %pad_add_fusion.info, f32[24,48,128]{2,1,0:T(8,128)S(1)} %get-tuple-element.111.px, f32[24,48,128]{2,1,0:T(8,128)S(1)} %get-tuple-element.112.sx, f32[3,16,48,128]{3,2,1,0:T(8,128)S(1)} %get-tuple-element.113.star, s32[1,48]{1,0:T(1,128)S(1)} %bitcast.15, ...), custom_call_target="tpu_custom_call" | custom-call | flops 9486736 | bytes 9486736 | tf_op jit(solution)/shard_map/pallas_call | solution.py:30
  (64 shorter events, 20.4 us)
Async XLA Ops:
  0.6 5.2 %copy-start.12 = (s32[256,1]{0,1:T(1,128)S(1)}, s32[256,1]{0,1:T(1,128)}, u32[]{:S(2)}) copy-start(s32[256,1]{0,1:T(1,128)} %param.13) | copy-start | bytes 3076
  5.7 2.7 %copy-start.4 = (f32[256,128]{1,0:T(8,128)S(1)}, f32[256,128]{1,0:T(8,128)}, u32[]{:S(2)}) copy-start(f32[256,128]{1,0:T(8,128)} %kern.1) | copy-start | bytes 393220
  5.7 2.8 %copy-start.10 = (s32[256]{0:T(256)S(1)}, s32[256]{0:T(256)}, u32[]{:S(2)}) copy-start(s32[256]{0:T(256)} %param.14) | copy-start | bytes 3076
  5.7 2.8 %copy-start.11 = (s32[256]{0:T(256)S(1)}, s32[256]{0:T(256)}, u32[]{:S(2)}) copy-start(s32[256]{0:T(256)} %param.15) | copy-start | bytes 3076
  5.7 1.5 %collective-permute-start = (f32[392,128]{1,0:T(8,128)S(1)}, f32[392,128]{1,0:T(8,128)S(1)}, u32[]{:S(2)}, u32[]{:S(2)}) collective-permute-start(f32[392,128]{1,0:T(8,128)S(1)} %get-tuple-element.64), channel_id=1, source_target_pairs={{0,16},{16,0},{1,17},{17,1},{2,18},{18,2},{3,19},{19,3},{4,20},{20... | collective-permute-start | bytes 602120 | tf_op jit(solution)/shard_map/ppermute | solution.py:81
  10.6 17.4 %all-to-all-start = ((f32[8,72,128]{2,1,0:T(8,128)}), f32[8,72,128]{2,1,0:T(8,128)S(1)}, u32[]{:S(2)}, u32[]{:S(2)}) async-start(f32[8,72,128]{2,1,0:T(8,128)} %bitcast.8), calls=%async_computation | async-start | bytes 589824 | tf_op jit(solution)/shard_map/all_to_all | solution.py:879
  14.9 16.4 %copy-start.9 = (f32[48]{0:T(128)S(1)}, f32[48]{0:T(128)}, u32[]{:S(2)}) copy-start(f32[48]{0:T(128)} %param.17) | copy-start | bytes 580
  14.9 7.5 %collective-permute-start.1 = (f32[104,128]{1,0:T(8,128)S(1)}, f32[104,128]{1,0:T(8,128)S(1)}, u32[]{:S(2)}, u32[]{:S(2)}) collective-permute-start(f32[104,128]{1,0:T(8,128)S(1)} %get-tuple-element.66), channel_id=1, source_target_pairs={{0,4},{4,0},{8,12},{12,8},{1,5},{5,1},{9,13},{13,9},{2,6},{6,2},{1... | collective-permute-start | bytes 159752 | tf_op jit(solution)/shard_map/ppermute | solution.py:81
  16.3 6.6 %collective-permute-start.2 = (f32[104,128]{1,0:T(8,128)S(1)}, f32[104,128]{1,0:T(8,128)S(1)}, u32[]{:S(2)}, u32[]{:S(2)}) collective-permute-start(f32[104,128]{1,0:T(8,128)S(1)} %get-tuple-element.67), channel_id=1, source_target_pairs={{4,8},{12,0},{8,4},{0,12},{5,9},{13,1},{9,5},{1,13},{6,10},{14,2},... | collective-permute-start | bytes 159752 | tf_op jit(solution)/shard_map/ppermute | solution.py:81
  16.4 3.8 %collective-permute-start.3 = (f32[8,128]{1,0:T(8,128)S(1)}, f32[8,128]{1,0:T(8,128)S(1)}, u32[]{:S(2)}, u32[]{:S(2)}) collective-permute-start(f32[8,128]{1,0:T(8,128)S(1)} %get-tuple-element.65.parts.after), channel_id=1, source_target_pairs={{0,8},{4,12},{8,0},{12,4},{1,9},{5,13},{9,1},{13,5},{2,10},{6,14},... | collective-permute-start | bytes 12296 | tf_op jit(solution)/shard_map/ppermute | solution.py:872
  23.6 7.7 %collective-permute-start.4 = (f32[104,128]{1,0:T(8,128)S(1)}, f32[104,128]{1,0:T(8,128)S(1)}, u32[]{:S(2)}, u32[]{:S(2)}) collective-permute-start(f32[104,128]{1,0:T(8,128)S(1)} %get-tuple-element.73), channel_id=1, source_target_pairs={{0,1},{1,0},{2,3},{3,2},{4,5},{5,4},{6,7},{7,6},{8,9},{9,8},{10,11... | collective-permute-start | bytes 159752 | tf_op jit(solution)/shard_map/ppermute | solution.py:81
  24.1 7.2 %collective-permute-start.5 = (f32[104,128]{1,0:T(8,128)S(1)}, f32[104,128]{1,0:T(8,128)S(1)}, u32[]{:S(2)}, u32[]{:S(2)}) collective-permute-start(f32[104,128]{1,0:T(8,128)S(1)} %get-tuple-element.74), channel_id=1, source_target_pairs={{1,2},{3,0},{2,1},{0,3},{5,6},{7,4},{6,5},{4,7},{9,10},{11,8},{10,... | collective-permute-start | bytes 159752 | tf_op jit(solution)/shard_map/ppermute | solution.py:81
  26.8 4.5 %collective-permute-start.6 = (f32[8,128]{1,0:T(8,128)S(1)}, f32[8,128]{1,0:T(8,128)S(1)}, u32[]{:S(2)}, u32[]{:S(2)}) collective-permute-start(f32[8,128]{1,0:T(8,128)S(1)} %get-tuple-element.68.parts), channel_id=1, source_target_pairs={{0,2},{1,3},{2,0},{3,1},{4,6},{5,7},{6,4},{7,5},{8,10},{9,11},{10,... | collective-permute-start | bytes 12296 | tf_op jit(solution)/shard_map/ppermute | solution.py:894
  37.2 1.8 %collective-permute-start.7 = (f32[17,48,128]{2,1,0:T(8,128)S(1)}, f32[17,48,128]{2,1,0:T(8,128)S(1)}, u32[]{:S(2)}, u32[]{:S(2)}) collective-permute-start(f32[17,48,128]{2,1,0:T(8,128)S(1)} %get-tuple-element.78), channel_id=1, source_target_pairs={{0,16},{16,0},{1,17},{17,1},{2,18},{18,2},{3,19},{19,3},{4,20},{20... | collective-permute-start | bytes 1253384 | tf_op jit(solution)/shard_map/ppermute | solution.py:81
  40.1 4.9 %collective-permute-start.8 = (f32[144,128]{1,0:T(8,128)S(1)}, f32[144,128]{1,0:T(8,128)S(1)}, u32[]{:S(2)}, u32[]{:S(2)}) collective-permute-start(f32[144,128]{1,0:T(8,128)S(1)} %get-tuple-element.82), channel_id=1, source_target_pairs={{0,4},{4,0},{8,12},{12,8},{1,5},{5,1},{9,13},{13,9},{2,6},{6,2},{1... | collective-permute-start | bytes 221192 | tf_op jit(solution)/shard_map/ppermute | solution.py:81
  40.6 6.4 %collective-permute-start.9 = (f32[144,128]{1,0:T(8,128)S(1)}, f32[144,128]{1,0:T(8,128)S(1)}, u32[]{:S(2)}, u32[]{:S(2)}) collective-permute-start(f32[144,128]{1,0:T(8,128)S(1)} %get-tuple-element.83), channel_id=1, source_target_pairs={{4,8},{12,0},{8,4},{0,12},{5,9},{13,1},{9,5},{1,13},{6,10},{14,2},... | collective-permute-start | bytes 221192 | tf_op jit(solution)/shard_map/ppermute | solution.py:81
  47.0 11.5 %copy-start.6 = (s32[48]{0:T(128)S(1)}, s32[48]{0:T(128)}, u32[]{:S(2)}) copy-start(s32[48]{0:T(128)} %param.18) | copy-start | bytes 580
  47.0 11.5 %copy-start.8 = (s32[48]{0:T(128)S(1)}, s32[48]{0:T(128)}, u32[]{:S(2)}) copy-start(s32[48]{0:T(128)} %param.19) | copy-start | bytes 580
  47.6 10.8 %collective-permute-start.10 = (f32[54,8,128]{2,1,0:T(8,128)S(1)}, f32[54,8,128]{2,1,0:T(8,128)S(1)}, u32[]{:S(2)}, u32[]{:S(2)}) collective-permute-start(f32[54,8,128]{2,1,0:T(8,128)S(1)} %get-tuple-element.90), channel_id=1, source_target_pairs={{0,1},{1,0},{2,3},{3,2},{4,5},{5,4},{6,7},{7,6},{8,9},{9,8},{10,11... | collective-permute-start | bytes 663560 | tf_op jit(solution)/shard_map/ppermute | solution.py:81
  49.0 9.4 %collective-permute-start.11 = (f32[54,8,128]{2,1,0:T(8,128)S(1)}, f32[54,8,128]{2,1,0:T(8,128)S(1)}, u32[]{:S(2)}, u32[]{:S(2)}) collective-permute-start(f32[54,8,128]{2,1,0:T(8,128)S(1)} %get-tuple-element.91), channel_id=1, source_target_pairs={{1,2},{2,1},{5,6},{6,5},{9,10},{10,9},{13,14},{14,13},{17,18},{18,... | collective-permute-start | bytes 663560 | tf_op jit(solution)/shard_map/ppermute | solution.py:81
  64.7 1.5 %collective-permute-start.12 = (f32[392,128]{1,0:T(8,128)S(1)}, f32[392,128]{1,0:T(8,128)S(1)}, u32[]{:S(2)}, u32[]{:S(2)}) collective-permute-start(f32[392,128]{1,0:T(8,128)S(1)} %get-tuple-element.95), channel_id=1, source_target_pairs={{0,16},{16,0},{1,17},{17,1},{2,18},{18,2},{3,19},{19,3},{4,20},{20... | collective-permute-start | bytes 602120 | tf_op jit(solution)/shard_map/ppermute | solution.py:81
  67.4 5.7 %collective-permute-start.13 = (f32[104,128]{1,0:T(8,128)S(1)}, f32[104,128]{1,0:T(8,128)S(1)}, u32[]{:S(2)}, u32[]{:S(2)}) collective-permute-start(f32[104,128]{1,0:T(8,128)S(1)} %get-tuple-element.97), channel_id=1, source_target_pairs={{0,4},{4,0},{8,12},{12,8},{1,5},{5,1},{9,13},{13,9},{2,6},{6,2},{1... | collective-permute-start | bytes 159752 | tf_op jit(solution)/shard_map/ppermute | solution.py:81
  68.1 5.1 %collective-permute-start.14 = (f32[104,128]{1,0:T(8,128)S(1)}, f32[104,128]{1,0:T(8,128)S(1)}, u32[]{:S(2)}, u32[]{:S(2)}) collective-permute-start(f32[104,128]{1,0:T(8,128)S(1)} %get-tuple-element.98), channel_id=1, source_target_pairs={{4,8},{12,0},{8,4},{0,12},{5,9},{13,1},{9,5},{1,13},{6,10},{14,2},... | collective-permute-start | bytes 159752 | tf_op jit(solution)/shard_map/ppermute | solution.py:81
  69.5 3.6 %collective-permute-start.15 = (f32[8,128]{1,0:T(8,128)S(1)}, f32[8,128]{1,0:T(8,128)S(1)}, u32[]{:S(2)}, u32[]{:S(2)}) collective-permute-start(f32[8,128]{1,0:T(8,128)S(1)} %get-tuple-element.96.parts), channel_id=1, source_target_pairs={{0,8},{4,12},{8,0},{12,4},{1,9},{5,13},{9,1},{13,5},{2,10},{6,14},... | collective-permute-start | bytes 12296 | tf_op jit(solution)/shard_map/ppermute | solution.py:872
  73.8 7.7 %collective-permute-start.16 = (f32[104,128]{1,0:T(8,128)S(1)}, f32[104,128]{1,0:T(8,128)S(1)}, u32[]{:S(2)}, u32[]{:S(2)}) collective-permute-start(f32[104,128]{1,0:T(8,128)S(1)} %get-tuple-element.105), channel_id=1, source_target_pairs={{0,1},{1,0},{2,3},{3,2},{4,5},{5,4},{6,7},{7,6},{8,9},{9,8},{10,11... | collective-permute-start | bytes 159752 | tf_op jit(solution)/shard_map/ppermute | solution.py:81
  73.8 7.6 %collective-permute-start.17 = (f32[104,128]{1,0:T(8,128)S(1)}, f32[104,128]{1,0:T(8,128)S(1)}, u32[]{:S(2)}, u32[]{:S(2)}) collective-permute-start(f32[104,128]{1,0:T(8,128)S(1)} %get-tuple-element.106), channel_id=1, source_target_pairs={{1,2},{3,0},{2,1},{0,3},{5,6},{7,4},{6,5},{4,7},{9,10},{11,8},{10,... | collective-permute-start | bytes 159752 | tf_op jit(solution)/shard_map/ppermute | solution.py:81
  75.3 6.1 %collective-permute-start.18 = (f32[8,128]{1,0:T(8,128)S(1)}, f32[8,128]{1,0:T(8,128)S(1)}, u32[]{:S(2)}, u32[]{:S(2)}) collective-permute-start(f32[8,128]{1,0:T(8,128)S(1)} %get-tuple-element.99.parts), channel_id=1, source_target_pairs={{0,2},{1,3},{2,0},{3,1},{4,6},{5,7},{6,4},{7,5},{8,10},{9,11},{10,... | collective-permute-start | bytes 12296 | tf_op jit(solution)/shard_map/ppermute | solution.py:894
  86.6 1.8 %collective-permute-start.19 = (f32[17,48,128]{2,1,0:T(8,128)S(1)}, f32[17,48,128]{2,1,0:T(8,128)S(1)}, u32[]{:S(2)}, u32[]{:S(2)}) collective-permute-start(f32[17,48,128]{2,1,0:T(8,128)S(1)} %get-tuple-element.110), channel_id=1, source_target_pairs={{0,16},{16,0},{1,17},{17,1},{2,18},{18,2},{3,19},{19,3},{4,20},{20... | collective-permute-start | bytes 1253384 | tf_op jit(solution)/shard_map/ppermute | solution.py:81
  89.6 4.9 %collective-permute-start.20 = (f32[144,128]{1,0:T(8,128)S(1)}, f32[144,128]{1,0:T(8,128)S(1)}, u32[]{:S(2)}, u32[]{:S(2)}) collective-permute-start(f32[144,128]{1,0:T(8,128)S(1)} %get-tuple-element.114), channel_id=1, source_target_pairs={{0,4},{4,0},{8,12},{12,8},{1,5},{5,1},{9,13},{13,9},{2,6},{6,2},{1... | collective-permute-start | bytes 221192 | tf_op jit(solution)/shard_map/ppermute | solution.py:81
  91.0 5.4 %collective-permute-start.21 = (f32[144,128]{1,0:T(8,128)S(1)}, f32[144,128]{1,0:T(8,128)S(1)}, u32[]{:S(2)}, u32[]{:S(2)}) collective-permute-start(f32[144,128]{1,0:T(8,128)S(1)} %get-tuple-element.115), channel_id=1, source_target_pairs={{4,8},{12,0},{8,4},{0,12},{5,9},{13,1},{9,5},{1,13},{6,10},{14,2},... | collective-permute-start | bytes 221192 | tf_op jit(solution)/shard_map/ppermute | solution.py:81
  97.0 10.7 %collective-permute-start.22 = (f32[54,8,128]{2,1,0:T(8,128)S(1)}, f32[54,8,128]{2,1,0:T(8,128)S(1)}, u32[]{:S(2)}, u32[]{:S(2)}) collective-permute-start(f32[54,8,128]{2,1,0:T(8,128)S(1)} %get-tuple-element.122), channel_id=1, source_target_pairs={{0,1},{1,0},{2,3},{3,2},{4,5},{5,4},{6,7},{7,6},{8,9},{9,8},{10,11... | collective-permute-start | bytes 663560 | tf_op jit(solution)/shard_map/ppermute | solution.py:81
  98.3 9.4 %collective-permute-start.23 = (f32[54,8,128]{2,1,0:T(8,128)S(1)}, f32[54,8,128]{2,1,0:T(8,128)S(1)}, u32[]{:S(2)}, u32[]{:S(2)}) collective-permute-start(f32[54,8,128]{2,1,0:T(8,128)S(1)} %get-tuple-element.123), channel_id=1, source_target_pairs={{1,2},{2,1},{5,6},{6,5},{9,10},{10,9},{13,14},{14,13},{17,18},{18,... | collective-permute-start | bytes 663560 | tf_op jit(solution)/shard_map/ppermute | solution.py:81
  (6 other events, 8.2 us)

commit v7 on v6

--- a/solution.py
+++ b/solution.py
@@ -145,10 +145,10 @@
         out[4 * HA * cells_z :, :] = parts
 
 
-def begin_kernel(nsend, turbines, info, vel, press, inx, iny, *outs):
+def begin_kernel(nsend, turbines, info, vel, press, places, *outs):
     _, cells_x, cells_z, width = vel.shape
     column = lambda x: jnp.sum(vel[0, x], axis=0, keepdims=True)
-    parts = inflow_parts(info, column, inx[...], iny[...], turbines, cells_x, width)
+    parts = inflow_parts(info, column, places[0:1, :], places[1:2, :], turbines, cells_x, width)
     outs[0][...] = parts
     planes = lambda f, x: vel[f, x] if f < 3 else press[x]
     fill_xsend(info, outs[1 : 1 + nsend], planes, parts, cells_x, cells_z)
@@ -721,7 +721,7 @@
         last_t[x] = pts[done][x + 1, ZO:end, :]
 
 
-def sweep_kernel(ax, ay, az, npack, last, turbines, info, px, sx, star, inx, iny, *refs):
+def sweep_kernel(ax, ay, az, npack, last, turbines, info, px, sx, star, places, *refs):
     ny, nz = len(ay.perms), len(az.perms)
     edge_m, edge_t, last_m, last_t, first_t, source_t = refs[:6]
     refs = refs[6:]
@@ -816,7 +816,7 @@
     loop(cells_x, gradient, 4)
     if not last:
         column = lambda x: jnp.sum(vel[0, x], axis=0, keepdims=True)
-        share = inflow_parts(info, column, inx[...], iny[...], turbines, cells_x, width)
+        share = inflow_parts(info, column, places[0:1, :], places[1:2, :], turbines, cells_x, width)
         parts[...] = share
         planes = lambda f, x: vel[f, x] if f < 3 else press[x]
         fill_xsend(info, sends, planes, share, cells_x, cells_z)
@@ -845,8 +845,7 @@
             row_counts.reshape(()),
         ]
     ).astype(jnp.int32)
-    inx = inflow_x[None, :]
-    iny = inflow_y[None, :]
+    places = jnp.stack([inflow_x, inflow_y])
     push = thrust[None, :]
     block = capacity + 8
     xsize = (4 * HA * cells_z + 8, width)
@@ -854,7 +853,7 @@
     parts, *xsend = call(
         functools.partial(begin_kernel, nx, turbines),
         [(8, width)] + [xsize] * nx,
-        [info, vel, press, inx, iny],
+        [info, vel, press, places],
     )
     zrows = z_table(cells_x)[1] + ny * 2 * HA
     zrows = -(-zrows // 8) * 8 + 8
@@ -959,7 +958,7 @@
         results = call(
             functools.partial(sweep_kernel, ax, ay, az, pack_b, last, turbines),
             outs,
-            [info, px, sx, star, inx, iny, *inner, *zr],
+            [info, px, sx, star, places, *inner, *zr],
             scratch=[
                 vm(ext_b + 2, tall, width),
                 vm(ext_b + 2, tall, width),

time: 115 us -> 115 us (level)
  local copies, waits for them, and re-layouts: 3.75 us -> 2.43 us
    unnamed x27 -> x19, local copies, waits for them, and re-layouts: 3.75 us -> 2.43 us
where the time goes in v7:
time: 115 us; the launch traced here: 114 us
  Pallas kernels  52.3 us (45%)
  starting transfers between devices  34.1 us (30%)
  waiting for transfers between devices  23 us (20%)
  local copies, waits for them, and re-layouts  2.43 us (2%)
  between operations  1.59 us (1%)
    pallas_call x18, Pallas kernels, call(): pl.pallas_call(kernel, out_shape=[jax.ShapeDtypeStruct(o, t) for o, t in...  52.3 us
    ppermute x20, starting transfers between devices, swap(): return [lax.ppermute(s, self.name, p) for s, p in zip(sends, perms)]  22.4 us
    ppermute x20, waiting for transfers between devices, swap(): return [lax.ppermute(s, self.name, p) for s, p in zip(sends, perms)]  16.8 us
    all_to_all x1, starting transfers between devices, body(): lax.all_to_all(packed.reshape(peers, block, width), ('gx', 'gy'), split_a...  4.23 us
    ppermute x2, starting transfers between devices, body(): cross = [lax.ppermute(parts, 'gz', az.cross)] if az.cross else []  4.13 us
    ppermute x2, waiting for transfers between devices, body(): cross = [lax.ppermute(parts, 'gy', ay.cross)] if ay.cross else []  4.01 us
    ppermute x2, starting transfers between devices, body(): cross = [lax.ppermute(parts, 'gy', ay.cross)] if ay.cross else []  3.38 us
    unnamed x19, local copies, waits for them, and re-layouts  2.43 us
  transfers between devices with their start and end apart: 25, of which 13 were waited for; matrix products, arithmetic and copies ran while one was open for 0% of the time, Pallas kernels for 16%

profile of v7, /device:TPU:12, one launch (start us, length us, event | category | flops | bytes accessed | tf_op | source)
XLA Modules:
  0.0 114.2 jit_solution(11177419620688978062)
XLA Ops:
  7.8 2.2 %shard_map.116 = f32[576,128]{1,0:T(8,128)} custom-call(s32[4]{0:T(128)S(1)} %pad_add_fusion.1.info, f32[256,128]{1,0:T(8,128)S(1)} %copy-done.4, s32[256,1]{1,0:T(8,128)S(1)} %copy.12.owners, s32[1,256]{1,0:T(1,128)S(1)} %bitcast.15, s32[1,256]{1,0:T(1,128)S(1)} %bitcast.16, f32[8,128]{1,0:T(8,128)S(1)} %get-tuple-element.65.parts.after), custom_call_target="tpu_custom_call" | custom-call | flops 433168 | bytes 433168 | tf_op jit(solution)/shard_map/pallas_call | solution.py:30
  10.0 4.2 %all-to-all-start = ((f32[8,72,128]{2,1,0:T(8,128)}), f32[8,72,128]{2,1,0:T(8,128)S(1)}, u32[]{:S(2)}, u32[]{:S(2)}) async-start(f32[8,72,128]{2,1,0:T(8,128)} %bitcast.8), calls=%async_computation | async-start | bytes 589824 | tf_op jit(solution)/shard_map/all_to_all | solution.py:878
  14.2 1.5 %collective-permute-start.1 = (f32[104,128]{1,0:T(8,128)S(1)}, f32[104,128]{1,0:T(8,128)S(1)}, u32[]{:S(2)}, u32[]{:S(2)}) collective-permute-start(f32[104,128]{1,0:T(8,128)S(1)} %get-tuple-element.66), channel_id=1, source_target_pairs={{0,4},{4,0},{8,12},{12,8},{1,5},{5,1},{9,13},{13,9},{2,6},{6,2},{1... | collective-permute-start | bytes 159752 | tf_op jit(solution)/shard_map/ppermute | solution.py:81
  15.8 2.0 %collective-permute-start.3 = (f32[8,128]{1,0:T(8,128)S(1)}, f32[8,128]{1,0:T(8,128)S(1)}, u32[]{:S(2)}, u32[]{:S(2)}) collective-permute-start(f32[8,128]{1,0:T(8,128)S(1)} %get-tuple-element.65.parts.after), channel_id=1, source_target_pairs={{0,8},{4,12},{8,0},{12,4},{1,9},{5,13},{9,1},{13,5},{2,10},{6,14},... | collective-permute-start | bytes 12296 | tf_op jit(solution)/shard_map/ppermute | solution.py:871
  17.7 1.8 %collective-permute-done.3.refs_3_ = f32[8,128]{1,0:T(8,128)S(1)} collective-permute-done((f32[8,128]{1,0:T(8,128)S(1)}, f32[8,128]{1,0:T(8,128)S(1)}, u32[]{:S(2)}, u32[]{:S(2)}) %collective-permute-start.3) | collective-permute-done | bytes 4128 | tf_op jit(solution)/shard_map/ppermute | solution.py:871
  19.5 2.2 %collective-permute-done.1.refs_1_ = f32[104,128]{1,0:T(8,128)S(1)} collective-permute-done((f32[104,128]{1,0:T(8,128)S(1)}, f32[104,128]{1,0:T(8,128)S(1)}, u32[]{:S(2)}, u32[]{:S(2)}) %collective-permute-start.1) | collective-permute-done | bytes 53280 | tf_op jit(solution)/shard_map/ppermute | solution.py:81
  23.4 2.7 %collective-permute-start.5 = (f32[104,128]{1,0:T(8,128)S(1)}, f32[104,128]{1,0:T(8,128)S(1)}, u32[]{:S(2)}, u32[]{:S(2)}) collective-permute-start(f32[104,128]{1,0:T(8,128)S(1)} %get-tuple-element.74), channel_id=1, source_target_pairs={{1,2},{3,0},{2,1},{0,3},{5,6},{7,4},{6,5},{4,7},{9,10},{11,8},{10,... | collective-permute-start | bytes 159752 | tf_op jit(solution)/shard_map/ppermute | solution.py:81
  28.4 2.2 %collective-permute-done.6.refs_5_ = f32[8,128]{1,0:T(8,128)S(1)} collective-permute-done((f32[8,128]{1,0:T(8,128)S(1)}, f32[8,128]{1,0:T(8,128)S(1)}, u32[]{:S(2)}, u32[]{:S(2)}) %collective-permute-start.6) | collective-permute-done | bytes 4128 | tf_op jit(solution)/shard_map/ppermute | solution.py:893
  30.7 5.9 %shard_map.118 = (f32[3,16,48,128]{3,2,1,0:T(8,128)S(1)}, f32[16,48,128]{2,1,0:T(8,128)S(1)}, f32[16,48,128]{2,1,0:T(8,128)S(1)}, f32[2,48,128]{2,1,0:T(8,128)S(1)}, f32[17,48,128]{2,1,0:T(8,128)S(1)}) custom-call(s32[4]{0:T(128)S(1)} %pad_add_fusion.1.info, f32[3,16,48,128]{3,2,1,0:T(8,128)S(1)} %copy-done.1, f32[16,48,128]{2,1,0:T(8,128)S(1)} %copy-done.3, ...), custom_call_target="tpu_custom_call" | custom-call | flops 6549712 | bytes 6549712 | tf_op jit(solution)/shard_map/pallas_call | solution.py:30
  36.6 1.7 %collective-permute-done.7.refs_0_ = f32[17,48,128]{2,1,0:T(8,128)S(1)} collective-permute-done((f32[17,48,128]{2,1,0:T(8,128)S(1)}, f32[17,48,128]{2,1,0:T(8,128)S(1)}, u32[]{:S(2)}, u32[]{:S(2)}) %collective-permute-start.7) | collective-permute-done | bytes 417824 | tf_op jit(solution)/shard_map/ppermute | solution.py:81
  39.9 2.5 %collective-permute-start.9 = (f32[144,128]{1,0:T(8,128)S(1)}, f32[144,128]{1,0:T(8,128)S(1)}, u32[]{:S(2)}, u32[]{:S(2)}) collective-permute-start(f32[144,128]{1,0:T(8,128)S(1)} %get-tuple-element.83), channel_id=1, source_target_pairs={{4,8},{12,0},{8,4},{0,12},{5,9},{13,1},{9,5},{1,13},{6,10},{14,2},... | collective-permute-start | bytes 221192 | tf_op jit(solution)/shard_map/ppermute | solution.py:81
  42.5 1.9 %collective-permute-done.8.refs_0_ = f32[144,128]{1,0:T(8,128)S(1)} collective-permute-done((f32[144,128]{1,0:T(8,128)S(1)}, f32[144,128]{1,0:T(8,128)S(1)}, u32[]{:S(2)}, u32[]{:S(2)}) %collective-permute-start.8) | collective-permute-done | bytes 73760 | tf_op jit(solution)/shard_map/ppermute | solution.py:81
  44.3 2.0 %collective-permute-done.9.refs_1_ = f32[144,128]{1,0:T(8,128)S(1)} collective-permute-done((f32[144,128]{1,0:T(8,128)S(1)}, f32[144,128]{1,0:T(8,128)S(1)}, u32[]{:S(2)}, u32[]{:S(2)}) %collective-permute-start.9) | collective-permute-done | bytes 73760 | tf_op jit(solution)/shard_map/ppermute | solution.py:81
  48.3 2.5 %collective-permute-start.11 = (f32[54,8,128]{2,1,0:T(8,128)S(1)}, f32[54,8,128]{2,1,0:T(8,128)S(1)}, u32[]{:S(2)}, u32[]{:S(2)}) collective-permute-start(f32[54,8,128]{2,1,0:T(8,128)S(1)} %get-tuple-element.91), channel_id=1, source_target_pairs={{1,2},{2,1},{5,6},{6,5},{9,10},{10,9},{13,14},{14,13},{17,18},{18,... | collective-permute-start | bytes 663560 | tf_op jit(solution)/shard_map/ppermute | solution.py:81
  50.9 6.9 %shard_map.120 = (f32[7,2,24,8,128]{4,3,2,1,0:T(8,128)S(1)}, f32[7,2,24,8,128]{4,3,2,1,0:T(8,128)S(1)}, f32[24,48,128]{2,1,0:T(8,128)S(1)}, f32[24,48,128]{2,1,0...) custom-call(s32[4]{0:T(128)S(1)} %pad_add_fusion.1.info, f32[24,48,128]{2,1,0:T(8,128)S(1)} %get-tuple-element.79.px, ...), custom_call_target="tpu_custom_call" | custom-call | flops 6438928 | bytes 6438928 | tf_op jit(solution)/shard_map/pallas_call | solution.py:30
  57.8 6.2 %shard_map.122 = (f32[3,16,48,128]{3,2,1,0:T(8,128)S(1)}, f32[16,48,128]{2,1,0:T(8,128)S(1)}, f32[8,128]{1,0:T(8,128)S(1)}, f32[392,128]{1,0:T(8,128)S(1)}) custom-call(s32[4]{0:T(128)S(1)} %pad_add_fusion.1.info, f32[24,48,128]{2,1,0:T(8,128)S(1)} %get-tuple-element.79.px, f32[24,48,128]{2,1,0:T(8,128)S(1)} %get-tuple-element.80.sx, ...), custom_call_target="tpu_custom_call" | custom-call | flops 9691536 | bytes 9691536 | tf_op jit(solution)/shard_map/pallas_call | solution.py:30
  64.1 1.4 %collective-permute-done.12.refs_0_.refs_4_ = f32[392,128]{1,0:T(8,128)S(1)} collective-permute-done((f32[392,128]{1,0:T(8,128)S(1)}, f32[392,128]{1,0:T(8,128)S(1)}, u32[]{:S(2)}, u32[]{:S(2)}) %collective-permute-start.12) | collective-permute-done | bytes 200736 | tf_op jit(solution)/shard_map/ppermute | solution.py:81
  67.4 1.5 %collective-permute-start.14 = (f32[104,128]{1,0:T(8,128)S(1)}, f32[104,128]{1,0:T(8,128)S(1)}, u32[]{:S(2)}, u32[]{:S(2)}) collective-permute-start(f32[104,128]{1,0:T(8,128)S(1)} %get-tuple-element.98), channel_id=1, source_target_pairs={{4,8},{12,0},{8,4},{0,12},{5,9},{13,1},{9,5},{1,13},{6,10},{14,2},... | collective-permute-start | bytes 159752 | tf_op jit(solution)/shard_map/ppermute | solution.py:81
  68.8 1.4 %collective-permute-start.15 = (f32[8,128]{1,0:T(8,128)S(1)}, f32[8,128]{1,0:T(8,128)S(1)}, u32[]{:S(2)}, u32[]{:S(2)}) collective-permute-start(f32[8,128]{1,0:T(8,128)S(1)} %get-tuple-element.96.parts), channel_id=1, source_target_pairs={{0,8},{4,12},{8,0},{12,4},{1,9},{5,13},{9,1},{13,5},{2,10},{6,14},... | collective-permute-start | bytes 12296 | tf_op jit(solution)/shard_map/ppermute | solution.py:871
  70.3 2.2 %collective-permute-done.15.refs_3_ = f32[8,128]{1,0:T(8,128)S(1)} collective-permute-done((f32[8,128]{1,0:T(8,128)S(1)}, f32[8,128]{1,0:T(8,128)S(1)}, u32[]{:S(2)}, u32[]{:S(2)}) %collective-permute-start.15) | collective-permute-done | bytes 4128 | tf_op jit(solution)/shard_map/ppermute | solution.py:871
  73.2 1.5 %collective-permute-start.17 = (f32[104,128]{1,0:T(8,128)S(1)}, f32[104,128]{1,0:T(8,128)S(1)}, u32[]{:S(2)}, u32[]{:S(2)}) collective-permute-start(f32[104,128]{1,0:T(8,128)S(1)} %get-tuple-element.106), channel_id=1, source_target_pairs={{1,2},{3,0},{2,1},{0,3},{5,6},{7,4},{6,5},{4,7},{9,10},{11,8},{10,... | collective-permute-start | bytes 159752 | tf_op jit(solution)/shard_map/ppermute | solution.py:81
  74.6 2.9 %collective-permute-start.18 = (f32[8,128]{1,0:T(8,128)S(1)}, f32[8,128]{1,0:T(8,128)S(1)}, u32[]{:S(2)}, u32[]{:S(2)}) collective-permute-start(f32[8,128]{1,0:T(8,128)S(1)} %get-tuple-element.99.parts), channel_id=1, source_target_pairs={{0,2},{1,3},{2,0},{3,1},{4,6},{5,7},{6,4},{7,5},{8,10},{9,11},{10,... | collective-permute-start | bytes 12296 | tf_op jit(solution)/shard_map/ppermute | solution.py:893
  77.5 3.2 %shard_map.125 = (f32[18,48,128]{2,1,0:T(8,128)S(1)}, f32[16,48,128]{2,1,0:T(8,128)S(1)}, f32[16,48,128]{2,1,0:T(8,128)S(1)}, f32[16,48,128]{2,1,0:T(8,128)S(1)}) custom-call(s32[4]{0:T(128)S(1)} %pad_add_fusion.1.info, f32[3,16,48,128]{3,2,1,0:T(8,128)S(1)} %get-tuple-element.92.vel, f32[16,48,128]{2,1,0:T(8,128)S(1)} %get-tuple-element.93.press, ...), custom_call_target="tpu_custom_call" | custom-call | flops 3502096 | bytes 3502096 | tf_op jit(solution)/shard_map/pallas_call | solution.py:30
  80.8 5.2 %shard_map.126 = (f32[3,16,48,128]{3,2,1,0:T(8,128)S(1)}, f32[16,48,128]{2,1,0:T(8,128)S(1)}, f32[16,48,128]{2,1,0:T(8,128)S(1)}, f32[2,48,128]{2,1,0:T(8,128)S(1)}, f32[17,48,128]{2,1,0:T(8,128)S(1)}) custom-call(s32[4]{0:T(128)S(1)} %pad_add_fusion.1.info, f32[3,16,48,128]{3,2,1,0:T(8,128)S(1)} %get-tuple-element.92.vel, ...), custom_call_target="tpu_custom_call" | custom-call | flops 8171728 | bytes 8171728 | tf_op jit(solution)/shard_map/pallas_call | solution.py:30
  86.0 1.7 %collective-permute-done.19.refs_0_ = f32[17,48,128]{2,1,0:T(8,128)S(1)} collective-permute-done((f32[17,48,128]{2,1,0:T(8,128)S(1)}, f32[17,48,128]{2,1,0:T(8,128)S(1)}, u32[]{:S(2)}, u32[]{:S(2)}) %collective-permute-start.19) | collective-permute-done | bytes 417824 | tf_op jit(solution)/shard_map/ppermute | solution.py:81
  88.9 1.5 %collective-permute-start.20 = (f32[144,128]{1,0:T(8,128)S(1)}, f32[144,128]{1,0:T(8,128)S(1)}, u32[]{:S(2)}, u32[]{:S(2)}) collective-permute-start(f32[144,128]{1,0:T(8,128)S(1)} %get-tuple-element.114), channel_id=1, source_target_pairs={{0,4},{4,0},{8,12},{12,8},{1,5},{5,1},{9,13},{13,9},{2,6},{6,2},{1... | collective-permute-start | bytes 221192 | tf_op jit(solution)/shard_map/ppermute | solution.py:81
  90.4 1.5 %collective-permute-start.21 = (f32[144,128]{1,0:T(8,128)S(1)}, f32[144,128]{1,0:T(8,128)S(1)}, u32[]{:S(2)}, u32[]{:S(2)}) collective-permute-start(f32[144,128]{1,0:T(8,128)S(1)} %get-tuple-element.115), channel_id=1, source_target_pairs={{4,8},{12,0},{8,4},{0,12},{5,9},{13,1},{9,5},{1,13},{6,10},{14,2},... | collective-permute-start | bytes 221192 | tf_op jit(solution)/shard_map/ppermute | solution.py:81
  91.8 1.9 %collective-permute-done.20.refs_0_ = f32[144,128]{1,0:T(8,128)S(1)} collective-permute-done((f32[144,128]{1,0:T(8,128)S(1)}, f32[144,128]{1,0:T(8,128)S(1)}, u32[]{:S(2)}, u32[]{:S(2)}) %collective-permute-start.20) | collective-permute-done | bytes 73760 | tf_op jit(solution)/shard_map/ppermute | solution.py:81
  93.7 2.0 %collective-permute-done.21.refs_1_ = f32[144,128]{1,0:T(8,128)S(1)} collective-permute-done((f32[144,128]{1,0:T(8,128)S(1)}, f32[144,128]{1,0:T(8,128)S(1)}, u32[]{:S(2)}, u32[]{:S(2)}) %collective-permute-start.21) | collective-permute-done | bytes 73760 | tf_op jit(solution)/shard_map/ppermute | solution.py:81
  97.6 2.5 %collective-permute-start.23 = (f32[54,8,128]{2,1,0:T(8,128)S(1)}, f32[54,8,128]{2,1,0:T(8,128)S(1)}, u32[]{:S(2)}, u32[]{:S(2)}) collective-permute-start(f32[54,8,128]{2,1,0:T(8,128)S(1)} %get-tuple-element.123), channel_id=1, source_target_pairs={{1,2},{2,1},{5,6},{6,5},{9,10},{10,9},{13,14},{14,13},{17,18},{18,... | collective-permute-start | bytes 663560 | tf_op jit(solution)/shard_map/ppermute | solution.py:81
  100.1 6.9 %shard_map.128 = (f32[7,2,24,8,128]{4,3,2,1,0:T(8,128)S(1)}, f32[7,2,24,8,128]{4,3,2,1,0:T(8,128)S(1)}, f32[24,48,128]{2,1,0:T(8,128)S(1)}, f32[24,48,128]{2,1,0...) custom-call(s32[4]{0:T(128)S(1)} %pad_add_fusion.1.info, ...), custom_call_target="tpu_custom_call" | custom-call | flops 6438928 | bytes 6438928 | tf_op jit(solution)/shard_map/pallas_call | solution.py:30
  107.0 7.1 %shard_map.130 = (f32[3,16,48,128]{3,2,1,0:T(8,128)}, f32[16,48,128]{2,1,0:T(8,128)}) custom-call(s32[4]{0:T(128)S(1)} %pad_add_fusion.1.info, f32[24,48,128]{2,1,0:T(8,128)S(1)} %get-tuple-element.111.px, f32[24,48,128]{2,1,0:T(8,128)S(1)} %get-tuple-element.112.sx, f32[3,16,48,128]{3,2,1,0:T(8,128)S(1)} %get-tuple-element.113.star, ...), custom_call_target="tpu_custom_call" | custom-call | flops 9486736 | bytes 9486736 | tf_op jit(solution)/shard_map/pallas_call | solution.py:30
  (57 shorter events, 19.8 us)
Async XLA Ops:
  0.6 4.5 %copy-start.8 = (s32[256,1]{0,1:T(1,128)S(1)}, s32[256,1]{0,1:T(1,128)}, u32[]{:S(2)}) copy-start(s32[256,1]{0,1:T(1,128)} %param.13) | copy-start | bytes 3076
  4.3 2.3 %copy-start.1 = (f32[3,16,48,128]{3,2,1,0:T(8,128)S(1)}, f32[3,16,48,128]{3,2,1,0:T(8,128)}, u32[]{:S(2)}) copy-start(f32[3,16,48,128]{3,2,1,0:T(8,128)} %vel.7) | copy-start | bytes 3538948
  4.3 2.3 %copy-start.3 = (f32[16,48,128]{2,1,0:T(8,128)S(1)}, f32[16,48,128]{2,1,0:T(8,128)}, u32[]{:S(2)}) copy-start(f32[16,48,128]{2,1,0:T(8,128)} %press.7) | copy-start | bytes 1179652
  5.1 2.7 %copy-start.4 = (f32[256,128]{1,0:T(8,128)S(1)}, f32[256,128]{1,0:T(8,128)}, u32[]{:S(2)}) copy-start(f32[256,128]{1,0:T(8,128)} %kern.1) | copy-start | bytes 393220
  5.1 2.8 %copy-start.6 = (s32[256]{0:T(256)S(1)}, s32[256]{0:T(256)}, u32[]{:S(2)}) copy-start(s32[256]{0:T(256)} %param.14) | copy-start | bytes 3076
  5.1 2.8 %copy-start.7 = (s32[256]{0:T(256)S(1)}, s32[256]{0:T(256)}, u32[]{:S(2)}) copy-start(s32[256]{0:T(256)} %param.15) | copy-start | bytes 3076
  5.1 1.5 %collective-permute-start = (f32[392,128]{1,0:T(8,128)S(1)}, f32[392,128]{1,0:T(8,128)S(1)}, u32[]{:S(2)}, u32[]{:S(2)}) collective-permute-start(f32[392,128]{1,0:T(8,128)S(1)} %get-tuple-element.64), channel_id=1, source_target_pairs={{0,16},{16,0},{1,17},{17,1},{2,18},{18,2},{3,19},{19,3},{4,20},{20... | collective-permute-start | bytes 602120 | tf_op jit(solution)/shard_map/ppermute | solution.py:81
  10.0 17.4 %all-to-all-start = ((f32[8,72,128]{2,1,0:T(8,128)}), f32[8,72,128]{2,1,0:T(8,128)S(1)}, u32[]{:S(2)}, u32[]{:S(2)}) async-start(f32[8,72,128]{2,1,0:T(8,128)} %bitcast.8), calls=%async_computation | async-start | bytes 589824 | tf_op jit(solution)/shard_map/all_to_all | solution.py:878
  14.2 16.4 %copy-start.5 = (f32[48]{0:T(128)S(1)}, f32[48]{0:T(128)}, u32[]{:S(2)}) copy-start(f32[48]{0:T(128)} %param.17) | copy-start | bytes 580
  14.2 7.5 %collective-permute-start.1 = (f32[104,128]{1,0:T(8,128)S(1)}, f32[104,128]{1,0:T(8,128)S(1)}, u32[]{:S(2)}, u32[]{:S(2)}) collective-permute-start(f32[104,128]{1,0:T(8,128)S(1)} %get-tuple-element.66), channel_id=1, source_target_pairs={{0,4},{4,0},{8,12},{12,8},{1,5},{5,1},{9,13},{13,9},{2,6},{6,2},{1... | collective-permute-start | bytes 159752 | tf_op jit(solution)/shard_map/ppermute | solution.py:81
  15.7 6.6 %collective-permute-start.2 = (f32[104,128]{1,0:T(8,128)S(1)}, f32[104,128]{1,0:T(8,128)S(1)}, u32[]{:S(2)}, u32[]{:S(2)}) collective-permute-start(f32[104,128]{1,0:T(8,128)S(1)} %get-tuple-element.67), channel_id=1, source_target_pairs={{4,8},{12,0},{8,4},{0,12},{5,9},{13,1},{9,5},{1,13},{6,10},{14,2},... | collective-permute-start | bytes 159752 | tf_op jit(solution)/shard_map/ppermute | solution.py:81
  15.8 3.8 %collective-permute-start.3 = (f32[8,128]{1,0:T(8,128)S(1)}, f32[8,128]{1,0:T(8,128)S(1)}, u32[]{:S(2)}, u32[]{:S(2)}) collective-permute-start(f32[8,128]{1,0:T(8,128)S(1)} %get-tuple-element.65.parts.after), channel_id=1, source_target_pairs={{0,8},{4,12},{8,0},{12,4},{1,9},{5,13},{9,1},{13,5},{2,10},{6,14},... | collective-permute-start | bytes 12296 | tf_op jit(solution)/shard_map/ppermute | solution.py:871
  22.9 7.7 %collective-permute-start.4 = (f32[104,128]{1,0:T(8,128)S(1)}, f32[104,128]{1,0:T(8,128)S(1)}, u32[]{:S(2)}, u32[]{:S(2)}) collective-permute-start(f32[104,128]{1,0:T(8,128)S(1)} %get-tuple-element.73), channel_id=1, source_target_pairs={{0,1},{1,0},{2,3},{3,2},{4,5},{5,4},{6,7},{7,6},{8,9},{9,8},{10,11... | collective-permute-start | bytes 159752 | tf_op jit(solution)/shard_map/ppermute | solution.py:81
  23.4 7.2 %collective-permute-start.5 = (f32[104,128]{1,0:T(8,128)S(1)}, f32[104,128]{1,0:T(8,128)S(1)}, u32[]{:S(2)}, u32[]{:S(2)}) collective-permute-start(f32[104,128]{1,0:T(8,128)S(1)} %get-tuple-element.74), channel_id=1, source_target_pairs={{1,2},{3,0},{2,1},{0,3},{5,6},{7,4},{6,5},{4,7},{9,10},{11,8},{10,... | collective-permute-start | bytes 159752 | tf_op jit(solution)/shard_map/ppermute | solution.py:81
  26.1 4.5 %collective-permute-start.6 = (f32[8,128]{1,0:T(8,128)S(1)}, f32[8,128]{1,0:T(8,128)S(1)}, u32[]{:S(2)}, u32[]{:S(2)}) collective-permute-start(f32[8,128]{1,0:T(8,128)S(1)} %get-tuple-element.68.parts), channel_id=1, source_target_pairs={{0,2},{1,3},{2,0},{3,1},{4,6},{5,7},{6,4},{7,5},{8,10},{9,11},{10,... | collective-permute-start | bytes 12296 | tf_op jit(solution)/shard_map/ppermute | solution.py:893
  36.6 1.8 %collective-permute-start.7 = (f32[17,48,128]{2,1,0:T(8,128)S(1)}, f32[17,48,128]{2,1,0:T(8,128)S(1)}, u32[]{:S(2)}, u32[]{:S(2)}) collective-permute-start(f32[17,48,128]{2,1,0:T(8,128)S(1)} %get-tuple-element.78), channel_id=1, source_target_pairs={{0,16},{16,0},{1,17},{17,1},{2,18},{18,2},{3,19},{19,3},{4,20},{20... | collective-permute-start | bytes 1253384 | tf_op jit(solution)/shard_map/ppermute | solution.py:81
  39.5 4.9 %collective-permute-start.8 = (f32[144,128]{1,0:T(8,128)S(1)}, f32[144,128]{1,0:T(8,128)S(1)}, u32[]{:S(2)}, u32[]{:S(2)}) collective-permute-start(f32[144,128]{1,0:T(8,128)S(1)} %get-tuple-element.82), channel_id=1, source_target_pairs={{0,4},{4,0},{8,12},{12,8},{1,5},{5,1},{9,13},{13,9},{2,6},{6,2},{1... | collective-permute-start | bytes 221192 | tf_op jit(solution)/shard_map/ppermute | solution.py:81
  39.9 6.4 %collective-permute-start.9 = (f32[144,128]{1,0:T(8,128)S(1)}, f32[144,128]{1,0:T(8,128)S(1)}, u32[]{:S(2)}, u32[]{:S(2)}) collective-permute-start(f32[144,128]{1,0:T(8,128)S(1)} %get-tuple-element.83), channel_id=1, source_target_pairs={{4,8},{12,0},{8,4},{0,12},{5,9},{13,1},{9,5},{1,13},{6,10},{14,2},... | collective-permute-start | bytes 221192 | tf_op jit(solution)/shard_map/ppermute | solution.py:81
  46.9 10.8 %collective-permute-start.10 = (f32[54,8,128]{2,1,0:T(8,128)S(1)}, f32[54,8,128]{2,1,0:T(8,128)S(1)}, u32[]{:S(2)}, u32[]{:S(2)}) collective-permute-start(f32[54,8,128]{2,1,0:T(8,128)S(1)} %get-tuple-element.90), channel_id=1, source_target_pairs={{0,1},{1,0},{2,3},{3,2},{4,5},{5,4},{6,7},{7,6},{8,9},{9,8},{10,11... | collective-permute-start | bytes 663560 | tf_op jit(solution)/shard_map/ppermute | solution.py:81
  48.3 9.4 %collective-permute-start.11 = (f32[54,8,128]{2,1,0:T(8,128)S(1)}, f32[54,8,128]{2,1,0:T(8,128)S(1)}, u32[]{:S(2)}, u32[]{:S(2)}) collective-permute-start(f32[54,8,128]{2,1,0:T(8,128)S(1)} %get-tuple-element.91), channel_id=1, source_target_pairs={{1,2},{2,1},{5,6},{6,5},{9,10},{10,9},{13,14},{14,13},{17,18},{18,... | collective-permute-start | bytes 663560 | tf_op jit(solution)/shard_map/ppermute | solution.py:81
  64.0 1.5 %collective-permute-start.12 = (f32[392,128]{1,0:T(8,128)S(1)}, f32[392,128]{1,0:T(8,128)S(1)}, u32[]{:S(2)}, u32[]{:S(2)}) collective-permute-start(f32[392,128]{1,0:T(8,128)S(1)} %get-tuple-element.95), channel_id=1, source_target_pairs={{0,16},{16,0},{1,17},{17,1},{2,18},{18,2},{3,19},{19,3},{4,20},{20... | collective-permute-start | bytes 602120 | tf_op jit(solution)/shard_map/ppermute | solution.py:81
  66.7 5.8 %collective-permute-start.13 = (f32[104,128]{1,0:T(8,128)S(1)}, f32[104,128]{1,0:T(8,128)S(1)}, u32[]{:S(2)}, u32[]{:S(2)}) collective-permute-start(f32[104,128]{1,0:T(8,128)S(1)} %get-tuple-element.97), channel_id=1, source_target_pairs={{0,4},{4,0},{8,12},{12,8},{1,5},{5,1},{9,13},{13,9},{2,6},{6,2},{1... | collective-permute-start | bytes 159752 | tf_op jit(solution)/shard_map/ppermute | solution.py:81
  67.4 5.1 %collective-permute-start.14 = (f32[104,128]{1,0:T(8,128)S(1)}, f32[104,128]{1,0:T(8,128)S(1)}, u32[]{:S(2)}, u32[]{:S(2)}) collective-permute-start(f32[104,128]{1,0:T(8,128)S(1)} %get-tuple-element.98), channel_id=1, source_target_pairs={{4,8},{12,0},{8,4},{0,12},{5,9},{13,1},{9,5},{1,13},{6,10},{14,2},... | collective-permute-start | bytes 159752 | tf_op jit(solution)/shard_map/ppermute | solution.py:81
  68.8 3.6 %collective-permute-start.15 = (f32[8,128]{1,0:T(8,128)S(1)}, f32[8,128]{1,0:T(8,128)S(1)}, u32[]{:S(2)}, u32[]{:S(2)}) collective-permute-start(f32[8,128]{1,0:T(8,128)S(1)} %get-tuple-element.96.parts), channel_id=1, source_target_pairs={{0,8},{4,12},{8,0},{12,4},{1,9},{5,13},{9,1},{13,5},{2,10},{6,14},... | collective-permute-start | bytes 12296 | tf_op jit(solution)/shard_map/ppermute | solution.py:871
  73.1 7.7 %collective-permute-start.16 = (f32[104,128]{1,0:T(8,128)S(1)}, f32[104,128]{1,0:T(8,128)S(1)}, u32[]{:S(2)}, u32[]{:S(2)}) collective-permute-start(f32[104,128]{1,0:T(8,128)S(1)} %get-tuple-element.105), channel_id=1, source_target_pairs={{0,1},{1,0},{2,3},{3,2},{4,5},{5,4},{6,7},{7,6},{8,9},{9,8},{10,11... | collective-permute-start | bytes 159752 | tf_op jit(solution)/shard_map/ppermute | solution.py:81
  73.2 7.6 %collective-permute-start.17 = (f32[104,128]{1,0:T(8,128)S(1)}, f32[104,128]{1,0:T(8,128)S(1)}, u32[]{:S(2)}, u32[]{:S(2)}) collective-permute-start(f32[104,128]{1,0:T(8,128)S(1)} %get-tuple-element.106), channel_id=1, source_target_pairs={{1,2},{3,0},{2,1},{0,3},{5,6},{7,4},{6,5},{4,7},{9,10},{11,8},{10,... | collective-permute-start | bytes 159752 | tf_op jit(solution)/shard_map/ppermute | solution.py:81
  74.6 6.1 %collective-permute-start.18 = (f32[8,128]{1,0:T(8,128)S(1)}, f32[8,128]{1,0:T(8,128)S(1)}, u32[]{:S(2)}, u32[]{:S(2)}) collective-permute-start(f32[8,128]{1,0:T(8,128)S(1)} %get-tuple-element.99.parts), channel_id=1, source_target_pairs={{0,2},{1,3},{2,0},{3,1},{4,6},{5,7},{6,4},{7,5},{8,10},{9,11},{10,... | collective-permute-start | bytes 12296 | tf_op jit(solution)/shard_map/ppermute | solution.py:893
  86.0 1.8 %collective-permute-start.19 = (f32[17,48,128]{2,1,0:T(8,128)S(1)}, f32[17,48,128]{2,1,0:T(8,128)S(1)}, u32[]{:S(2)}, u32[]{:S(2)}) collective-permute-start(f32[17,48,128]{2,1,0:T(8,128)S(1)} %get-tuple-element.110), channel_id=1, source_target_pairs={{0,16},{16,0},{1,17},{17,1},{2,18},{18,2},{3,19},{19,3},{4,20},{20... | collective-permute-start | bytes 1253384 | tf_op jit(solution)/shard_map/ppermute | solution.py:81
  88.9 4.9 %collective-permute-start.20 = (f32[144,128]{1,0:T(8,128)S(1)}, f32[144,128]{1,0:T(8,128)S(1)}, u32[]{:S(2)}, u32[]{:S(2)}) collective-permute-start(f32[144,128]{1,0:T(8,128)S(1)} %get-tuple-element.114), channel_id=1, source_target_pairs={{0,4},{4,0},{8,12},{12,8},{1,5},{5,1},{9,13},{13,9},{2,6},{6,2},{1... | collective-permute-start | bytes 221192 | tf_op jit(solution)/shard_map/ppermute | solution.py:81
  90.4 5.4 %collective-permute-start.21 = (f32[144,128]{1,0:T(8,128)S(1)}, f32[144,128]{1,0:T(8,128)S(1)}, u32[]{:S(2)}, u32[]{:S(2)}) collective-permute-start(f32[144,128]{1,0:T(8,128)S(1)} %get-tuple-element.115), channel_id=1, source_target_pairs={{4,8},{12,0},{8,4},{0,12},{5,9},{13,1},{9,5},{1,13},{6,10},{14,2},... | collective-permute-start | bytes 221192 | tf_op jit(solution)/shard_map/ppermute | solution.py:81
  96.3 10.7 %collective-permute-start.22 = (f32[54,8,128]{2,1,0:T(8,128)S(1)}, f32[54,8,128]{2,1,0:T(8,128)S(1)}, u32[]{:S(2)}, u32[]{:S(2)}) collective-permute-start(f32[54,8,128]{2,1,0:T(8,128)S(1)} %get-tuple-element.122), channel_id=1, source_target_pairs={{0,1},{1,0},{2,3},{3,2},{4,5},{5,4},{6,7},{7,6},{8,9},{9,8},{10,11... | collective-permute-start | bytes 663560 | tf_op jit(solution)/shard_map/ppermute | solution.py:81
  97.6 9.4 %collective-permute-start.23 = (f32[54,8,128]{2,1,0:T(8,128)S(1)}, f32[54,8,128]{2,1,0:T(8,128)S(1)}, u32[]{:S(2)}, u32[]{:S(2)}) collective-permute-start(f32[54,8,128]{2,1,0:T(8,128)S(1)} %get-tuple-element.123), channel_id=1, source_target_pairs={{1,2},{2,1},{5,6},{6,5},{9,10},{10,9},{13,14},{14,13},{17,18},{18,... | collective-permute-start | bytes 663560 | tf_op jit(solution)/shard_map/ppermute | solution.py:81
  (2 other events, 2.3 us)
